TPU v7x, 256 devices: a whole 4x4x8 slice. The times are simulated.
256 devices in a mesh: pole: 8 (over x_hi, y), row: 32 (over x_lo, z, core).
Axes of the slice: x: 4 (x_hi: 2, x_lo: 2; x = x_hi * 2 + x_lo), y: 4, z: 8, core: 2. Of those that a mesh axis runs over, the one named last changes fastest.
Arguments:
- basis: bfloat16 [131072, 128], P('row'), may hold values from -24 to 24
- inverses: bfloat16 [8, 256, 512, 512], P('pole', 'row'), may hold values from -1.5 to 1.5
- lower: bfloat16 [256, 512, 512], P('row'), may hold values from -0.03955078 to 0.03955078
- upper: bfloat16 [256, 512, 512], P('row'), may hold values from -0.03955078 to 0.03955078
- pole_weights: float32 [8], P('pole'), may hold values from 0.5 to 1.5
Outputs:
- new_basis: float32 [131072, 128], P(('row', 'pole'))
All inputs are finite; a program needn't handle non-finite values.
Results may differ from a plain program's by a relative error of at most 0.003.
Values may be sent and summed in bfloat16 or wider, within the bound.
No kernel may reach another device: no remote copies, remote signals or barrier semaphores. Data moves between devices by JAX's collectives and lax.ppermute only.
A program may use at most 64 MiB of HBM per device.

v0:
```python
import jax
import jax.numpy as jnp
from jax import lax
from jax.sharding import PartitionSpec as P

SWEEPS = 4


def padded_2(value, sides, width):
    for axis, dim in sides:
        peers, length = (lax.axis_size(axis), value.shape[dim])
        up = [(i, (i + 1) % peers) for i in range(peers - 1)]
        down = [(j, i) for i, j in up]
        last = lax.slice_in_dim(value, length - width, length, axis=dim)
        initial = lax.slice_in_dim(value, 0, width, axis=dim)
        before = lax.ppermute(last, axis, up)
        after = lax.ppermute(initial, axis, down)
        value = jnp.concatenate([before, value, after], axis=dim)
    return value


def sent_to_all(value, axis):
    copies = jnp.broadcast_to(value, (lax.axis_size(axis), *value.shape))
    return lax.all_to_all(copies, axis, split_axis=0, concat_axis=0, tiled=True)


def of_everyone(value, axis):
    return sent_to_all(value, axis).sum(axis=0)


def shards(basis, inverses, lower, upper, pole_weights):
    rows, width = basis.shape
    count = inverses.shape[1]
    size = inverses.shape[-1]
    inverse = inverses[0]
    blocks = basis.reshape(count, size, width)
    state = jnp.einsum("bij,bjk->bik", inverse, blocks, preferred_element_type=jnp.float32).astype(
        jnp.bfloat16
    )
    for sweep in range(SWEEPS):
        padded = padded_2(state.reshape(rows, width), (("row", 0),), size)
        padded = padded.reshape(count + 2, size, width)
        rhs = blocks.astype(jnp.float32)
        rhs = rhs + jnp.einsum(
            "bij,bjk->bik", lower, padded[:-2], preferred_element_type=jnp.float32
        )
        rhs = rhs + jnp.einsum(
            "bij,bjk->bik", upper, padded[2:], preferred_element_type=jnp.float32
        )
        state = jnp.einsum(
            "bij,bjk->bik", inverse, rhs.astype(jnp.bfloat16), preferred_element_type=jnp.float32
        ).astype(jnp.bfloat16)
    weighted = pole_weights[0] * state.reshape(rows, width).astype(jnp.float32)
    total_rows = rows * lax.axis_size("row")
    filtered = lax.psum(weighted, "pole")
    share = rows // lax.axis_size("pole")
    mine = lax.dynamic_slice_in_dim(filtered, lax.axis_index("pole") * share, share, 0)
    partial_gram = jnp.dot(filtered.T, filtered)
    gram = of_everyone(partial_gram, "row")
    gram = gram / total_rows
    factor = jnp.linalg.cholesky(gram)
    solved = jax.scipy.linalg.solve_triangular(factor, mine.T, lower=True)
    return solved.T


def solution(mesh):
    return jax.shard_map(
        shards,
        mesh=mesh,
        in_specs=(
            P("row", None),
            P("pole", "row", None, None),
            P("row", None, None),
            P("row", None, None),
            P("pole"),
        ),
        out_specs=P(("row", "pole"), None),
        check_vma=False,
    )
```

profile of v0, /device:TPU:1, one launch (start us, length us, event | category | flops | bytes accessed | tf_op | source)
XLA Modules:
  0.0 302.5 jit_solution(8116113924164155831)
XLA Ops:
  6.5 0.0 all-reduce.2.cloned.1.call-start
  6.5 0.0 copy-start
  6.5 3.8 %fusion.18 = bf16[8,512,128]{2,1,0:T(8,128)(2,1)S(1)} fusion(bf16[8,512,128]{2,1,0:T(8,128)(2,1)} %bitcast.142, bf16[1,8,512,512]{3,2,1,0:T(8,128)(2,1)} %param.6), kind=kOutput, calls=%fused_computation.23 | convolution fusion | flops 537395200 | bytes 6291456 | tf_op jit(solution)/shard_map/bij,bjk->bik/dot_general | solution.py:37
  10.4 4.9 %collective-permute-start = (bf16[512,128]{1,0:T(8,128)(2,1)S(1)}, bf16[512,128]{1,0:T(8,128)(2,1)S(1)}, u32[]{:S(2)}, u32[]{:S(2)}) collective-permute-start(bf16[512,128]{1,0:T(8,128)(2,1)S(1)} %get-tuple-element.20), channel_id=1, source_target_pairs={{0,1},{1,2},{2,3},{3,4},{4,5},{5,6},{6,7},{7,8},{8,9},{9,10},{10,1... | collective-permute-start | bytes 393224 | tf_op jit(solution)/shard_map/ppermute | solution.py:16
  15.3 1.9 collective-permute-start.1
  17.3 0.0 copy-done
  17.3 0.5 copy.38
  17.8 0.0 collective-permute-done
  17.8 3.9 %collective-permute-done.1 = bf16[512,128]{1,0:T(8,128)(2,1)} collective-permute-done((bf16[512,128]{1,0:T(8,128)(2,1)S(1)}, bf16[512,128]{1,0:T(8,128)(2,1)}, u32[]{:S(2)}, u32[]{:S(2)}) %collective-permute-start.1) | collective-permute-done | bytes 131104 | tf_op jit(solution)/shard_map/ppermute | solution.py:17
  21.7 2.0 pad_maximum_fusion.6
  23.7 3.7 %fusion.50 = f32[8,128,512]{2,1,0:T(8,128)S(1)} fusion(bf16[8,512,128]{2,1,0:T(8,128)(2,1)S(1)} %bitcast.131, bf16[8,512,512]{2,1,0:T(8,128)(2,1)} %param.7), kind=kOutput, calls=%fused_computation.59 | convolution fusion | flops 536870912 | bytes 7340032 | tf_op jit(solution)/shard_map/bij,bjk->bik/dot_general | solution.py:44
  27.4 7.7 %fusion.41 = bf16[8,512,128]{1,2,0:T(8,128)(2,1)} fusion(bf16[1,8,512,512]{3,2,1,0:T(8,128)(2,1)} %param.6, bf16[8,512,128]{1,2,0:T(8,128)(2,1)S(1)} %copy.38, f32[8,128,512]{2,1,0:T(8,128)S(1)} %fusion.50, bf16[8,512,128]{2,1,0:T(8,128)(2,1)} %bitcast.138, bf16[8,512,512]{2,1,0:T(8,128)(2,1)} %param.8), kind=kOutput, calls=%fused_computation.30 | convolution fusion | flops 1076363264 | bytes 13631488 | tf_op jit(solution)/shard_map/bij,bjk->bik/dot_general | solution.py:50
  35.1 1.0 slice_bitcast_fusion.4
  36.1 1.9 collective-permute-start.2
  38.0 2.4 collective-permute-start.3
  40.4 1.6 copy.41
  42.1 0.0 collective-permute-done.2
  42.1 0.1 copy.42
  42.2 2.4 collective-permute-done.3
  44.6 0.1 copy.44
  44.7 1.1 pad_maximum_fusion.4
  45.8 3.7 %fusion.51 = f32[8,128,512]{2,1,0:T(8,128)S(1)} fusion(bf16[8,512,128]{2,1,0:T(8,128)(2,1)S(1)} %bitcast.132, bf16[8,512,512]{2,1,0:T(8,128)(2,1)} %param.7), kind=kOutput, calls=%fused_computation.60 | convolution fusion | flops 536870912 | bytes 7340032 | tf_op jit(solution)/shard_map/bij,bjk->bik/dot_general | solution.py:44
  49.5 7.7 %fusion.38 = bf16[8,512,128]{1,2,0:T(8,128)(2,1)} fusion(bf16[1,8,512,512]{3,2,1,0:T(8,128)(2,1)} %param.6, bf16[8,512,128]{1,2,0:T(8,128)(2,1)S(1)} %copy.38, f32[8,128,512]{2,1,0:T(8,128)S(1)} %fusion.51, bf16[8,512,128]{2,1,0:T(8,128)(2,1)} %bitcast.139, bf16[8,512,512]{2,1,0:T(8,128)(2,1)} %param.8), kind=kOutput, calls=%fused_computation.29 | convolution fusion | flops 1076363264 | bytes 13631488 | tf_op jit(solution)/shard_map/bij,bjk->bik/dot_general | solution.py:50
  57.2 1.0 slice_bitcast_fusion.2
  58.2 1.9 collective-permute-start.4
  60.1 2.4 collective-permute-start.5
  62.5 1.6 copy.46
  64.2 0.0 collective-permute-done.4
  64.2 0.1 copy.47
  64.3 2.4 collective-permute-done.5
  66.7 0.1 copy.49
  66.8 1.1 pad_maximum_fusion.2
  67.9 3.7 %fusion.52 = f32[8,128,512]{2,1,0:T(8,128)S(1)} fusion(bf16[8,512,128]{2,1,0:T(8,128)(2,1)S(1)} %bitcast.133, bf16[8,512,512]{2,1,0:T(8,128)(2,1)} %param.7), kind=kOutput, calls=%fused_computation.61 | convolution fusion | flops 536870912 | bytes 7340032 | tf_op jit(solution)/shard_map/bij,bjk->bik/dot_general | solution.py:44
  71.6 7.7 %fusion.35 = bf16[8,512,128]{1,2,0:T(8,128)(2,1)} fusion(bf16[1,8,512,512]{3,2,1,0:T(8,128)(2,1)} %param.6, bf16[8,512,128]{1,2,0:T(8,128)(2,1)S(1)} %copy.38, f32[8,128,512]{2,1,0:T(8,128)S(1)} %fusion.52, bf16[8,512,128]{2,1,0:T(8,128)(2,1)} %bitcast.140, bf16[8,512,512]{2,1,0:T(8,128)(2,1)} %param.8), kind=kOutput, calls=%fused_computation.28 | convolution fusion | flops 1076363264 | bytes 13631488 | tf_op jit(solution)/shard_map/bij,bjk->bik/dot_general | solution.py:50
  79.3 1.0 slice_bitcast_fusion
  80.3 1.9 collective-permute-start.6
  82.2 2.6 collective-permute-start.7
  85.5 1.6 copy.51
  87.1 0.0 collective-permute-done.6
  87.1 0.1 copy.52
  87.2 4.0 %collective-permute-done.7 = bf16[512,128]{0,1:T(8,128)(2,1)S(1)} collective-permute-done((bf16[512,128]{0,1:T(8,128)(2,1)S(1)}, bf16[512,128]{0,1:T(8,128)(2,1)S(1)}, u32[]{:S(2)}, u32[]{:S(2)}) %collective-permute-start.7) | collective-permute-done | bytes 131104 | tf_op jit(solution)/shard_map/ppermute | solution.py:17
  91.2 0.1 copy.54
  91.3 1.1 pad_maximum_fusion
  92.5 3.7 %fusion.53 = f32[8,128,512]{2,1,0:T(8,128)S(1)} fusion(bf16[8,512,128]{2,1,0:T(8,128)(2,1)S(1)} %bitcast.134, bf16[8,512,512]{2,1,0:T(8,128)(2,1)} %param.7), kind=kOutput, calls=%fused_computation.62 | convolution fusion | flops 536870912 | bytes 7340032 | tf_op jit(solution)/shard_map/bij,bjk->bik/dot_general | solution.py:44
  96.2 8.0 %multiply_bitcast_fusion = f32[8,512,128]{1,2,0:T(8,128)} fusion(bf16[1,8,512,512]{3,2,1,0:T(8,128)(2,1)} %param.6, bf16[8,512,128]{1,2,0:T(8,128)(2,1)S(1)} %copy.38, f32[8,128,512]{2,1,0:T(8,128)S(1)} %fusion.53, bf16[8,512,128]{2,1,0:T(8,128)(2,1)} %bitcast.130, bf16[8,512,512]{2,1,0:T(8,128)(2,1)} %param.8, f32[]{:T(128)} %bitcast.128), kind=kOutput, calls=%fused_computation.22 | convolution fusion | flops 1077411840 | bytes 14680068 | tf_op jit(solution)/shard_map/bij,bjk->bik/dot_general | solution.py:50
  104.1 2.9 copy.56
  107.0 0.0 all-reduce.2.cloned.1.call-update
  107.1 97.2 %all-reduce.2.cloned.1.call-done = f32[4096,128]{1,0:T(8,128)} async-done(((f32[4096,128]{1,0:T(8,128)}), f32[4096,128]{1,0:T(8,128)}) %all-reduce.2.cloned.1.call-update) | async-done | bytes 2097168 | tf_op jit(solution)/shard_map/psum | solution.py:55
  204.2 2.7 fusion.54
  206.9 1.6 broadcast_in_dim.5
  208.5 12.6 %all-to-all-start = ((f32[32,128,128]{2,1,0:T(8,128)}), f32[32,128,128]{2,1,0:T(8,128)S(1)}, u32[]{:S(2)}, u32[]{:S(2)}) async-start(f32[32,128,128]{2,1,0:T(8,128)} %broadcast_in_dim.5), calls=%async_computation | async-start | bytes 4194304 | tf_op jit(solution)/shard_map/all_to_all | solution.py:24
  221.1 49.4 %all-to-all-done = f32[32,128,128]{2,1,0:T(8,128)S(1)} async-done(((f32[32,128,128]{2,1,0:T(8,128)}), f32[32,128,128]{2,1,0:T(8,128)S(1)}, u32[]{:S(2)}, u32[]{:S(2)}) %all-to-all-start) | async-done | bytes 2097184 | tf_op jit(solution)/shard_map/all_to_all | solution.py:24
  270.5 0.1 reduce_sum.11
  270.6 0.1 copy.57
  270.7 11.7 %cholesky.16 = f32[128,128]{1,0:T(8,128)S(1)} custom-call(f32[128,128]{1,0:T(8,128)S(1)} %fusion.48), custom_call_target="Cholesky" | custom-call | tf_op jit(solution)/shard_map/jit(cholesky)/cholesky | solution.py:61
  282.5 0.6 compare_reduce_fusion
  283.1 0.7 fusion.46
  283.8 9.8 %custom-call.7 = f32[1,128,128]{1,2,0:T(8,128)S(1)} custom-call(f32[1,128,128]{2,1,0:T(8,128)S(1)} %fusion.46), custom_call_target="InvertDiagBlocksLowerTriangular" | custom-call | tf_op jit(solution)/shard_map/jit(_solve_triangular)/triangular_solve | solution.py:62
  293.6 2.0 fusion.44
  (3 shorter events, 0.1 us)
Async XLA Ops:
  6.5 197.7 %all-reduce.2.cloned.1.call-start = ((), (), s32[]{:S(2)}) async-start(), calls=%async_computation.1 | async-start | bytes 4194304 | tf_op jit(solution)/shard_map/psum | solution.py:55
  6.5 10.7 %copy-start = (bf16[4096,128]{1,0:T(8,128)(2,1)S(1)}, bf16[4096,128]{1,0:T(8,128)(2,1)}, u32[]{:S(2)}) copy-start(bf16[4096,128]{1,0:T(8,128)(2,1)} %param.5) | copy-start | bytes 3145732
  10.4 7.4 %collective-permute-start = (bf16[512,128]{1,0:T(8,128)(2,1)S(1)}, bf16[512,128]{1,0:T(8,128)(2,1)S(1)}, u32[]{:S(2)}, u32[]{:S(2)}) collective-permute-start(bf16[512,128]{1,0:T(8,128)(2,1)S(1)} %get-tuple-element.20), channel_id=1, source_target_pairs={{0,1},{1,2},{2,3},{3,4},{4,5},{5,6},{6,7},{7,8},{8,9},{9,10},{10,1... | collective-permute-start | bytes 393224 | tf_op jit(solution)/shard_map/ppermute | solution.py:16
  15.3 6.4 %collective-permute-start.1 = (bf16[512,128]{1,0:T(8,128)(2,1)S(1)}, bf16[512,128]{1,0:T(8,128)(2,1)}, u32[]{:S(2)}, u32[]{:S(2)}) collective-permute-start(bf16[512,128]{1,0:T(8,128)(2,1)S(1)} %get-tuple-element.19), channel_id=1, source_target_pairs={{1,0},{2,1},{3,2},{4,3},{5,4},{6,5},{7,6},{8,7},{9,8},{10,9},{11,1... | collective-permute-start | bytes 393224 | tf_op jit(solution)/shard_map/ppermute | solution.py:17
  36.1 6.0 %collective-permute-start.2 = (bf16[512,128]{0,1:T(8,128)(2,1)S(1)}, bf16[512,128]{0,1:T(8,128)(2,1)S(1)}, u32[]{:S(2)}, u32[]{:S(2)}) collective-permute-start(bf16[512,128]{0,1:T(8,128)(2,1)S(1)} %get-tuple-element.16), channel_id=1, source_target_pairs={{0,1},{1,2},{2,3},{3,4},{4,5},{5,6},{6,7},{7,8},{8,9},{9,10},{10,1... | collective-permute-start | bytes 393224 | tf_op jit(solution)/shard_map/ppermute | solution.py:16
  38.0 6.6 %collective-permute-start.3 = (bf16[512,128]{0,1:T(8,128)(2,1)S(1)}, bf16[512,128]{0,1:T(8,128)(2,1)S(1)}, u32[]{:S(2)}, u32[]{:S(2)}) collective-permute-start(bf16[512,128]{0,1:T(8,128)(2,1)S(1)} %get-tuple-element.15), channel_id=1, source_target_pairs={{1,0},{2,1},{3,2},{4,3},{5,4},{6,5},{7,6},{8,7},{9,8},{10,9},{11,1... | collective-permute-start | bytes 393224 | tf_op jit(solution)/shard_map/ppermute | solution.py:17
  58.2 6.0 %collective-permute-start.4 = (bf16[512,128]{0,1:T(8,128)(2,1)S(1)}, bf16[512,128]{0,1:T(8,128)(2,1)S(1)}, u32[]{:S(2)}, u32[]{:S(2)}) collective-permute-start(bf16[512,128]{0,1:T(8,128)(2,1)S(1)} %get-tuple-element.12), channel_id=1, source_target_pairs={{0,1},{1,2},{2,3},{3,4},{4,5},{5,6},{6,7},{7,8},{8,9},{9,10},{10,1... | collective-permute-start | bytes 393224 | tf_op jit(solution)/shard_map/ppermute | solution.py:16
  60.1 6.6 %collective-permute-start.5 = (bf16[512,128]{0,1:T(8,128)(2,1)S(1)}, bf16[512,128]{0,1:T(8,128)(2,1)S(1)}, u32[]{:S(2)}, u32[]{:S(2)}) collective-permute-start(bf16[512,128]{0,1:T(8,128)(2,1)S(1)} %get-tuple-element.11), channel_id=1, source_target_pairs={{1,0},{2,1},{3,2},{4,3},{5,4},{6,5},{7,6},{8,7},{9,8},{10,9},{11,1... | collective-permute-start | bytes 393224 | tf_op jit(solution)/shard_map/ppermute | solution.py:17
  80.3 6.8 %collective-permute-start.6 = (bf16[512,128]{0,1:T(8,128)(2,1)S(1)}, bf16[512,128]{0,1:T(8,128)(2,1)S(1)}, u32[]{:S(2)}, u32[]{:S(2)}) collective-permute-start(bf16[512,128]{0,1:T(8,128)(2,1)S(1)} %get-tuple-element.8), channel_id=1, source_target_pairs={{0,1},{1,2},{2,3},{3,4},{4,5},{5,6},{6,7},{7,8},{8,9},{9,10},{10,1... | collective-permute-start | bytes 393224 | tf_op jit(solution)/shard_map/ppermute | solution.py:16
  82.2 9.0 %collective-permute-start.7 = (bf16[512,128]{0,1:T(8,128)(2,1)S(1)}, bf16[512,128]{0,1:T(8,128)(2,1)S(1)}, u32[]{:S(2)}, u32[]{:S(2)}) collective-permute-start(bf16[512,128]{0,1:T(8,128)(2,1)S(1)} %get-tuple-element.7), channel_id=1, source_target_pairs={{1,0},{2,1},{3,2},{4,3},{5,4},{6,5},{7,6},{8,7},{9,8},{10,9},{11,1... | collective-permute-start | bytes 393224 | tf_op jit(solution)/shard_map/ppermute | solution.py:17
  208.5 62.0 %all-to-all-start = ((f32[32,128,128]{2,1,0:T(8,128)}), f32[32,128,128]{2,1,0:T(8,128)S(1)}, u32[]{:S(2)}, u32[]{:S(2)}) async-start(f32[32,128,128]{2,1,0:T(8,128)} %broadcast_in_dim.5), calls=%async_computation | async-start | bytes 4194304 | tf_op jit(solution)/shard_map/all_to_all | solution.py:24
Sparse Core Ops, SparseCore 0:
  107.2 96.9 all-reduce.1
where the time goes:
time: 304 us; the launch traced here: 302 us
  waiting for transfers between devices  159 us (52%)
  matrix products  54.3 us (18%)
  starting transfers between devices  32.7 us (11%)
  other arithmetic  28.4 us (9%)
  between operations  14.3 us (5%)
  local copies, waits for them, and re-layouts  13.6 us (4%)
    psum x1, waiting for transfers between devices, shards(): filtered = lax.psum(weighted, 'pole')  97.2 us
    all_to_all x1, waiting for transfers between devices, sent_to_all(): return lax.all_to_all(copies, axis, split_axis=0, concat_axis=0, tiled=True)  49.4 us
    dot_general x4, matrix products, shards(): jnp.einsum('bij,bjk->bik', inverse, rhs.astype(jnp.bfloat16), preferred_e...  31 us
    dot_general x4, matrix products, shards(): jnp.einsum('bij,bjk->bik', lower, padded[:-2], preferred_element_type=jnp...  14.8 us
    ppermute x4, waiting for transfers between devices, padded_2(): after = lax.ppermute(initial, axis, down)  12.7 us
    all_to_all x1, starting transfers between devices, sent_to_all(): return lax.all_to_all(copies, axis, split_axis=0, concat_axis=0, tiled=True)  12.6 us
    another operation x3, other arithmetic, shards(): factor = jnp.linalg.cholesky(gram)  12.4 us
    ppermute x4, starting transfers between devices, padded_2(): before = lax.ppermute(last, axis, up)  10.7 us
  transfers between devices with their start and end apart: 10, of which 6 were waited for; matrix products, arithmetic and copies ran while one was open for 2% of the time, Pallas kernels for 0%

commit v1 on v0

v1 whole, which is shorter than its diff:
```python
import functools

import jax
import jax.numpy as jnp
from jax import lax
from jax.experimental import pallas as pl
from jax.experimental.pallas import tpu as pltpu
from jax.sharding import Mesh, PartitionSpec as P

SWEEPS = 4
EXTRA = 16
F32 = jnp.float32
BF16 = jnp.bfloat16
HI = lax.Precision.HIGHEST
VM = pl.BlockSpec(memory_space=pltpu.VMEM)
SM = pl.BlockSpec(memory_space=pltpu.SMEM)
LIMIT = 50 << 20


def dot(a, b):
    return jnp.dot(a, b, preferred_element_type=F32)


def params():
    return pltpu.CompilerParams(vmem_limit_bytes=LIMIT)


def cost(flops, moved):
    return pl.CostEstimate(flops=int(flops), bytes_accessed=int(moved), transcendentals=0)


def first_edges_kernel(inv_a, inv_b, basis_a, basis_b, first, last):
    first[...] = dot(inv_a[0, 0], basis_a[...]).astype(BF16)
    last[...] = dot(inv_b[0, 0], basis_b[...]).astype(BF16)


def first_edges(inverses, basis, count, size, width):
    edge = count - 1
    out = jax.ShapeDtypeStruct((size, width), BF16)
    return pl.pallas_call(
        first_edges_kernel,
        grid=(1,),
        out_shape=(out, out),
        in_specs=[
            pl.BlockSpec((1, 1, size, size), lambda i: (0, 0, 0, 0)),
            pl.BlockSpec((1, 1, size, size), lambda i: (0, edge, 0, 0)),
            pl.BlockSpec((size, width), lambda i: (0, 0)),
            pl.BlockSpec((size, width), lambda i: (edge, 0)),
        ],
        out_specs=(
            pl.BlockSpec((size, width), lambda i: (0, 0)),
            pl.BlockSpec((size, width), lambda i: (0, 0)),
        ),
        compiler_params=params(),
        name="first_edges",
    )(inverses, inverses, basis, basis)


def advance(count, left, right, start, first, middle, last, out, partial):
    def state(b):
        if b == 0:
            return first
        if b == count - 1:
            return last
        return middle[b - 1]

    for b in range(1, count - 1):
        value = start[b] + dot(left[b], state(b - 1)) + dot(right[b], state(b + 1))
        out[b - 1, : value.shape[0]] = value.astype(BF16)
    partial[0] = start[0] + dot(right[0], state(1))
    partial[1] = start[count - 1] + dot(left[count - 1], state(count - 2))


def setup_kernel(count, inv, lower, upper, basis, left, right, start, middle, partial, held):
    b = pl.program_id(0)
    inverse = inv[0, 0]
    left[b] = dot(inverse, lower[0]).astype(BF16)
    right[b] = dot(inverse, upper[0]).astype(BF16)
    value = dot(inverse, basis[...])
    start[b] = value
    held[b] = value.astype(BF16)

    @pl.when(b == count - 1)
    def _():
        advance(
            count, left, right, start, held[0],
            [held[i] for i in range(1, count - 1)], held[count - 1], middle, partial,
        )


def setup(inverses, lower, upper, basis, count, size, width):
    flops = 2 * count * size * size * (2 * size + 3 * width)
    return pl.pallas_call(
        functools.partial(setup_kernel, count),
        grid=(count,),
        out_shape=(
            jax.ShapeDtypeStruct((count, size, size), BF16),
            jax.ShapeDtypeStruct((count, size, size), BF16),
            jax.ShapeDtypeStruct((count, size, width), F32),
            jax.ShapeDtypeStruct((count - 2, size, width), BF16),
            jax.ShapeDtypeStruct((2, size, width), F32),
        ),
        in_specs=[
            pl.BlockSpec((1, 1, size, size), lambda b: (0, b, 0, 0)),
            pl.BlockSpec((1, size, size), lambda b: (b, 0, 0)),
            pl.BlockSpec((1, size, size), lambda b: (b, 0, 0)),
            pl.BlockSpec((size, width), lambda b: (b, 0)),
        ],
        out_specs=(VM, VM, VM, VM, VM),
        scratch_shapes=[pltpu.VMEM((count, size, width), BF16)],
        compiler_params=params(),
        cost_estimate=cost(flops, 6 * count * size * size),
        name="setup",
    )(inverses, lower, upper, basis)


def edges_kernel(count, left, right, partial, before, after, first, last):
    first[...] = (partial[0] + dot(left[0], before[...])).astype(BF16)
    last[...] = (partial[1] + dot(right[count - 1], after[...])).astype(BF16)


def edges(left, right, partial, before, after):
    count, size, _ = left.shape
    width = before.shape[-1]
    out = jax.ShapeDtypeStruct((size, width), BF16)
    return pl.pallas_call(
        functools.partial(edges_kernel, count),
        out_shape=(out, out),
        in_specs=[VM] * 5,
        out_specs=(VM, VM),
        compiler_params=params(),
        cost_estimate=cost(4 * size * size * width, 4 * size * size),
        name="edges",
    )(left, right, partial, before, after)


def sweep_kernel(count, left, right, start, first, middle, last, out, partial):
    advance(count, left, right, start, first[...], middle, last[...], out, partial)


def sweep(left, right, start, first, middle, last):
    count, size, _ = left.shape
    width = first.shape[-1]
    return pl.pallas_call(
        functools.partial(sweep_kernel, count),
        out_shape=(
            jax.ShapeDtypeStruct((count - 2, size, width), BF16),
            jax.ShapeDtypeStruct((2, size, width), F32),
        ),
        in_specs=[VM] * 6,
        out_specs=(VM, VM),
        compiler_params=params(),
        cost_estimate=cost(4 * count * size * size * width, 4 * count * size * size),
        name="sweep",
    )(left, right, start, first, middle, last)


def finish_kernel(count, size, weight, left, right, partial, before, after, middle, out):
    out[0, :size] = (partial[0] + dot(left[0], before[...])).astype(BF16)
    for b in range(1, count - 1):
        out[b, :size] = middle[b - 1]
    out[count - 1, :size] = (partial[1] + dot(right[count - 1], after[...])).astype(BF16)
    width = out.shape[-1]
    full = jnp.full((EXTRA, width), weight[0], F32)
    high = full.astype(BF16)
    rest = full - high.astype(F32)
    mid = rest.astype(BF16)
    low = (rest - mid.astype(F32)).astype(BF16)
    place = lax.broadcasted_iota(jnp.int32, (EXTRA, width), 0)
    rows = jnp.where(
        place == 0, high.astype(F32), jnp.where(place == 1, mid.astype(F32), low.astype(F32))
    ).astype(BF16)
    for b in range(count):
        out[b, size:] = rows


def finish(weight, left, right, partial, before, after, middle):
    count, size, _ = left.shape
    width = before.shape[-1]
    return pl.pallas_call(
        functools.partial(finish_kernel, count, size),
        out_shape=jax.ShapeDtypeStruct((count, size + EXTRA, width), BF16),
        in_specs=[SM] + [VM] * 6,
        out_specs=VM,
        compiler_params=params(),
        cost_estimate=cost(4 * size * size * width, 4 * size * size),
        name="finish",
    )(weight, left, right, partial, before, after, middle)


def gram_kernel(size, parts, received, filtered, gram):
    total = None
    for p in range(received.shape[0]):
        rows = received[p, size : size + 3].astype(F32)
        weight = rows[0:1] + rows[1:2] + rows[2:3]
        term = weight * received[p, :size].astype(F32)
        total = term if total is None else total + term
    filtered[...] = total
    value = lax.dot_general(
        total, total, (((0,), (0,)), ((), ())), precision=HI, preferred_element_type=F32
    )
    gram[...] = value.reshape(gram.shape)


def partial_gram(received, parts):
    poles, rows, width = received.shape
    size = rows - EXTRA
    return pl.pallas_call(
        functools.partial(gram_kernel, size, parts),
        out_shape=(
            jax.ShapeDtypeStruct((size, width), F32),
            jax.ShapeDtypeStruct((parts, width // parts, width), F32),
        ),
        in_specs=[VM],
        out_specs=(VM, VM),
        compiler_params=params(),
        name="gram",
    )(received)


def orthonormal_kernel(total_rows, gram, filtered, out, work):
    n = out.shape[-1]
    lanes = lax.broadcasted_iota(jnp.int32, (8, 2 * n), 1)
    subs = lax.broadcasted_iota(jnp.int32, (8, 2 * n), 0)
    work[:, :n] = gram[...].reshape(n, n) / total_rows
    work[:, n:] = (
        lax.broadcasted_iota(jnp.int32, (n, n), 0) == lax.broadcasted_iota(jnp.int32, (n, n), 1)
    ).astype(F32)
    for p in range(n // 8):
        rows = work[8 * p : 8 * p + 8, :]
        for j in range(8):
            column = rows[:, 8 * p + j : 8 * p + j + 1]
            scale = lax.rsqrt(column[j : j + 1])
            pivot = rows[j : j + 1] * scale
            rows = jnp.where(subs == j, pivot, jnp.where(subs > j, rows - (column * scale) * pivot, rows))
        work[8 * p : 8 * p + 8, :] = rows
        if 8 * p + 8 < n:
            change = lax.dot_general(
                rows[:, :n], rows, (((0,), (0,)), ((), ())), precision=HI, preferred_element_type=F32
            )
            work[8 * p + 8 :, :] = work[8 * p + 8 :, :] - change[8 * p + 8 :, :]
    out[...] = lax.dot_general(
        filtered[...], work[:, n:], (((1,), (1,)), ((), ())), precision=HI, preferred_element_type=F32
    )


def orthonormal(gram, filtered, total_rows):
    n = filtered.shape[-1]
    return pl.pallas_call(
        functools.partial(orthonormal_kernel, float(total_rows)),
        out_shape=jax.ShapeDtypeStruct(filtered.shape, F32),
        in_specs=[VM, VM],
        out_specs=VM,
        scratch_shapes=[pltpu.VMEM((n, 2 * n), F32)],
        compiler_params=params(),
        name="orthonormal",
    )(gram, filtered)


POLE = ("x_hi", "y")
ROW = ("x_lo", "z", "core")
PLANE = ("x_hi", "y", "x_lo")
LINE = ("z", "core")


def neighbours(first, last):
    peers = lax.axis_size(ROW)
    up = [(i, i + 1) for i in range(peers - 1)]
    down = [(j, i) for i, j in up]
    return lax.ppermute(last, ROW, up), lax.ppermute(first, ROW, down)


def exchange(value, axes):
    return lax.all_to_all(value, axes, split_axis=0, concat_axis=0, tiled=True)


def shards(basis, inverses, lower, upper, pole_weights):
    rows, width = basis.shape
    count = inverses.shape[1]
    size = inverses.shape[-1]
    first, last = first_edges(inverses, basis, count, size, width)
    before, after = neighbours(first, last)
    left, right, start, middle, partial = setup(inverses, lower, upper, basis, count, size, width)
    for _ in range(SWEEPS - 1):
        first, last = edges(left, right, partial, before, after)
        before, after = neighbours(first, last)
        middle, partial = sweep(left, right, start, first, middle, last)
    solved = finish(pole_weights, left, right, partial, before, after, middle)
    received = exchange(solved, POLE)
    plane = lax.axis_size(PLANE)
    filtered, gram = partial_gram(received, plane)
    gram = exchange(gram, PLANE).sum(0, keepdims=True)
    line = lax.axis_size(LINE)
    gram = exchange(jnp.broadcast_to(gram, (line, *gram.shape[1:])), LINE).sum(0, keepdims=True)
    gram = exchange(jnp.broadcast_to(gram, (plane, *gram.shape[1:])), PLANE)
    return orthonormal(gram, filtered, rows * lax.axis_size(ROW))


def solution(mesh):
    devices = mesh.devices.reshape(2, 4, 2, 8, 2)
    inner = Mesh(devices, ("x_hi", "y", "x_lo", "z", "core"))
    return jax.shard_map(
        shards,
        mesh=inner,
        in_specs=(
            P(ROW, None),
            P(POLE, ROW, None, None),
            P(ROW, None, None),
            P(ROW, None, None),
            P(POLE),
        ),
        out_specs=P(ROW + POLE, None),
        check_vma=False,
    )
```

time: 304 us -> 158 us (0.52)
  waiting for transfers between devices: 159 us -> 0.02 us
  Pallas kernels: 0 us -> 69.1 us
  blocking collectives: 0 us -> 63 us
  matrix products: 54.3 us -> 0 us
  other arithmetic: 28.4 us -> 0.04 us
  between operations: 14.3 us -> 0.82 us
  local copies, waits for them, and re-layouts: 13.6 us -> 1.24 us
  starting transfers between devices: 32.7 us -> 23.5 us
    psum x1 -> x0, waiting for transfers between devices: 97.2 us -> none  [shards(): filtered = lax.psum(weighted, 'pole')]
    pallas_call x0 -> x11, Pallas kernels: none -> 69.1 us  [the longest x3 18.4 us: sweep(): pl.pallas_call(functools.partial(sweep_kernel, count), out_shape=(jax.Sha...]
    all_to_all x0 -> x4, blocking collectives: none -> 63 us  [exchange(): return lax.all_to_all(value, axes, split_axis=0, concat_axis=0, tiled=True)]
    dot_general x10 -> x0, matrix products: 52.2 us -> none  [the longest x4 31 us: shards(): jnp.einsum('bij,bjk->bik', inverse, rhs.astype(jnp.bfloat16), preferred_e...]
    all_to_all x1 -> x0, waiting for transfers between devices: 49.4 us -> none  [sent_to_all(): return lax.all_to_all(copies, axis, split_axis=0, concat_axis=0, tiled=True)]
    another operation x5 -> x0, other arithmetic: 22.9 us -> none  [the longest x3 12.4 us: shards(): factor = jnp.linalg.cholesky(gram)]
    ppermute x8, waiting for transfers between devices: 12.7 us -> 0.02 us  [neighbours(): return (lax.ppermute(last, ROW, up), lax.ppermute(first, ROW, down))]
    all_to_all x1 -> x0, starting transfers between devices: 12.6 us -> none  [sent_to_all(): return lax.all_to_all(copies, axis, split_axis=0, concat_axis=0, tiled=True)]
  transfers between devices with their start and end apart: 10 -> 8, of which waited for: 6 -> 0; matrix products, arithmetic and copies ran while one was open for 2% -> 0% of each run, Pallas kernels for 0% -> 22%
where the time goes in v1:
time: 158 us
  Pallas kernels  69.1 us (44%)
  blocking collectives  63 us (40%)
  starting transfers between devices  23.5 us (15%)
    all_to_all x4, blocking collectives, exchange(): return lax.all_to_all(value, axes, split_axis=0, concat_axis=0, tiled=True)  63 us
    ppermute x8, starting transfers between devices, neighbours(): return (lax.ppermute(last, ROW, up), lax.ppermute(first, ROW, down))  23.5 us
    pallas_call x3, Pallas kernels, sweep(): pl.pallas_call(functools.partial(sweep_kernel, count), out_shape=(jax.Sha...  18.4 us
    pallas_call x1, Pallas kernels, orthonormal(): pl.pallas_call(functools.partial(orthonormal_kernel, float(total_rows)),...  16.8 us
    pallas_call x1, Pallas kernels, setup(): pl.pallas_call(functools.partial(setup_kernel, count), grid=(count,), out...  16.1 us
    pallas_call x3, Pallas kernels, edges(): pl.pallas_call(functools.partial(edges_kernel, count), out_shape=(out, ou...  11.7 us
    pallas_call x1, Pallas kernels, finish(): pl.pallas_call(functools.partial(finish_kernel, count, size), out_shape=j...  3.96 us
  transfers between devices with their start and end apart: 8, of which 0 were waited for; matrix products, arithmetic and copies ran while one was open for 0% of the time, Pallas kernels for 22%

profile of v1, /device:TPU:1, one launch (start us, length us, event | category | flops | bytes accessed | tf_op | source)
XLA Modules:
  0.0 157.7 jit_solution(10151035425123168100)
XLA Ops:
  0.0 0.0 copy-start
  0.0 1.2 copy-done
  1.2 1.6 %first_edges.1 = (bf16[512,128]{1,0:T(8,128)(2,1)S(1)}, bf16[512,128]{1,0:T(8,128)(2,1)S(1)}) custom-call(bf16[1,8,512,512]{3,2,1,0:T(8,128)(2,1)} %inv_b.1, bf16[1,8,512,512]{3,2,1,0:T(8,128)(2,1)} %inv_b.1, bf16[4096,128]{1,0:T(8,128)(2,1)S(1)} %copy-done, bf16[4096,128]{1,0:T(8,128)(2,1)S(1)} %copy-done), custom_call_target="tpu_custom_call" | custom-call | tf_op jit(solution)/shard_map/first_edges/pallas_call | solution.py:40
  2.9 4.9 %collective-permute-start = (bf16[512,128]{1,0:T(8,128)(2,1)S(1)}, bf16[512,128]{1,0:T(8,128)(2,1)S(1)}, u32[]{:S(2)}, u32[]{:S(2)}) collective-permute-start(bf16[512,128]{1,0:T(8,128)(2,1)S(1)} %get-tuple-element.30), channel_id=1, source_target_pairs={{0,1},{1,2},{2,3},{3,4},{4,5},{5,6},{6,7},{7,8},{8,9},{9,10},{10,1... | collective-permute-start | bytes 393224 | tf_op jit(solution)/shard_map/ppermute | solution.py:270
  7.8 1.9 %collective-permute-start.1 = (bf16[512,128]{1,0:T(8,128)(2,1)S(1)}, bf16[512,128]{1,0:T(8,128)(2,1)S(1)}, u32[]{:S(2)}, u32[]{:S(2)}) collective-permute-start(bf16[512,128]{1,0:T(8,128)(2,1)S(1)} %get-tuple-element.31), channel_id=1, source_target_pairs={{1,0},{2,1},{3,2},{4,3},{5,4},{6,5},{7,6},{8,7},{9,8},{10,9},{11,1... | collective-permute-start | bytes 393224 | tf_op jit(solution)/shard_map/ppermute | solution.py:270
  9.7 16.1 %setup.1 = (bf16[8,512,512]{2,1,0:T(8,128)(2,1)}, bf16[8,512,512]{2,1,0:T(8,128)(2,1)}, f32[8,512,128]{2,1,0:T(8,128)}, bf16[6,512,128]{2,1,0:T(8,128)(2,1)S(1)}, f32[2,512,128]{2,1,0:T(8,128)S(1)}) custom-call(bf16[1,8,512,512]{3,2,1,0:T(8,128)(2,1)} %inv_b.1, bf16[8,512,512]{2,1,0:T(8,128)(2,1)} %lower.1, bf16[8,512,512]{2,1,0:T(8,128)(2,1)} %upper.1, ...), custom_call_target="tpu_custom_call" | custom-call | flops 5905580032 | bytes 12582912 | tf_op jit(solution)/shard_map/setup/pallas_call | solution.py:93
  25.8 0.0 collective-permute-done.before
  25.8 0.0 collective-permute-done.1.after
  25.8 3.9 %edges.3 = (bf16[512,128]{1,0:T(8,128)(2,1)S(1)}, bf16[512,128]{1,0:T(8,128)(2,1)S(1)}) custom-call(bf16[8,512,512]{2,1,0:T(8,128)(2,1)} %get-tuple-element.26.left, bf16[8,512,512]{2,1,0:T(8,128)(2,1)} %get-tuple-element.27.right, f32[2,512,128]{2,1,0:T(8,128)S(1)} %get-tuple-element.29.partial, bf16[512,128]{1,0:T(8,128)(2,1)S(1)} %collective-permute-done.before, ...), custom_call_target="tpu_custom_call" | custom-call | flops 134217728 | bytes 1048576 | tf_op jit(solution)/shard_map/edges/pallas_call | solution.py:126
  29.7 3.6 %collective-permute-start.2 = (bf16[512,128]{1,0:T(8,128)(2,1)S(1)}, bf16[512,128]{1,0:T(8,128)(2,1)S(1)}, u32[]{:S(2)}, u32[]{:S(2)}) collective-permute-start(bf16[512,128]{1,0:T(8,128)(2,1)S(1)} %get-tuple-element.34.last), channel_id=1, source_target_pairs={{0,1},{1,2},{2,3},{3,4},{4,5},{5,6},{6,7},{7,8},{8,9},{9,10},{10,1... | collective-permute-start | bytes 393224 | tf_op jit(solution)/shard_map/ppermute | solution.py:270
  33.4 1.9 %collective-permute-start.3 = (bf16[512,128]{1,0:T(8,128)(2,1)S(1)}, bf16[512,128]{1,0:T(8,128)(2,1)S(1)}, u32[]{:S(2)}, u32[]{:S(2)}) collective-permute-start(bf16[512,128]{1,0:T(8,128)(2,1)S(1)} %get-tuple-element.32.first), channel_id=1, source_target_pairs={{1,0},{2,1},{3,2},{4,3},{5,4},{6,5},{7,6},{8,7},{9,8},{10,9},{11,1... | collective-permute-start | bytes 393224 | tf_op jit(solution)/shard_map/ppermute | solution.py:270
  35.3 6.1 %sweep.3 = (bf16[6,512,128]{2,1,0:T(8,128)(2,1)S(1)}, f32[2,512,128]{2,1,0:T(8,128)S(1)}) custom-call(bf16[8,512,512]{2,1,0:T(8,128)(2,1)} %get-tuple-element.26.left, bf16[8,512,512]{2,1,0:T(8,128)(2,1)} %get-tuple-element.27.right, f32[8,512,128]{2,1,0:T(8,128)} %get-tuple-element.28.start, bf16[512,128]{1,0:T(8,128)(2,1)S(1)} %get-tuple-element.32.first, ...), custom_call_target="tpu_custom_call" | custom-call | flops 1073741824 | bytes 8388608 | tf_op jit(solution)/shard_map/sweep/pallas_call | solution.py:144
  41.5 0.0 collective-permute-done.2.before
  41.5 0.0 collective-permute-done.3.after
  41.5 3.9 %edges.4 = (bf16[512,128]{1,0:T(8,128)(2,1)S(1)}, bf16[512,128]{1,0:T(8,128)(2,1)S(1)}) custom-call(bf16[8,512,512]{2,1,0:T(8,128)(2,1)} %get-tuple-element.26.left, bf16[8,512,512]{2,1,0:T(8,128)(2,1)} %get-tuple-element.27.right, f32[2,512,128]{2,1,0:T(8,128)S(1)} %get-tuple-element.35.partial, bf16[512,128]{1,0:T(8,128)(2,1)S(1)} %collective-permute-done.2.before, ...), custom_call_target="tpu_custom_call" | custom-call | flops 134217728 | bytes 1048576 | tf_op jit(solution)/shard_map/edges/pallas_call | solution.py:126
  45.4 3.6 %collective-permute-start.4 = (bf16[512,128]{1,0:T(8,128)(2,1)S(1)}, bf16[512,128]{1,0:T(8,128)(2,1)S(1)}, u32[]{:S(2)}, u32[]{:S(2)}) collective-permute-start(bf16[512,128]{1,0:T(8,128)(2,1)S(1)} %get-tuple-element.38.last), channel_id=1, source_target_pairs={{0,1},{1,2},{2,3},{3,4},{4,5},{5,6},{6,7},{7,8},{8,9},{9,10},{10,1... | collective-permute-start | bytes 393224 | tf_op jit(solution)/shard_map/ppermute | solution.py:270
  49.0 1.9 %collective-permute-start.5 = (bf16[512,128]{1,0:T(8,128)(2,1)S(1)}, bf16[512,128]{1,0:T(8,128)(2,1)S(1)}, u32[]{:S(2)}, u32[]{:S(2)}) collective-permute-start(bf16[512,128]{1,0:T(8,128)(2,1)S(1)} %get-tuple-element.36.first), channel_id=1, source_target_pairs={{1,0},{2,1},{3,2},{4,3},{5,4},{6,5},{7,6},{8,7},{9,8},{10,9},{11,1... | collective-permute-start | bytes 393224 | tf_op jit(solution)/shard_map/ppermute | solution.py:270
  51.0 6.1 %sweep.4 = (bf16[6,512,128]{2,1,0:T(8,128)(2,1)S(1)}, f32[2,512,128]{2,1,0:T(8,128)S(1)}) custom-call(bf16[8,512,512]{2,1,0:T(8,128)(2,1)} %get-tuple-element.26.left, bf16[8,512,512]{2,1,0:T(8,128)(2,1)} %get-tuple-element.27.right, f32[8,512,128]{2,1,0:T(8,128)} %get-tuple-element.28.start, bf16[512,128]{1,0:T(8,128)(2,1)S(1)} %get-tuple-element.36.first, ...), custom_call_target="tpu_custom_call" | custom-call | flops 1073741824 | bytes 8388608 | tf_op jit(solution)/shard_map/sweep/pallas_call | solution.py:144
  57.1 0.0 collective-permute-done.4.before
  57.1 0.0 collective-permute-done.5.after
  57.1 3.9 %edges.5 = (bf16[512,128]{1,0:T(8,128)(2,1)S(1)}, bf16[512,128]{1,0:T(8,128)(2,1)S(1)}) custom-call(bf16[8,512,512]{2,1,0:T(8,128)(2,1)} %get-tuple-element.26.left, bf16[8,512,512]{2,1,0:T(8,128)(2,1)} %get-tuple-element.27.right, f32[2,512,128]{2,1,0:T(8,128)S(1)} %get-tuple-element.39.partial, bf16[512,128]{1,0:T(8,128)(2,1)S(1)} %collective-permute-done.4.before, ...), custom_call_target="tpu_custom_call" | custom-call | flops 134217728 | bytes 1048576 | tf_op jit(solution)/shard_map/edges/pallas_call | solution.py:126
  61.0 3.6 %collective-permute-start.6 = (bf16[512,128]{1,0:T(8,128)(2,1)S(1)}, bf16[512,128]{1,0:T(8,128)(2,1)S(1)}, u32[]{:S(2)}, u32[]{:S(2)}) collective-permute-start(bf16[512,128]{1,0:T(8,128)(2,1)S(1)} %get-tuple-element.42.last), channel_id=1, source_target_pairs={{0,1},{1,2},{2,3},{3,4},{4,5},{5,6},{6,7},{7,8},{8,9},{9,10},{10,1... | collective-permute-start | bytes 393224 | tf_op jit(solution)/shard_map/ppermute | solution.py:270
  64.7 1.9 %collective-permute-start.7 = (bf16[512,128]{1,0:T(8,128)(2,1)S(1)}, bf16[512,128]{1,0:T(8,128)(2,1)S(1)}, u32[]{:S(2)}, u32[]{:S(2)}) collective-permute-start(bf16[512,128]{1,0:T(8,128)(2,1)S(1)} %get-tuple-element.40.first), channel_id=1, source_target_pairs={{1,0},{2,1},{3,2},{4,3},{5,4},{6,5},{7,6},{8,7},{9,8},{10,9},{11,1... | collective-permute-start | bytes 393224 | tf_op jit(solution)/shard_map/ppermute | solution.py:270
  67.2 6.1 %sweep.5 = (bf16[6,512,128]{2,1,0:T(8,128)(2,1)S(1)}, f32[2,512,128]{2,1,0:T(8,128)S(1)}) custom-call(bf16[8,512,512]{2,1,0:T(8,128)(2,1)} %get-tuple-element.26.left, bf16[8,512,512]{2,1,0:T(8,128)(2,1)} %get-tuple-element.27.right, f32[8,512,128]{2,1,0:T(8,128)} %get-tuple-element.28.start, bf16[512,128]{1,0:T(8,128)(2,1)S(1)} %get-tuple-element.40.first, ...), custom_call_target="tpu_custom_call" | custom-call | flops 1073741824 | bytes 8388608 | tf_op jit(solution)/shard_map/sweep/pallas_call | solution.py:144
  73.4 0.0 collective-permute-done.6.before
  73.4 0.0 collective-permute-done.7.after
  73.4 4.0 %finish.1 = bf16[8,528,128]{2,1,0:T(8,128)(2,1)S(1)} custom-call(f32[1]{0:T(128)S(6)} %copy.6.weight, bf16[8,512,512]{2,1,0:T(8,128)(2,1)} %get-tuple-element.26.left, bf16[8,512,512]{2,1,0:T(8,128)(2,1)} %get-tuple-element.27.right, f32[2,512,128]{2,1,0:T(8,128)S(1)} %get-tuple-element.43.partial, bf16[512,128]{1,0:T(8,128)(2,1)S(1)} %collective-permute-done.6.before, ...), custom_call_target="tpu_custom_call" | custom-call | flops 134217728 | bytes 1048576 | tf_op jit(solution)/shard_map/finish/pallas_call | solution.py:180
  77.4 23.4 %all_to_all.20.received = bf16[8,528,128]{2,1,0:T(8,128)(2,1)S(1)} all-to-all(bf16[8,528,128]{2,1,0:T(8,128)(2,1)S(1)} %finish.1), channel_id=1, replica_groups=mesh['x_hi'=2,'y'=4,'x_lo'=2,'z'=8,'core'=2] {'x_hi','y'}, dimensions={0} | all-to-all | bytes 2162688 | tf_op jit(solution)/shard_map/all_to_all | solution.py:274
  100.7 0.6 gram.1
  101.3 11.9 %all_to_all.21 = f32[16,8,128]{2,1,0:T(8,128)S(1)} all-to-all(f32[16,8,128]{2,1,0:T(8,128)S(1)} %get-tuple-element.45), channel_id=1, replica_groups=mesh['x_hi'=2,'y'=4,'x_lo'=2,'z'=8,'core'=2] {'x_hi','y','x_lo'}, dimensions={0} | all-to-all | bytes 131072 | tf_op jit(solution)/shard_map/all_to_all | solution.py:274
  113.2 18.3 %all_to_all.22 = f32[16,8,128]{2,1,0:T(8,128)S(1)} all-to-all(f32[16,8,128]{2,1,0:T(8,128)S(1)} %broadcast_in_dim.4), channel_id=1, replica_groups=mesh['x_hi'=2,'y'=4,'x_lo'=2,'z'=8,'core'=2] {'z','core'}, dimensions={0} | all-to-all | bytes 131072 | tf_op jit(solution)/shard_map/all_to_all | solution.py:274
  131.6 9.4 %all_to_all.23.gram = f32[16,8,128]{2,1,0:T(8,128)S(1)} all-to-all(f32[16,8,128]{2,1,0:T(8,128)S(1)} %broadcast_in_dim.5), channel_id=1, replica_groups=mesh['x_hi'=2,'y'=4,'x_lo'=2,'z'=8,'core'=2] {'x_hi','y','x_lo'}, dimensions={0} | all-to-all | bytes 131072 | tf_op jit(solution)/shard_map/all_to_all | solution.py:274
  141.0 16.8 %orthonormal.1 = f32[512,128]{1,0:T(8,128)} custom-call(f32[16,8,128]{2,1,0:T(8,128)S(1)} %all_to_all.23.gram, f32[512,128]{1,0:T(8,128)S(1)} %get-tuple-element.46.filtered), custom_call_target="tpu_custom_call" | custom-call | tf_op jit(solution)/shard_map/orthonormal/pallas_call | solution.py:249
  (4 shorter events, 0.1 us)
Async XLA Ops:
  0.0 1.2 copy-start
  2.9 23.0 %collective-permute-start = (bf16[512,128]{1,0:T(8,128)(2,1)S(1)}, bf16[512,128]{1,0:T(8,128)(2,1)S(1)}, u32[]{:S(2)}, u32[]{:S(2)}) collective-permute-start(bf16[512,128]{1,0:T(8,128)(2,1)S(1)} %get-tuple-element.30), channel_id=1, source_target_pairs={{0,1},{1,2},{2,3},{3,4},{4,5},{5,6},{6,7},{7,8},{8,9},{9,10},{10,1... | collective-permute-start | bytes 393224 | tf_op jit(solution)/shard_map/ppermute | solution.py:270
  7.8 18.0 %collective-permute-start.1 = (bf16[512,128]{1,0:T(8,128)(2,1)S(1)}, bf16[512,128]{1,0:T(8,128)(2,1)S(1)}, u32[]{:S(2)}, u32[]{:S(2)}) collective-permute-start(bf16[512,128]{1,0:T(8,128)(2,1)S(1)} %get-tuple-element.31), channel_id=1, source_target_pairs={{1,0},{2,1},{3,2},{4,3},{5,4},{6,5},{7,6},{8,7},{9,8},{10,9},{11,1... | collective-permute-start | bytes 393224 | tf_op jit(solution)/shard_map/ppermute | solution.py:270
  29.7 11.7 %collective-permute-start.2 = (bf16[512,128]{1,0:T(8,128)(2,1)S(1)}, bf16[512,128]{1,0:T(8,128)(2,1)S(1)}, u32[]{:S(2)}, u32[]{:S(2)}) collective-permute-start(bf16[512,128]{1,0:T(8,128)(2,1)S(1)} %get-tuple-element.34.last), channel_id=1, source_target_pairs={{0,1},{1,2},{2,3},{3,4},{4,5},{5,6},{6,7},{7,8},{8,9},{9,10},{10,1... | collective-permute-start | bytes 393224 | tf_op jit(solution)/shard_map/ppermute | solution.py:270
  33.4 8.1 %collective-permute-start.3 = (bf16[512,128]{1,0:T(8,128)(2,1)S(1)}, bf16[512,128]{1,0:T(8,128)(2,1)S(1)}, u32[]{:S(2)}, u32[]{:S(2)}) collective-permute-start(bf16[512,128]{1,0:T(8,128)(2,1)S(1)} %get-tuple-element.32.first), channel_id=1, source_target_pairs={{1,0},{2,1},{3,2},{4,3},{5,4},{6,5},{7,6},{8,7},{9,8},{10,9},{11,1... | collective-permute-start | bytes 393224 | tf_op jit(solution)/shard_map/ppermute | solution.py:270
  45.4 11.7 %collective-permute-start.4 = (bf16[512,128]{1,0:T(8,128)(2,1)S(1)}, bf16[512,128]{1,0:T(8,128)(2,1)S(1)}, u32[]{:S(2)}, u32[]{:S(2)}) collective-permute-start(bf16[512,128]{1,0:T(8,128)(2,1)S(1)} %get-tuple-element.38.last), channel_id=1, source_target_pairs={{0,1},{1,2},{2,3},{3,4},{4,5},{5,6},{6,7},{7,8},{8,9},{9,10},{10,1... | collective-permute-start | bytes 393224 | tf_op jit(solution)/shard_map/ppermute | solution.py:270
  49.0 8.1 %collective-permute-start.5 = (bf16[512,128]{1,0:T(8,128)(2,1)S(1)}, bf16[512,128]{1,0:T(8,128)(2,1)S(1)}, u32[]{:S(2)}, u32[]{:S(2)}) collective-permute-start(bf16[512,128]{1,0:T(8,128)(2,1)S(1)} %get-tuple-element.36.first), channel_id=1, source_target_pairs={{1,0},{2,1},{3,2},{4,3},{5,4},{6,5},{7,6},{8,7},{9,8},{10,9},{11,1... | collective-permute-start | bytes 393224 | tf_op jit(solution)/shard_map/ppermute | solution.py:270
  61.0 12.4 %collective-permute-start.6 = (bf16[512,128]{1,0:T(8,128)(2,1)S(1)}, bf16[512,128]{1,0:T(8,128)(2,1)S(1)}, u32[]{:S(2)}, u32[]{:S(2)}) collective-permute-start(bf16[512,128]{1,0:T(8,128)(2,1)S(1)} %get-tuple-element.42.last), channel_id=1, source_target_pairs={{0,1},{1,2},{2,3},{3,4},{4,5},{5,6},{6,7},{7,8},{8,9},{9,10},{10,1... | collective-permute-start | bytes 393224 | tf_op jit(solution)/shard_map/ppermute | solution.py:270
  64.7 8.7 %collective-permute-start.7 = (bf16[512,128]{1,0:T(8,128)(2,1)S(1)}, bf16[512,128]{1,0:T(8,128)(2,1)S(1)}, u32[]{:S(2)}, u32[]{:S(2)}) collective-permute-start(bf16[512,128]{1,0:T(8,128)(2,1)S(1)} %get-tuple-element.40.first), channel_id=1, source_target_pairs={{1,0},{2,1},{3,2},{4,3},{5,4},{6,5},{7,6},{8,7},{9,8},{10,9},{11,1... | collective-permute-start | bytes 393224 | tf_op jit(solution)/shard_map/ppermute | solution.py:270

commit v2 on v1

--- a/solution.py
+++ b/solution.py
@@ -13,14 +13,19 @@
 BF16 = jnp.bfloat16
 HI = lax.Precision.HIGHEST
 VM = pl.BlockSpec(memory_space=pltpu.VMEM)
+HBM = pl.BlockSpec(memory_space=pltpu.HBM)
 SM = pl.BlockSpec(memory_space=pltpu.SMEM)
-LIMIT = 50 << 20
+LIMIT = 16 << 20
 
 
 def dot(a, b):
     return jnp.dot(a, b, preferred_element_type=F32)
 
 
+def in_hbm(value):
+    return pltpu.with_memory_space_constraint(value, pltpu.HBM)
+
+
 def params():
     return pltpu.CompilerParams(vmem_limit_bytes=LIMIT)
 
@@ -29,31 +34,37 @@
     return pl.CostEstimate(flops=int(flops), bytes_accessed=int(moved), transcendentals=0)
 
 
-def first_edges_kernel(inv_a, inv_b, basis_a, basis_b, first, last):
-    first[...] = dot(inv_a[0, 0], basis_a[...]).astype(BF16)
-    last[...] = dot(inv_b[0, 0], basis_b[...]).astype(BF16)
+def first_edges_kernel(count, inverses, basis, first, last, inverse, block, sem):
+    size = first.shape[0]
+    copies = []
+    for slot, b in enumerate((0, count - 1)):
+        copies.append(pltpu.make_async_copy(inverses.at[0, b], inverse.at[slot], sem.at[2 * slot]))
+        copies.append(
+            pltpu.make_async_copy(basis.at[pl.ds(b * size, size)], block.at[slot], sem.at[2 * slot + 1])
+        )
+    for copy in copies:
+        copy.start()
+    for slot, out in enumerate((first, last)):
+        copies[2 * slot].wait()
+        copies[2 * slot + 1].wait()
+        out[...] = dot(inverse[slot], block[slot]).astype(BF16)
 
 
 def first_edges(inverses, basis, count, size, width):
-    edge = count - 1
     out = jax.ShapeDtypeStruct((size, width), BF16)
     return pl.pallas_call(
-        first_edges_kernel,
-        grid=(1,),
+        functools.partial(first_edges_kernel, count),
         out_shape=(out, out),
-        in_specs=[
-            pl.BlockSpec((1, 1, size, size), lambda i: (0, 0, 0, 0)),
-            pl.BlockSpec((1, 1, size, size), lambda i: (0, edge, 0, 0)),
-            pl.BlockSpec((size, width), lambda i: (0, 0)),
-            pl.BlockSpec((size, width), lambda i: (edge, 0)),
+        in_specs=[HBM] * 2,
+        out_specs=(VM, VM),
+        scratch_shapes=[
+            pltpu.VMEM((2, size, size), BF16),
+            pltpu.VMEM((2, size, width), BF16),
+            pltpu.SemaphoreType.DMA((4,)),
         ],
-        out_specs=(
-            pl.BlockSpec((size, width), lambda i: (0, 0)),
-            pl.BlockSpec((size, width), lambda i: (0, 0)),
-        ),
         compiler_params=params(),
         name="first_edges",
-    )(inverses, inverses, basis, basis)
+    )(in_hbm(inverses), in_hbm(basis))
 
 
 def advance(count, left, right, start, first, middle, last, out, partial):
@@ -65,34 +76,41 @@
         return middle[b - 1]
 
     for b in range(1, count - 1):
-        value = start[b] + dot(left[b], state(b - 1)) + dot(right[b], state(b + 1))
-        out[b - 1, : value.shape[0]] = value.astype(BF16)
-    partial[0] = start[0] + dot(right[0], state(1))
-    partial[1] = start[count - 1] + dot(left[count - 1], state(count - 2))
-
-
-def setup_kernel(count, inv, lower, upper, basis, left, right, start, middle, partial, held):
-    b = pl.program_id(0)
-    inverse = inv[0, 0]
-    left[b] = dot(inverse, lower[0]).astype(BF16)
-    right[b] = dot(inverse, upper[0]).astype(BF16)
-    value = dot(inverse, basis[...])
-    start[b] = value
-    held[b] = value.astype(BF16)
-
-    @pl.when(b == count - 1)
-    def _():
-        advance(
-            count, left, right, start, held[0],
-            [held[i] for i in range(1, count - 1)], held[count - 1], middle, partial,
-        )
+        value = start[b] + dot(left[b], state(b - 1)[...]) + dot(right[b], state(b + 1)[...])
+        out[b - 1] = value.astype(BF16)
+    partial[0] = start[0] + dot(right[0], state(1)[...])
+    partial[1] = start[count - 1] + dot(left[count - 1], state(count - 2)[...])
+
+
+def setup_kernel(
+    count, inv, lower, upper, basis, left, right, start, middle, partial, held, below, above, sem
+):
+    size = inv.shape[-1]
+    copies = []
+    for b in range(count):
+        copies.append(pltpu.make_async_copy(lower.at[b], below.at[b], sem.at[2 * b]))
+        copies.append(pltpu.make_async_copy(upper.at[b], above.at[b], sem.at[2 * b + 1]))
+    for copy in copies:
+        copy.start()
+    for b in range(count):
+        value = dot(inv[0, b], basis[b * size : (b + 1) * size])
+        start[b] = value
+        held[b] = value.astype(BF16)
+    for b in range(count):
+        copies[2 * b].wait()
+        left[b] = dot(inv[0, b], below[b]).astype(BF16)
+        copies[2 * b + 1].wait()
+        right[b] = dot(inv[0, b], above[b]).astype(BF16)
+    advance(
+        count, left, right, start, held.at[0],
+        [held.at[i] for i in range(1, count - 1)], held.at[count - 1], middle, partial,
+    )
 
 
 def setup(inverses, lower, upper, basis, count, size, width):
     flops = 2 * count * size * size * (2 * size + 3 * width)
     return pl.pallas_call(
         functools.partial(setup_kernel, count),
-        grid=(count,),
         out_shape=(
             jax.ShapeDtypeStruct((count, size, size), BF16),
             jax.ShapeDtypeStruct((count, size, size), BF16),
@@ -100,18 +118,18 @@
             jax.ShapeDtypeStruct((count - 2, size, width), BF16),
             jax.ShapeDtypeStruct((2, size, width), F32),
         ),
-        in_specs=[
-            pl.BlockSpec((1, 1, size, size), lambda b: (0, b, 0, 0)),
-            pl.BlockSpec((1, size, size), lambda b: (b, 0, 0)),
-            pl.BlockSpec((1, size, size), lambda b: (b, 0, 0)),
-            pl.BlockSpec((size, width), lambda b: (b, 0)),
+        in_specs=[VM, HBM, HBM, VM],
+        out_specs=(VM, VM, VM, VM, VM),
+        scratch_shapes=[
+            pltpu.VMEM((count, size, width), BF16),
+            pltpu.VMEM((count, size, size), BF16),
+            pltpu.VMEM((count, size, size), BF16),
+            pltpu.SemaphoreType.DMA((2 * count,)),
         ],
-        out_specs=(VM, VM, VM, VM, VM),
-        scratch_shapes=[pltpu.VMEM((count, size, width), BF16)],
         compiler_params=params(),
         cost_estimate=cost(flops, 6 * count * size * size),
         name="setup",
-    )(inverses, lower, upper, basis)
+    )(inverses, in_hbm(lower), in_hbm(upper), basis)
 
 
 def edges_kernel(count, left, right, partial, before, after, first, last):
@@ -135,7 +153,8 @@
 
 
 def sweep_kernel(count, left, right, start, first, middle, last, out, partial):
-    advance(count, left, right, start, first[...], middle, last[...], out, partial)
+    middles = [middle.at[i] for i in range(count - 2)]
+    advance(count, left, right, start, first, middles, last, out, partial)
 
 
 def sweep(left, right, start, first, middle, last):

time: 158 us -> 127 us (0.80)
  Pallas kernels: 69.1 us -> 37.8 us
  waiting for transfers between devices: 0.02 us -> 5.61 us
  starting transfers between devices: 23.5 us -> 21.3 us
  blocking collectives: 63 us -> 61.3 us
    pallas_call x3, Pallas kernels: 18.4 us -> 6.2 us  [sweep(): pl.pallas_call(functools.partial(sweep_kernel, count), out_shape=(jax.Sha...]
    pallas_call x3, Pallas kernels: 11.7 us -> 1.32 us  [edges(): pl.pallas_call(functools.partial(edges_kernel, count), out_shape=(out, ou...]
    ppermute x8, waiting for transfers between devices: 0.02 us -> 5.61 us  [neighbours(): return (lax.ppermute(last, ROW, up), lax.ppermute(first, ROW, down))]
    pallas_call x2, Pallas kernels: 17.7 us -> 12.4 us  [the longest x1 10.3 us: setup(): pl.pallas_call(functools.partial(setup_kernel, count), out_shape=(jax.Sha...]
    pallas_call x1, Pallas kernels: 3.96 us -> 0.5 us  [finish(): pl.pallas_call(functools.partial(finish_kernel, count, size), out_shape=j...]
    ppermute x8, starting transfers between devices: 23.5 us -> 21.3 us  [neighbours(): return (lax.ppermute(last, ROW, up), lax.ppermute(first, ROW, down))]
    all_to_all x4, blocking collectives: 63 us -> 61.3 us  [exchange(): return lax.all_to_all(value, axes, split_axis=0, concat_axis=0, tiled=True)]
  transfers between devices with their start and end apart: 8 -> 8, of which waited for: 0 -> 3; matrix products, arithmetic and copies ran while one was open for 0% -> 0% of each run, Pallas kernels for 22% -> 13%
where the time goes in v2:
time: 127 us
  blocking collectives  61.3 us (48%)
  Pallas kernels  37.8 us (30%)
  starting transfers between devices  21.3 us (17%)
  waiting for transfers between devices  5.61 us (4%)
    all_to_all x4, blocking collectives, exchange(): return lax.all_to_all(value, axes, split_axis=0, concat_axis=0, tiled=True)  61.3 us
    ppermute x8, starting transfers between devices, neighbours(): return (lax.ppermute(last, ROW, up), lax.ppermute(first, ROW, down))  21.3 us
    pallas_call x1, Pallas kernels, orthonormal(): pl.pallas_call(functools.partial(orthonormal_kernel, float(total_rows)),...  16.8 us
    pallas_call x1, Pallas kernels, setup(): pl.pallas_call(functools.partial(setup_kernel, count), out_shape=(jax.Sha...  10.3 us
    pallas_call x3, Pallas kernels, sweep(): pl.pallas_call(functools.partial(sweep_kernel, count), out_shape=(jax.Sha...  6.2 us
    ppermute x8, waiting for transfers between devices, neighbours(): return (lax.ppermute(last, ROW, up), lax.ppermute(first, ROW, down))  5.61 us
  transfers between devices with their start and end apart: 8, of which 3 were waited for; matrix products, arithmetic and copies ran while one was open for 0% of the time, Pallas kernels for 13%

profile of v2, /device:TPU:1, one launch (start us, length us, event | category | flops | bytes accessed | tf_op | source)
XLA Modules:
  0.0 126.8 jit_solution(474743240353432222)
XLA Ops:
  0.0 0.0 copy-start.1
  0.0 0.0 copy-start
  0.0 2.1 %first_edges.1 = (bf16[512,128]{1,0:T(8,128)(2,1)S(1)}, bf16[512,128]{1,0:T(8,128)(2,1)S(1)}) custom-call(bf16[1,8,512,512]{3,2,1,0:T(8,128)(2,1)} %inverses.1, bf16[4096,128]{1,0:T(8,128)(2,1)} %basis.3), custom_call_target="tpu_custom_call" | custom-call | tf_op jit(solution)/shard_map/first_edges/pallas_call | solution.py:55
  2.1 4.9 %collective-permute-start = (bf16[512,128]{1,0:T(8,128)(2,1)S(1)}, bf16[512,128]{1,0:T(8,128)(2,1)S(1)}, u32[]{:S(2)}, u32[]{:S(2)}) collective-permute-start(bf16[512,128]{1,0:T(8,128)(2,1)S(1)} %get-tuple-element.30), channel_id=1, source_target_pairs={{0,1},{1,2},{2,3},{3,4},{4,5},{5,6},{6,7},{7,8},{8,9},{9,10},{10,1... | collective-permute-start | bytes 393224 | tf_op jit(solution)/shard_map/ppermute | solution.py:289
  7.0 1.9 %collective-permute-start.1 = (bf16[512,128]{1,0:T(8,128)(2,1)S(1)}, bf16[512,128]{1,0:T(8,128)(2,1)S(1)}, u32[]{:S(2)}, u32[]{:S(2)}) collective-permute-start(bf16[512,128]{1,0:T(8,128)(2,1)S(1)} %get-tuple-element.31), channel_id=1, source_target_pairs={{1,0},{2,1},{3,2},{4,3},{5,4},{6,5},{7,6},{8,7},{9,8},{10,9},{11,1... | collective-permute-start | bytes 393224 | tf_op jit(solution)/shard_map/ppermute | solution.py:289
  9.0 0.0 copy-done.1
  9.0 0.0 copy-done
  9.0 10.3 %setup.1 = (bf16[8,512,512]{2,1,0:T(8,128)(2,1)S(1)}, bf16[8,512,512]{2,1,0:T(8,128)(2,1)S(1)}, f32[8,512,128]{2,1,0:T(8,128)S(1)}, bf16[6,512,128]{2,1,0:T(8,128)(2,1)S(1)}, f32[2,512,128]{2,1,0:T(8,128)S(1)}) custom-call(bf16[1,8,512,512]{3,2,1,0:T(8,128)(2,1)S(1)} %copy-done, bf16[8,512,512]{2,1,0:T(8,128)(2,1)} %lower.1, bf16[8,512,512]{2,1,0:T(8,128)(2,1)} %upper.1, ...), custom_call_target="tpu_custom_call" | custom-call | flops 5905580032 | bytes 12582912 | tf_op jit(solution)/shard_map/setup/pallas_call | solution.py:112
  19.3 0.0 collective-permute-done.before
  19.4 0.0 collective-permute-done.1.after
  19.4 0.4 edges.3
  19.8 3.6 %collective-permute-start.2 = (bf16[512,128]{1,0:T(8,128)(2,1)S(1)}, bf16[512,128]{1,0:T(8,128)(2,1)S(1)}, u32[]{:S(2)}, u32[]{:S(2)}) collective-permute-start(bf16[512,128]{1,0:T(8,128)(2,1)S(1)} %get-tuple-element.34.last), channel_id=1, source_target_pairs={{0,1},{1,2},{2,3},{3,4},{4,5},{5,6},{6,7},{7,8},{8,9},{9,10},{10,1... | collective-permute-start | bytes 393224 | tf_op jit(solution)/shard_map/ppermute | solution.py:289
  23.5 1.9 %collective-permute-start.3 = (bf16[512,128]{1,0:T(8,128)(2,1)S(1)}, bf16[512,128]{1,0:T(8,128)(2,1)S(1)}, u32[]{:S(2)}, u32[]{:S(2)}) collective-permute-start(bf16[512,128]{1,0:T(8,128)(2,1)S(1)} %get-tuple-element.32.first), channel_id=1, source_target_pairs={{1,0},{2,1},{3,2},{4,3},{5,4},{6,5},{7,6},{8,7},{9,8},{10,9},{11,1... | collective-permute-start | bytes 393224 | tf_op jit(solution)/shard_map/ppermute | solution.py:289
  25.4 2.1 %sweep.3 = (bf16[6,512,128]{2,1,0:T(8,128)(2,1)S(1)}, f32[2,512,128]{2,1,0:T(8,128)S(1)}) custom-call(bf16[8,512,512]{2,1,0:T(8,128)(2,1)S(1)} %get-tuple-element.26.left, bf16[8,512,512]{2,1,0:T(8,128)(2,1)S(1)} %get-tuple-element.27.right, f32[8,512,128]{2,1,0:T(8,128)S(1)} %get-tuple-element.28.start, bf16[512,128]{1,0:T(8,128)(2,1)S(1)} %get-tuple-element.32.first, ...), custom_call_target="tpu_custom_call" | custom-call | flops 1073741824 | bytes 8388608 | tf_op jit(solution)/shard_map/sweep/pallas_call | solution.py:163
  27.5 0.0 collective-permute-done.2.before
  27.5 2.3 %collective-permute-done.3.after = bf16[512,128]{1,0:T(8,128)(2,1)S(1)} collective-permute-done((bf16[512,128]{1,0:T(8,128)(2,1)S(1)}, bf16[512,128]{1,0:T(8,128)(2,1)S(1)}, u32[]{:S(2)}, u32[]{:S(2)}) %collective-permute-start.3) | collective-permute-done | bytes 131104 | tf_op jit(solution)/shard_map/ppermute | solution.py:289
  29.7 0.4 edges.4
  30.2 1.9 %collective-permute-start.4 = (bf16[512,128]{1,0:T(8,128)(2,1)S(1)}, bf16[512,128]{1,0:T(8,128)(2,1)S(1)}, u32[]{:S(2)}, u32[]{:S(2)}) collective-permute-start(bf16[512,128]{1,0:T(8,128)(2,1)S(1)} %get-tuple-element.38.last), channel_id=1, source_target_pairs={{0,1},{1,2},{2,3},{3,4},{4,5},{5,6},{6,7},{7,8},{8,9},{9,10},{10,1... | collective-permute-start | bytes 393224 | tf_op jit(solution)/shard_map/ppermute | solution.py:289
  32.1 2.4 %collective-permute-start.5 = (bf16[512,128]{1,0:T(8,128)(2,1)S(1)}, bf16[512,128]{1,0:T(8,128)(2,1)S(1)}, u32[]{:S(2)}, u32[]{:S(2)}) collective-permute-start(bf16[512,128]{1,0:T(8,128)(2,1)S(1)} %get-tuple-element.36.first), channel_id=1, source_target_pairs={{1,0},{2,1},{3,2},{4,3},{5,4},{6,5},{7,6},{8,7},{9,8},{10,9},{11,1... | collective-permute-start | bytes 393224 | tf_op jit(solution)/shard_map/ppermute | solution.py:289
  34.5 2.1 %sweep.4 = (bf16[6,512,128]{2,1,0:T(8,128)(2,1)S(1)}, f32[2,512,128]{2,1,0:T(8,128)S(1)}) custom-call(bf16[8,512,512]{2,1,0:T(8,128)(2,1)S(1)} %get-tuple-element.26.left, bf16[8,512,512]{2,1,0:T(8,128)(2,1)S(1)} %get-tuple-element.27.right, f32[8,512,128]{2,1,0:T(8,128)S(1)} %get-tuple-element.28.start, bf16[512,128]{1,0:T(8,128)(2,1)S(1)} %get-tuple-element.36.first, ...), custom_call_target="tpu_custom_call" | custom-call | flops 1073741824 | bytes 8388608 | tf_op jit(solution)/shard_map/sweep/pallas_call | solution.py:163
  36.6 0.0 collective-permute-done.4.before
  36.6 2.1 %collective-permute-done.5.after = bf16[512,128]{1,0:T(8,128)(2,1)S(1)} collective-permute-done((bf16[512,128]{1,0:T(8,128)(2,1)S(1)}, bf16[512,128]{1,0:T(8,128)(2,1)S(1)}, u32[]{:S(2)}, u32[]{:S(2)}) %collective-permute-start.5) | collective-permute-done | bytes 131104 | tf_op jit(solution)/shard_map/ppermute | solution.py:289
  38.7 0.4 edges.5
  39.1 1.9 %collective-permute-start.6 = (bf16[512,128]{1,0:T(8,128)(2,1)S(1)}, bf16[512,128]{1,0:T(8,128)(2,1)S(1)}, u32[]{:S(2)}, u32[]{:S(2)}) collective-permute-start(bf16[512,128]{1,0:T(8,128)(2,1)S(1)} %get-tuple-element.42.last), channel_id=1, source_target_pairs={{0,1},{1,2},{2,3},{3,4},{4,5},{5,6},{6,7},{7,8},{8,9},{9,10},{10,1... | collective-permute-start | bytes 393224 | tf_op jit(solution)/shard_map/ppermute | solution.py:289
  41.1 2.6 %collective-permute-start.7 = (bf16[512,128]{1,0:T(8,128)(2,1)S(1)}, bf16[512,128]{1,0:T(8,128)(2,1)S(1)}, u32[]{:S(2)}, u32[]{:S(2)}) collective-permute-start(bf16[512,128]{1,0:T(8,128)(2,1)S(1)} %get-tuple-element.40.first), channel_id=1, source_target_pairs={{1,0},{2,1},{3,2},{4,3},{5,4},{6,5},{7,6},{8,7},{9,8},{10,9},{11,1... | collective-permute-start | bytes 393224 | tf_op jit(solution)/shard_map/ppermute | solution.py:289
  44.3 2.1 %sweep.5 = (bf16[6,512,128]{2,1,0:T(8,128)(2,1)S(1)}, f32[2,512,128]{2,1,0:T(8,128)S(1)}) custom-call(bf16[8,512,512]{2,1,0:T(8,128)(2,1)S(1)} %get-tuple-element.26.left, bf16[8,512,512]{2,1,0:T(8,128)(2,1)S(1)} %get-tuple-element.27.right, f32[8,512,128]{2,1,0:T(8,128)S(1)} %get-tuple-element.28.start, bf16[512,128]{1,0:T(8,128)(2,1)S(1)} %get-tuple-element.40.first, ...), custom_call_target="tpu_custom_call" | custom-call | flops 1073741824 | bytes 8388608 | tf_op jit(solution)/shard_map/sweep/pallas_call | solution.py:163
  46.4 0.0 collective-permute-done.6.before
  46.4 1.2 collective-permute-done.7.after
  47.6 0.5 finish.1
  48.1 23.4 %all_to_all.20.received = bf16[8,528,128]{2,1,0:T(8,128)(2,1)S(1)} all-to-all(bf16[8,528,128]{2,1,0:T(8,128)(2,1)S(1)} %finish.1), channel_id=1, replica_groups=mesh['x_hi'=2,'y'=4,'x_lo'=2,'z'=8,'core'=2] {'x_hi','y'}, dimensions={0} | all-to-all | bytes 2162688 | tf_op jit(solution)/shard_map/all_to_all | solution.py:293
  71.5 0.6 gram.1
  72.1 9.7 %all_to_all.21 = f32[16,8,128]{2,1,0:T(8,128)S(1)} all-to-all(f32[16,8,128]{2,1,0:T(8,128)S(1)} %get-tuple-element.45), channel_id=1, replica_groups=mesh['x_hi'=2,'y'=4,'x_lo'=2,'z'=8,'core'=2] {'x_hi','y','x_lo'}, dimensions={0} | all-to-all | bytes 131072 | tf_op jit(solution)/shard_map/all_to_all | solution.py:293
  81.8 18.9 %all_to_all.22 = f32[16,8,128]{2,1,0:T(8,128)S(1)} all-to-all(f32[16,8,128]{2,1,0:T(8,128)S(1)} %broadcast_in_dim.4), channel_id=1, replica_groups=mesh['x_hi'=2,'y'=4,'x_lo'=2,'z'=8,'core'=2] {'z','core'}, dimensions={0} | all-to-all | bytes 131072 | tf_op jit(solution)/shard_map/all_to_all | solution.py:293
  100.7 9.3 %all_to_all.23.gram = f32[16,8,128]{2,1,0:T(8,128)S(1)} all-to-all(f32[16,8,128]{2,1,0:T(8,128)S(1)} %broadcast_in_dim.5), channel_id=1, replica_groups=mesh['x_hi'=2,'y'=4,'x_lo'=2,'z'=8,'core'=2] {'x_hi','y','x_lo'}, dimensions={0} | all-to-all | bytes 131072 | tf_op jit(solution)/shard_map/all_to_all | solution.py:293
  110.0 16.8 %orthonormal.1 = f32[512,128]{1,0:T(8,128)} custom-call(f32[16,8,128]{2,1,0:T(8,128)S(1)} %all_to_all.23.gram, f32[512,128]{1,0:T(8,128)S(1)} %get-tuple-element.46.filtered), custom_call_target="tpu_custom_call" | custom-call | tf_op jit(solution)/shard_map/orthonormal/pallas_call | solution.py:268
  (4 shorter events, 0.1 us)
Async XLA Ops:
  0.0 9.0 %copy-start.1 = (bf16[4096,128]{1,0:T(8,128)(2,1)S(1)}, bf16[4096,128]{1,0:T(8,128)(2,1)}, u32[]{:S(2)}) copy-start(bf16[4096,128]{1,0:T(8,128)(2,1)} %basis.3) | copy-start | bytes 3145732
  0.0 9.0 %copy-start = (bf16[1,8,512,512]{3,2,1,0:T(8,128)(2,1)S(1)}, bf16[1,8,512,512]{3,2,1,0:T(8,128)(2,1)}, u32[]{:S(2)}) copy-start(bf16[1,8,512,512]{3,2,1,0:T(8,128)(2,1)} %inverses.1) | copy-start | bytes 12582916
  2.1 17.2 %collective-permute-start = (bf16[512,128]{1,0:T(8,128)(2,1)S(1)}, bf16[512,128]{1,0:T(8,128)(2,1)S(1)}, u32[]{:S(2)}, u32[]{:S(2)}) collective-permute-start(bf16[512,128]{1,0:T(8,128)(2,1)S(1)} %get-tuple-element.30), channel_id=1, source_target_pairs={{0,1},{1,2},{2,3},{3,4},{4,5},{5,6},{6,7},{7,8},{8,9},{9,10},{10,1... | collective-permute-start | bytes 393224 | tf_op jit(solution)/shard_map/ppermute | solution.py:289
  7.0 12.3 %collective-permute-start.1 = (bf16[512,128]{1,0:T(8,128)(2,1)S(1)}, bf16[512,128]{1,0:T(8,128)(2,1)S(1)}, u32[]{:S(2)}, u32[]{:S(2)}) collective-permute-start(bf16[512,128]{1,0:T(8,128)(2,1)S(1)} %get-tuple-element.31), channel_id=1, source_target_pairs={{1,0},{2,1},{3,2},{4,3},{5,4},{6,5},{7,6},{8,7},{9,8},{10,9},{11,1... | collective-permute-start | bytes 393224 | tf_op jit(solution)/shard_map/ppermute | solution.py:289
  19.8 7.7 %collective-permute-start.2 = (bf16[512,128]{1,0:T(8,128)(2,1)S(1)}, bf16[512,128]{1,0:T(8,128)(2,1)S(1)}, u32[]{:S(2)}, u32[]{:S(2)}) collective-permute-start(bf16[512,128]{1,0:T(8,128)(2,1)S(1)} %get-tuple-element.34.last), channel_id=1, source_target_pairs={{0,1},{1,2},{2,3},{3,4},{4,5},{5,6},{6,7},{7,8},{8,9},{9,10},{10,1... | collective-permute-start | bytes 393224 | tf_op jit(solution)/shard_map/ppermute | solution.py:289
  23.5 6.3 %collective-permute-start.3 = (bf16[512,128]{1,0:T(8,128)(2,1)S(1)}, bf16[512,128]{1,0:T(8,128)(2,1)S(1)}, u32[]{:S(2)}, u32[]{:S(2)}) collective-permute-start(bf16[512,128]{1,0:T(8,128)(2,1)S(1)} %get-tuple-element.32.first), channel_id=1, source_target_pairs={{1,0},{2,1},{3,2},{4,3},{5,4},{6,5},{7,6},{8,7},{9,8},{10,9},{11,1... | collective-permute-start | bytes 393224 | tf_op jit(solution)/shard_map/ppermute | solution.py:289
  30.2 6.4 %collective-permute-start.4 = (bf16[512,128]{1,0:T(8,128)(2,1)S(1)}, bf16[512,128]{1,0:T(8,128)(2,1)S(1)}, u32[]{:S(2)}, u32[]{:S(2)}) collective-permute-start(bf16[512,128]{1,0:T(8,128)(2,1)S(1)} %get-tuple-element.38.last), channel_id=1, source_target_pairs={{0,1},{1,2},{2,3},{3,4},{4,5},{5,6},{6,7},{7,8},{8,9},{9,10},{10,1... | collective-permute-start | bytes 393224 | tf_op jit(solution)/shard_map/ppermute | solution.py:289
  32.1 6.6 %collective-permute-start.5 = (bf16[512,128]{1,0:T(8,128)(2,1)S(1)}, bf16[512,128]{1,0:T(8,128)(2,1)S(1)}, u32[]{:S(2)}, u32[]{:S(2)}) collective-permute-start(bf16[512,128]{1,0:T(8,128)(2,1)S(1)} %get-tuple-element.36.first), channel_id=1, source_target_pairs={{1,0},{2,1},{3,2},{4,3},{5,4},{6,5},{7,6},{8,7},{9,8},{10,9},{11,1... | collective-permute-start | bytes 393224 | tf_op jit(solution)/shard_map/ppermute | solution.py:289
  39.1 7.2 %collective-permute-start.6 = (bf16[512,128]{1,0:T(8,128)(2,1)S(1)}, bf16[512,128]{1,0:T(8,128)(2,1)S(1)}, u32[]{:S(2)}, u32[]{:S(2)}) collective-permute-start(bf16[512,128]{1,0:T(8,128)(2,1)S(1)} %get-tuple-element.42.last), channel_id=1, source_target_pairs={{0,1},{1,2},{2,3},{3,4},{4,5},{5,6},{6,7},{7,8},{8,9},{9,10},{10,1... | collective-permute-start | bytes 393224 | tf_op jit(solution)/shard_map/ppermute | solution.py:289
  41.1 6.6 %collective-permute-start.7 = (bf16[512,128]{1,0:T(8,128)(2,1)S(1)}, bf16[512,128]{1,0:T(8,128)(2,1)S(1)}, u32[]{:S(2)}, u32[]{:S(2)}) collective-permute-start(bf16[512,128]{1,0:T(8,128)(2,1)S(1)} %get-tuple-element.40.first), channel_id=1, source_target_pairs={{1,0},{2,1},{3,2},{4,3},{5,4},{6,5},{7,6},{8,7},{9,8},{10,9},{11,1... | collective-permute-start | bytes 393224 | tf_op jit(solution)/shard_map/ppermute | solution.py:289

commit v3 on v2

v3 whole, which is shorter than its diff:
```python
import functools

import jax
import jax.numpy as jnp
from jax import lax
from jax.experimental import pallas as pl
from jax.experimental.pallas import tpu as pltpu
from jax.sharding import Mesh, PartitionSpec as P

SWEEPS = 4
EXTRA = 16
F32 = jnp.float32
BF16 = jnp.bfloat16
HI = lax.Precision.HIGHEST
VM = pl.BlockSpec(memory_space=pltpu.VMEM)
HBM = pl.BlockSpec(memory_space=pltpu.HBM)
SM = pl.BlockSpec(memory_space=pltpu.SMEM)
LIMIT = 16 << 20


def dot(a, b):
    return jnp.dot(a, b, preferred_element_type=F32)


def in_hbm(value):
    return pltpu.with_memory_space_constraint(value, pltpu.HBM)


def params():
    return pltpu.CompilerParams(vmem_limit_bytes=LIMIT)


def cost(flops, moved):
    return pl.CostEstimate(flops=int(flops), bytes_accessed=int(moved), transcendentals=0)


class Side:
    def __init__(self, low, count):
        self.low = low
        self.edge = 0 if low else count - 1
        self.inner = 1 if low else count - 2

    def outward(self, lower, upper):
        return lower if self.low else upper

    def inward(self, lower, upper):
        return upper if self.low else lower


def sides(count):
    return Side(True, count), Side(False, count)


def rounded(value):
    return value.astype(BF16)


def first_edges_kernel(
    count, inverses, lower, upper, basis, low, high, local, inv, outward, inward, block, sem
):
    size, width = block.shape[-2:]
    copies = []
    for k, side in enumerate(sides(count)):
        group = []
        for j, b in enumerate((side.edge, side.inner)):
            group.append((inverses.at[0, b], inv.at[k, j]))
            group.append((basis.at[pl.ds(b * size, size)], block.at[k, j]))
        group.append((side.outward(lower, upper).at[side.edge], outward.at[k]))
        group.append((side.inward(lower, upper).at[side.edge], inward.at[k]))
        copies.append(
            [pltpu.make_async_copy(a, b, sem.at[6 * k + i]) for i, (a, b) in enumerate(group)]
        )
    for copy in copies[0] + copies[1]:
        copy.start()
    for k, out in enumerate((low, high)):
        for copy in copies[k]:
            copy.wait()
        out[:, :width] = rounded(dot(inv[k, 0], block[k, 0]))
        inner = rounded(dot(inv[k, 1], block[k, 1]))
        out[:, 2 * width :] = rounded(dot(inv[k, 0], outward[k]))
        rhs = block[k, 0].astype(F32) + dot(inward[k], inner)
        value = dot(inv[k, 0], rounded(rhs))
        out[:, width : 2 * width] = rounded(value)
        local[k] = value


def first_edges(inverses, lower, upper, basis, count, size, width):
    out = jax.ShapeDtypeStruct((size, 2 * width + size), BF16)
    return pl.pallas_call(
        functools.partial(first_edges_kernel, count),
        out_shape=(out, out, jax.ShapeDtypeStruct((2, size, width), F32)),
        in_specs=[HBM] * 4,
        out_specs=(VM, VM, VM),
        scratch_shapes=[
            pltpu.VMEM((2, 2, size, size), BF16),
            pltpu.VMEM((2, size, size), BF16),
            pltpu.VMEM((2, size, size), BF16),
            pltpu.VMEM((2, 2, size, width), BF16),
            pltpu.SemaphoreType.DMA((12,)),
        ],
        compiler_params=params(),
        name="first_edges",
    )(in_hbm(inverses), in_hbm(lower), in_hbm(upper), in_hbm(basis))


def right_side(basis, b, size):
    return basis[b * size : (b + 1) * size].astype(F32)


def two_sweeps(count, size, inv, lower, upper, basis, state, held, middle, known):
    for b in range(1, count - 1):
        rhs = right_side(basis, b, size) + dot(lower[b], state(b - 1)) + dot(upper[b], state(b + 1))
        held[b] = rounded(dot(inv[0, b], rounded(rhs)))
    for k, side in enumerate(sides(count)):
        step = 1 if side.low else -1
        for j, b in enumerate((side.edge, side.inner)):
            known[2 * k + j] = right_side(basis, b, size) + dot(
                side.inward(lower, upper)[b], held[b + step]
            )
    for b in range(2, count - 2):
        rhs = right_side(basis, b, size) + dot(lower[b], held[b - 1]) + dot(upper[b], held[b + 1])
        middle[b - 2] = rounded(dot(inv[0, b], rounded(rhs)))


def first_pair_kernel(
    count, inv, lower, upper, basis, low, high, below, above, middle, known, start, held, sem
):
    size, width = start.shape[1:]
    copies = []
    for b in range(count):
        copies.append(pltpu.make_async_copy(lower.at[b], below.at[b], sem.at[2 * b]))
        copies.append(pltpu.make_async_copy(upper.at[b], above.at[b], sem.at[2 * b + 1]))
    for copy in copies:
        copy.start()
    start[0] = low[:, :width]
    start[count - 1] = high[:, :width]
    for b in range(1, count - 1):
        start[b] = rounded(dot(inv[0, b], basis[b * size : (b + 1) * size]))
    for copy in copies:
        copy.wait()
    two_sweeps(count, size, inv, below, above, basis, lambda b: start[b], held, middle, known)


def pair_cost(count, size, width):
    return cost(12 * (count - 2) * size * size * width, 6 * count * size * size)


def first_pair(inverses, lower, upper, basis, low, high, count, size, width):
    couplings = jax.ShapeDtypeStruct((count, size, size), BF16)
    return pl.pallas_call(
        functools.partial(first_pair_kernel, count),
        out_shape=(
            couplings,
            couplings,
            jax.ShapeDtypeStruct((count - 4, size, width), BF16),
            jax.ShapeDtypeStruct((4, size, width), F32),
        ),
        in_specs=[VM, HBM, HBM, VM, VM, VM],
        out_specs=(VM, VM, VM, VM),
        scratch_shapes=[
            pltpu.VMEM((count, size, width), BF16),
            pltpu.VMEM((count, size, width), BF16),
            pltpu.SemaphoreType.DMA((2 * count,)),
        ],
        compiler_params=params(),
        cost_estimate=pair_cost(count, size, width),
        name="first_pair",
    )(inverses, in_hbm(lower), in_hbm(upper), basis, low, high)


def pair_kernel(count, inv, lower, upper, basis, low, high, inner, previous, middle, known, held):
    size, width = held.shape[1:]

    def state(b):
        if b == 0:
            return low[:, :width]
        if b == count - 1:
            return high[:, :width]
        if b == 1:
            return inner[0]
        if b == count - 2:
            return inner[1]
        return previous[b - 2]

    two_sweeps(count, size, inv, lower, upper, basis, state, held, middle, known)


def pair(inverses, lower, upper, basis, low, high, inner, previous):
    count, size, _ = lower.shape
    width = basis.shape[-1]
    return pl.pallas_call(
        functools.partial(pair_kernel, count),
        out_shape=(
            jax.ShapeDtypeStruct((count - 4, size, width), BF16),
            jax.ShapeDtypeStruct((4, size, width), F32),
        ),
        in_specs=[VM] * 8,
        out_specs=(VM, VM),
        scratch_shapes=[pltpu.VMEM((count, size, width), BF16)],
        compiler_params=params(),
        cost_estimate=pair_cost(count, size, width),
        name="pair",
    )(inverses, lower, upper, basis, low, high, inner, previous)


def absorbed(k, side, inv, lower, upper, known, joint, halo_joint, own, halo, local):
    width = known.shape[-1]
    halo_next = rounded(
        halo[:, width : 2 * width].astype(F32) + dot(halo_joint[:, 2 * width :], own[:, :width])
    )
    edge_next = rounded(local[k] + dot(joint[:, 2 * width :], halo[:, :width]))
    out = []
    for j, (b, value) in enumerate(((side.edge, halo_next), (side.inner, edge_next))):
        rhs = known[2 * k + j] + dot(side.outward(lower, upper)[b], value)
        out.append(rounded(dot(inv[0, b], rounded(rhs))))
    return out


def meet_kernel(
    count, inv, lower, upper, basis, known, low, high, local, before, after,
    low_out, high_out, local_out, inner_out,
):
    size, width = known.shape[1:]
    pieces = ((low, before, low_out), (high, after, high_out))
    for k, (side, (own, halo, out)) in enumerate(zip(sides(count), pieces)):
        edge, inner = absorbed(k, side, inv, lower, upper, known, own, halo, own, halo, local)
        rhs = right_side(basis, side.edge, size) + dot(
            side.inward(lower, upper)[side.edge], inner
        )
        value = dot(inv[0, side.edge], rounded(rhs))
        out[:, :width] = edge
        out[:, width:] = rounded(value)
        local_out[k] = value
        inner_out[k] = inner


def meet(inverses, lower, upper, basis, known, low, high, local, before, after):
    count, size, _ = lower.shape
    width = basis.shape[-1]
    out = jax.ShapeDtypeStruct((size, 2 * width), BF16)
    return pl.pallas_call(
        functools.partial(meet_kernel, count),
        out_shape=(
            out,
            out,
            jax.ShapeDtypeStruct((2, size, width), F32),
            jax.ShapeDtypeStruct((2, size, width), BF16),
        ),
        in_specs=[VM] * 10,
        out_specs=(VM, VM, VM, VM),
        compiler_params=params(),
        cost_estimate=cost(32 * size * size * width, 24 * size * size),
        name="meet",
    )(inverses, lower, upper, basis, known, low, high, local, before, after)


def finish_kernel(
    count, weight, inv, lower, upper, known, middle, low_joint, high_joint, before_joint,
    after_joint, low, high, local, before, after, out,
):
    size, width = known.shape[1:]
    pieces = (
        (low_joint, before_joint, low, before),
        (high_joint, after_joint, high, after),
    )
    for k, (side, parts) in enumerate(zip(sides(count), pieces)):
        edge, inner = absorbed(k, side, inv, lower, upper, known, *parts, local)
        out[side.edge, :size] = edge
        out[side.inner, :size] = inner
    for b in range(2, count - 2):
        out[b, :size] = middle[b - 2]
    full = jnp.full((EXTRA, width), weight[0], F32)
    high_part = rounded(full)
    rest = full - high_part.astype(F32)
    mid_part = rounded(rest)
    low_part = rounded(rest - mid_part.astype(F32))
    place = lax.broadcasted_iota(jnp.int32, (EXTRA, width), 0)
    rows = jnp.where(
        place == 0,
        high_part.astype(F32),
        jnp.where(place == 1, mid_part.astype(F32), low_part.astype(F32)),
    )
    for b in range(count):
        out[b, size:] = rounded(rows)


def finish(weight, inverses, lower, upper, known, middle, *pieces):
    count, size, _ = lower.shape
    width = known.shape[-1]
    return pl.pallas_call(
        functools.partial(finish_kernel, count),
        out_shape=jax.ShapeDtypeStruct((count, size + EXTRA, width), BF16),
        in_specs=[SM] + [VM] * (5 + len(pieces)),
        out_specs=VM,
        compiler_params=params(),
        cost_estimate=cost(24 * size * size * width, 24 * size * size),
        name="finish",
    )(weight, inverses, lower, upper, known, middle, *pieces)


def gram_kernel(size, parts, received, filtered, gram):
    total = None
    for p in range(received.shape[0]):
        rows = received[p, size : size + 3].astype(F32)
        weight = rows[0:1] + rows[1:2] + rows[2:3]
        term = weight * received[p, :size].astype(F32)
        total = term if total is None else total + term
    filtered[...] = total
    value = lax.dot_general(
        total, total, (((0,), (0,)), ((), ())), precision=HI, preferred_element_type=F32
    )
    gram[...] = value.reshape(gram.shape)


def partial_gram(received, parts):
    poles, rows, width = received.shape
    size = rows - EXTRA
    return pl.pallas_call(
        functools.partial(gram_kernel, size, parts),
        out_shape=(
            jax.ShapeDtypeStruct((size, width), F32),
            jax.ShapeDtypeStruct((parts, width // parts, width), F32),
        ),
        in_specs=[VM],
        out_specs=(VM, VM),
        compiler_params=params(),
        name="gram",
    )(received)


def eliminate(value, work, inverse):
    n = value.shape[-1]
    subs = lax.broadcasted_iota(jnp.int32, (8, 2 * n), 0)
    work[:, :n] = value
    work[:, n:] = (
        lax.broadcasted_iota(jnp.int32, (n, n), 0) == lax.broadcasted_iota(jnp.int32, (n, n), 1)
    ).astype(F32)
    for p in range(n // 8):
        rows = work[8 * p : 8 * p + 8, :]
        for j in range(8):
            column = rows[:, 8 * p + j : 8 * p + j + 1]
            scale = lax.rsqrt(column[j : j + 1])
            pivot = rows[j : j + 1] * scale
            rows = jnp.where(
                subs == j, pivot, jnp.where(subs > j, rows - (column * scale) * pivot, rows)
            )
        work[8 * p : 8 * p + 8, :] = rows
        if 8 * p + 8 < n:
            change = lax.dot_general(
                rows[:, :n], rows, (((0,), (0,)), ((), ())), precision=HI, preferred_element_type=F32
            )
            work[8 * p + 8 :, :] = work[8 * p + 8 :, :] - change[8 * p + 8 :, :]
    inverse[...] = work[:, n:]


def orthonormal_kernel(total_rows, gram, filtered, out, work, inverse):
    n = out.shape[-1]
    value = gram[...].reshape(n, n) / total_rows
    rows = lax.broadcasted_iota(jnp.int32, (n, n), 0)
    cols = lax.broadcasted_iota(jnp.int32, (n, n), 1)
    same = rows == cols

    def phi(x):
        return jnp.where(rows > cols, x, jnp.where(same, 0.5 * x, 0.0))

    def exact(a, b):
        return jnp.dot(a, b, precision=HI, preferred_element_type=F32)

    def short(a, b):
        return dot(rounded(a), rounded(b))

    diagonal = jnp.where(same, value, 0.0)
    across = lax.rsqrt(jnp.sum(diagonal, axis=0, keepdims=True))
    down = lax.rsqrt(jnp.sum(diagonal, axis=1, keepdims=True))
    excess = jnp.where(same, 0.0, value * across * down)
    first = jnp.where(rows > cols, excess, 0.0)
    first_t = excess - first
    product = exact(first, excess)
    second_excess = -product - exact(first_t - product, first_t)
    second = phi(second_excess)
    second_t = second_excess - second
    product = short(second, second_excess)
    third_excess = -product - short(second_t - product, second_t)
    third = phi(third_excess)
    factor = exact(second, first) - first - second
    factor = jnp.where(same, 1.0 + factor, factor)
    factor = factor - short(third, factor)
    inverse[...] = factor * across
    error = jnp.sum(third_excess * third_excess)

    @pl.when(jnp.logical_not(error < 1e-7))
    def _():
        eliminate(value, work, inverse)

    out[...] = lax.dot_general(
        filtered[...], inverse[...], (((1,), (1,)), ((), ())), precision=HI, preferred_element_type=F32
    )


def orthonormal(gram, filtered, total_rows):
    n = filtered.shape[-1]
    return pl.pallas_call(
        functools.partial(orthonormal_kernel, float(total_rows)),
        out_shape=jax.ShapeDtypeStruct(filtered.shape, F32),
        in_specs=[VM, VM],
        out_specs=VM,
        scratch_shapes=[pltpu.VMEM((n, 2 * n), F32), pltpu.VMEM((n, n), F32)],
        compiler_params=params(),
        name="orthonormal",
    )(gram, filtered)


POLE = ("x_hi", "y")
ROW = ("x_lo", "z", "core")
PLANE = ("x_hi", "y", "x_lo")
LINE = ("z", "core")


def neighbours(first, last):
    peers = lax.axis_size(ROW)
    up = [(i, i + 1) for i in range(peers - 1)]
    down = [(j, i) for i, j in up]
    return lax.ppermute(last, ROW, up), lax.ppermute(first, ROW, down)


def exchange(value, axes):
    return lax.all_to_all(value, axes, split_axis=0, concat_axis=0, tiled=True)


def shards(basis, inverses, lower, upper, pole_weights):
    rows, width = basis.shape
    count = inverses.shape[1]
    size = inverses.shape[-1]
    low, high, local = first_edges(inverses, lower, upper, basis, count, size, width)
    joints = (low, high)
    before, after = halo_joints = neighbours(low, high)
    lower, upper, middle, known = first_pair(
        inverses, lower, upper, basis, low, high, count, size, width
    )
    for _ in range(SWEEPS // 2 - 1):
        low, high, local, inner = meet(
            inverses, lower, upper, basis, known, low, high, local, before, after
        )
        before, after = neighbours(low, high)
        middle, known = pair(inverses, lower, upper, basis, low, high, inner, middle)
    solved = finish(
        pole_weights, inverses, lower, upper, known, middle, *joints, *halo_joints,
        low, high, local, before, after,
    )
    received = exchange(solved, POLE)
    plane = lax.axis_size(PLANE)
    filtered, gram = partial_gram(received, plane)
    gram = exchange(gram, PLANE).sum(0, keepdims=True)
    line = lax.axis_size(LINE)
    gram = exchange(jnp.broadcast_to(gram, (line, *gram.shape[1:])), LINE).sum(0, keepdims=True)
    gram = exchange(jnp.broadcast_to(gram, (plane, *gram.shape[1:])), PLANE)
    return orthonormal(gram, filtered, rows * lax.axis_size(ROW))


def solution(mesh):
    devices = mesh.devices.reshape(2, 4, 2, 8, 2)
    inner = Mesh(devices, ("x_hi", "y", "x_lo", "z", "core"))
    return jax.shard_map(
        shards,
        mesh=inner,
        in_specs=(
            P(ROW, None),
            P(POLE, ROW, None, None),
            P(ROW, None, None),
            P(ROW, None, None),
            P(POLE),
        ),
        out_specs=P(ROW + POLE, None),
        check_vma=False,
    )
```

time: 127 us -> 125 us (0.984)
  Pallas kernels: 37.8 us -> 50.8 us
  starting transfers between devices: 21.3 us -> 12.8 us
  waiting for transfers between devices: 5.61 us -> 0.01 us
    pallas_call x8 -> x4, Pallas kernels: 18.4 us -> 28 us  [the longest x1 13.1 us: first_pair(): pl.pallas_call(functools.partial(first_pair_kernel, count), out_shape=(co...]
    ppermute x8 -> x4, starting transfers between devices: 21.3 us -> 12.8 us  [neighbours(): return (lax.ppermute(last, ROW, up), lax.ppermute(first, ROW, down))]
    ppermute x8 -> x4, waiting for transfers between devices: 5.61 us -> 0.01 us  [neighbours(): return (lax.ppermute(last, ROW, up), lax.ppermute(first, ROW, down))]
    pallas_call x1, Pallas kernels: 2.09 us -> 4.48 us  [first_edges(): pl.pallas_call(functools.partial(first_edges_kernel, count), out_shape=(o...]
  transfers between devices with their start and end apart: 8 -> 4, of which waited for: 3 -> 0; matrix products, arithmetic and copies ran while one was open for 0% -> 0% of each run, Pallas kernels for 13% -> 18%
where the time goes in v3:
time: 125 us
  blocking collectives  60.2 us (48%)
  Pallas kernels  50.8 us (41%)
  starting transfers between devices  12.8 us (10%)
    all_to_all x4, blocking collectives, exchange(): return lax.all_to_all(value, axes, split_axis=0, concat_axis=0, tiled=True)  60.2 us
    pallas_call x1, Pallas kernels, orthonormal(): pl.pallas_call(functools.partial(orthonormal_kernel, float(total_rows)),...  17.7 us
    pallas_call x1, Pallas kernels, first_pair(): pl.pallas_call(functools.partial(first_pair_kernel, count), out_shape=(co...  13.1 us
    ppermute x4, starting transfers between devices, neighbours(): return (lax.ppermute(last, ROW, up), lax.ppermute(first, ROW, down))  12.8 us
    pallas_call x1, Pallas kernels, pair(): pl.pallas_call(functools.partial(pair_kernel, count), out_shape=(jax.Shap...  9.34 us
    pallas_call x1, Pallas kernels, first_edges(): pl.pallas_call(functools.partial(first_edges_kernel, count), out_shape=(o...  4.48 us
    pallas_call x1, Pallas kernels, meet(): pl.pallas_call(functools.partial(meet_kernel, count), out_shape=(out, out...  3.44 us
  transfers between devices with their start and end apart: 4, of which 0 were waited for; matrix products, arithmetic and copies ran while one was open for 0% of the time, Pallas kernels for 18%

profile of v3, /device:TPU:1, one launch (start us, length us, event | category | flops | bytes accessed | tf_op | source)
XLA Modules:
  0.0 124.6 jit_solution(16757090594899562667)
XLA Ops:
  0.0 0.0 copy-start
  0.0 0.0 copy-start.1
  0.0 4.5 %first_edges.1 = (bf16[512,768]{1,0:T(8,128)(2,1)S(1)}, bf16[512,768]{1,0:T(8,128)(2,1)S(1)}, f32[2,512,128]{2,1,0:T(8,128)S(1)}) custom-call(bf16[1,8,512,512]{3,2,1,0:T(8,128)(2,1)} %inv.7, bf16[8,512,512]{2,1,0:T(8,128)(2,1)} %lower.3, bf16[8,512,512]{2,1,0:T(8,128)(2,1)} %upper.3, bf16[4096,128]{1,0:T(8,128)(2,1)} %basis.7), custom_call_target="tpu_custom_call" | custom-call | tf_op jit(solution)/shard_map/first_edges/pallas_call | solution.py:89
  4.5 5.1 %collective-permute-start.1 = (bf16[512,768]{1,0:T(8,128)(2,1)S(1)}, bf16[512,768]{1,0:T(8,128)(2,1)S(1)}, u32[]{:S(2)}, u32[]{:S(2)}) collective-permute-start(bf16[512,768]{1,0:T(8,128)(2,1)S(1)} %get-tuple-element.20.low.low_joint), channel_id=1, source_target_pairs={{1,0},{2,1},{3,2},{4,3},{5,4},{6,5},{7,6},{8,7},{9,8},{10,9},{11,1... | collective-permute-start | bytes 2359304 | tf_op jit(solution)/shard_map/ppermute | solution.py:423
  9.6 1.9 %collective-permute-start = (bf16[512,768]{1,0:T(8,128)(2,1)S(1)}, bf16[512,768]{1,0:T(8,128)(2,1)S(1)}, u32[]{:S(2)}, u32[]{:S(2)}) collective-permute-start(bf16[512,768]{1,0:T(8,128)(2,1)S(1)} %get-tuple-element.21.high.high_joint), channel_id=1, source_target_pairs={{0,1},{1,2},{2,3},{3,4},{4,5},{5,6},{6,7},{7,8},{8,9},{9,10},{10,1... | collective-permute-start | bytes 2359304 | tf_op jit(solution)/shard_map/ppermute | solution.py:423
  11.6 0.0 copy-done
  11.6 0.0 copy-done.1
  11.6 13.1 %first_pair.1 = (bf16[8,512,512]{2,1,0:T(8,128)(2,1)S(1)}, bf16[8,512,512]{2,1,0:T(8,128)(2,1)S(1)}, bf16[4,512,128]{2,1,0:T(8,128)(2,1)S(1)}, f32[4,512,128]{2,1,0:T(8,128)S(1)}) custom-call(bf16[1,8,512,512]{3,2,1,0:T(8,128)(2,1)S(1)} %copy-done, bf16[8,512,512]{2,1,0:T(8,128)(2,1)} %lower.3, bf16[8,512,512]{2,1,0:T(8,128)(2,1)} %upper.3, ...), custom_call_target="tpu_custom_call" | custom-call | flops 2415919104 | bytes 12582912 | tf_op jit(solution)/shard_map/first_pair/pallas_call | solution.py:150
  24.7 0.0 collective-permute-done.1.after.after_joint
  24.7 0.0 collective-permute-done.before.before_joint
  24.7 3.4 %meet.1 = (bf16[512,256]{1,0:T(8,128)(2,1)S(1)}, bf16[512,256]{1,0:T(8,128)(2,1)S(1)}, f32[2,512,128]{2,1,0:T(8,128)S(1)}, bf16[2,512,128]{2,1,0:T(8,128)(2,1)S(1)}) custom-call(bf16[1,8,512,512]{3,2,1,0:T(8,128)(2,1)S(1)} %copy-done, bf16[8,512,512]{2,1,0:T(8,128)(2,1)S(1)} %get-tuple-element.22.lower, bf16[8,512,512]{2,1,0:T(8,128)(2,1)S(1)} %get-tuple-element.23.upper, ...), custom_call_target="tpu_custom_call" | custom-call | flops 1073741824 | bytes 6291456 | tf_op jit(solution)/shard_map/meet/pallas_call | solution.py:241
  28.1 2.5 %collective-permute-start.3 = (bf16[512,256]{1,0:T(8,128)(2,1)S(1)}, bf16[512,256]{1,0:T(8,128)(2,1)S(1)}, u32[]{:S(2)}, u32[]{:S(2)}) collective-permute-start(bf16[512,256]{1,0:T(8,128)(2,1)S(1)} %get-tuple-element.26.low), channel_id=1, source_target_pairs={{1,0},{2,1},{3,2},{4,3},{5,4},{6,5},{7,6},{8,7},{9,8},{10,9},{11,1... | collective-permute-start | bytes 786440 | tf_op jit(solution)/shard_map/ppermute | solution.py:423
  30.6 3.3 %collective-permute-start.2 = (bf16[512,256]{1,0:T(8,128)(2,1)S(1)}, bf16[512,256]{1,0:T(8,128)(2,1)S(1)}, u32[]{:S(2)}, u32[]{:S(2)}) collective-permute-start(bf16[512,256]{1,0:T(8,128)(2,1)S(1)} %get-tuple-element.27.high), channel_id=1, source_target_pairs={{0,1},{1,2},{2,3},{3,4},{4,5},{5,6},{6,7},{7,8},{8,9},{9,10},{10,1... | collective-permute-start | bytes 786440 | tf_op jit(solution)/shard_map/ppermute | solution.py:423
  34.5 9.3 %pair.1 = (bf16[4,512,128]{2,1,0:T(8,128)(2,1)S(1)}, f32[4,512,128]{2,1,0:T(8,128)S(1)}) custom-call(bf16[1,8,512,512]{3,2,1,0:T(8,128)(2,1)S(1)} %copy-done, bf16[8,512,512]{2,1,0:T(8,128)(2,1)S(1)} %get-tuple-element.22.lower, bf16[8,512,512]{2,1,0:T(8,128)(2,1)S(1)} %get-tuple-element.23.upper, bf16[4096,128]{1,0:T(8,128)(2,1)S(1)} %copy-done.1, ...), custom_call_target="tpu_custom_call" | custom-call | flops 2415919104 | bytes 12582912 | tf_op jit(solution)/shard_map/pair/pallas_call | solution.py:191
  43.9 0.0 collective-permute-done.3.after
  43.9 0.0 collective-permute-done.2.before
  43.9 2.2 %finish.1 = bf16[8,528,128]{2,1,0:T(8,128)(2,1)S(1)} custom-call(f32[1]{0:T(128)S(6)} %copy.6.weight, bf16[1,8,512,512]{3,2,1,0:T(8,128)(2,1)S(1)} %copy-done, bf16[8,512,512]{2,1,0:T(8,128)(2,1)S(1)} %get-tuple-element.22.lower, bf16[8,512,512]{2,1,0:T(8,128)(2,1)S(1)} %get-tuple-element.23.upper, f32[4,512,128]{2,1,0:T(8,128)S(1)} %get-tuple-element.30.known, ...), custom_call_target="tpu_custom_call" | custom-call | flops 805306368 | bytes 6291456 | tf_op jit(solution)/shard_map/finish/pallas_call | solution.py:290
  46.1 23.8 %all_to_all.20.received = bf16[8,528,128]{2,1,0:T(8,128)(2,1)S(1)} all-to-all(bf16[8,528,128]{2,1,0:T(8,128)(2,1)S(1)} %finish.1), channel_id=1, replica_groups=mesh['x_hi'=2,'y'=4,'x_lo'=2,'z'=8,'core'=2] {'x_hi','y'}, dimensions={0} | all-to-all | bytes 2162688 | tf_op jit(solution)/shard_map/all_to_all | solution.py:427
  69.9 0.5 gram.1
  70.4 9.1 %all_to_all.21 = f32[16,8,128]{2,1,0:T(8,128)S(1)} all-to-all(f32[16,8,128]{2,1,0:T(8,128)S(1)} %get-tuple-element.33), channel_id=1, replica_groups=mesh['x_hi'=2,'y'=4,'x_lo'=2,'z'=8,'core'=2] {'x_hi','y','x_lo'}, dimensions={0} | all-to-all | bytes 131072 | tf_op jit(solution)/shard_map/all_to_all | solution.py:427
  79.5 17.9 %all_to_all.22 = f32[16,8,128]{2,1,0:T(8,128)S(1)} all-to-all(f32[16,8,128]{2,1,0:T(8,128)S(1)} %broadcast_in_dim.4), channel_id=1, replica_groups=mesh['x_hi'=2,'y'=4,'x_lo'=2,'z'=8,'core'=2] {'z','core'}, dimensions={0} | all-to-all | bytes 131072 | tf_op jit(solution)/shard_map/all_to_all | solution.py:427
  97.5 9.4 %all_to_all.23.gram = f32[16,8,128]{2,1,0:T(8,128)S(1)} all-to-all(f32[16,8,128]{2,1,0:T(8,128)S(1)} %broadcast_in_dim.5), channel_id=1, replica_groups=mesh['x_hi'=2,'y'=4,'x_lo'=2,'z'=8,'core'=2] {'x_hi','y','x_lo'}, dimensions={0} | all-to-all | bytes 131072 | tf_op jit(solution)/shard_map/all_to_all | solution.py:427
  106.9 17.7 %orthonormal.1 = f32[512,128]{1,0:T(8,128)} custom-call(f32[16,8,128]{2,1,0:T(8,128)S(1)} %all_to_all.23.gram, f32[512,128]{1,0:T(8,128)S(1)} %get-tuple-element.34.filtered), custom_call_target="tpu_custom_call" | custom-call | tf_op jit(solution)/shard_map/orthonormal/pallas_call | solution.py:402
  (4 shorter events, 0.1 us)
Async XLA Ops:
  0.0 11.6 %copy-start = (bf16[1,8,512,512]{3,2,1,0:T(8,128)(2,1)S(1)}, bf16[1,8,512,512]{3,2,1,0:T(8,128)(2,1)}, u32[]{:S(2)}) copy-start(bf16[1,8,512,512]{3,2,1,0:T(8,128)(2,1)} %inv.7) | copy-start | bytes 12582916
  0.0 11.6 %copy-start.1 = (bf16[4096,128]{1,0:T(8,128)(2,1)S(1)}, bf16[4096,128]{1,0:T(8,128)(2,1)}, u32[]{:S(2)}) copy-start(bf16[4096,128]{1,0:T(8,128)(2,1)} %basis.7) | copy-start | bytes 3145732
  4.5 20.2 %collective-permute-start.1 = (bf16[512,768]{1,0:T(8,128)(2,1)S(1)}, bf16[512,768]{1,0:T(8,128)(2,1)S(1)}, u32[]{:S(2)}, u32[]{:S(2)}) collective-permute-start(bf16[512,768]{1,0:T(8,128)(2,1)S(1)} %get-tuple-element.20.low.low_joint), channel_id=1, source_target_pairs={{1,0},{2,1},{3,2},{4,3},{5,4},{6,5},{7,6},{8,7},{9,8},{10,9},{11,1... | collective-permute-start | bytes 2359304 | tf_op jit(solution)/shard_map/ppermute | solution.py:423
  9.6 15.0 %collective-permute-start = (bf16[512,768]{1,0:T(8,128)(2,1)S(1)}, bf16[512,768]{1,0:T(8,128)(2,1)S(1)}, u32[]{:S(2)}, u32[]{:S(2)}) collective-permute-start(bf16[512,768]{1,0:T(8,128)(2,1)S(1)} %get-tuple-element.21.high.high_joint), channel_id=1, source_target_pairs={{0,1},{1,2},{2,3},{3,4},{4,5},{5,6},{6,7},{7,8},{8,9},{9,10},{10,1... | collective-permute-start | bytes 2359304 | tf_op jit(solution)/shard_map/ppermute | solution.py:423
  28.1 15.8 %collective-permute-start.3 = (bf16[512,256]{1,0:T(8,128)(2,1)S(1)}, bf16[512,256]{1,0:T(8,128)(2,1)S(1)}, u32[]{:S(2)}, u32[]{:S(2)}) collective-permute-start(bf16[512,256]{1,0:T(8,128)(2,1)S(1)} %get-tuple-element.26.low), channel_id=1, source_target_pairs={{1,0},{2,1},{3,2},{4,3},{5,4},{6,5},{7,6},{8,7},{9,8},{10,9},{11,1... | collective-permute-start | bytes 786440 | tf_op jit(solution)/shard_map/ppermute | solution.py:423
  30.6 13.3 %collective-permute-start.2 = (bf16[512,256]{1,0:T(8,128)(2,1)S(1)}, bf16[512,256]{1,0:T(8,128)(2,1)S(1)}, u32[]{:S(2)}, u32[]{:S(2)}) collective-permute-start(bf16[512,256]{1,0:T(8,128)(2,1)S(1)} %get-tuple-element.27.high), channel_id=1, source_target_pairs={{0,1},{1,2},{2,3},{3,4},{4,5},{5,6},{6,7},{7,8},{8,9},{9,10},{10,1... | collective-permute-start | bytes 786440 | tf_op jit(solution)/shard_map/ppermute | solution.py:423

commit v4 on v3

--- a/solution.py
+++ b/solution.py
@@ -59,28 +59,43 @@
     count, inverses, lower, upper, basis, low, high, local, inv, outward, inward, block, sem
 ):
     size, width = block.shape[-2:]
-    copies = []
-    for k, side in enumerate(sides(count)):
-        group = []
-        for j, b in enumerate((side.edge, side.inner)):
-            group.append((inverses.at[0, b], inv.at[k, j]))
-            group.append((basis.at[pl.ds(b * size, size)], block.at[k, j]))
-        group.append((side.outward(lower, upper).at[side.edge], outward.at[k]))
-        group.append((side.inward(lower, upper).at[side.edge], inward.at[k]))
-        copies.append(
-            [pltpu.make_async_copy(a, b, sem.at[6 * k + i]) for i, (a, b) in enumerate(group)]
-        )
-    for copy in copies[0] + copies[1]:
-        copy.start()
-    for k, out in enumerate((low, high)):
-        for copy in copies[k]:
-            copy.wait()
-        out[:, :width] = rounded(dot(inv[k, 0], block[k, 0]))
-        inner = rounded(dot(inv[k, 1], block[k, 1]))
-        out[:, 2 * width :] = rounded(dot(inv[k, 0], outward[k]))
-        rhs = block[k, 0].astype(F32) + dot(inward[k], inner)
-        value = dot(inv[k, 0], rounded(rhs))
-        out[:, width : 2 * width] = rounded(value)
+    both = list(enumerate(sides(count)))
+    outs = (low, high)
+    copies = {}
+
+    def begin(name, k, source, target):
+        copies[name, k] = pltpu.make_async_copy(source, target, sem.at[len(copies)])
+        copies[name, k].start()
+
+    for j in range(2):
+        for k, side in both:
+            b = side.inner if j else side.edge
+            begin(("basis", j), k, basis.at[pl.ds(b * size, size)], block.at[k, j])
+            begin(("inverse", j), k, inverses.at[0, b], inv.at[k, j])
+    for k, side in both:
+        begin("inward", k, side.inward(lower, upper).at[side.edge], inward.at[k])
+    for k, side in both:
+        begin("outward", k, side.outward(lower, upper).at[side.edge], outward.at[k])
+    inner = []
+    for j in range(2):
+        for k, side in both:
+            copies[("basis", j), k].wait()
+            copies[("inverse", j), k].wait()
+            value = rounded(dot(inv[k, j], block[k, j]))
+            if j:
+                inner.append(value)
+            else:
+                outs[k][:, :width] = value
+    rhs = []
+    for k, side in both:
+        copies["inward", k].wait()
+        rhs.append(rounded(block[k, 0].astype(F32) + dot(inward[k], inner[k])))
+    for k, side in both:
+        copies["outward", k].wait()
+        outs[k][:, 2 * width :] = rounded(dot(inv[k, 0], outward[k]))
+    for k, side in both:
+        value = dot(inv[k, 0], rhs[k])
+        outs[k][:, width : 2 * width] = rounded(value)
         local[k] = value
 
 
@@ -107,10 +122,15 @@
     return basis[b * size : (b + 1) * size].astype(F32)
 
 
-def two_sweeps(count, size, inv, lower, upper, basis, state, held, middle, known):
+def two_sweeps(count, size, inv, lower, upper, basis, state, held, rhs, middle, known):
     for b in range(1, count - 1):
-        rhs = right_side(basis, b, size) + dot(lower[b], state(b - 1)) + dot(upper[b], state(b + 1))
-        held[b] = rounded(dot(inv[0, b], rounded(rhs)))
+        value = right_side(basis, b, size) + dot(lower[b], state(b - 1)) + dot(upper[b], state(b + 1))
+        rhs[b] = rounded(value)
+    for b in range(1, count - 1):
+        held[b] = rounded(dot(inv[0, b], rhs[b]))
+    for b in range(2, count - 2):
+        value = right_side(basis, b, size) + dot(lower[b], held[b - 1]) + dot(upper[b], held[b + 1])
+        rhs[b] = rounded(value)
     for k, side in enumerate(sides(count)):
         step = 1 if side.low else -1
         for j, b in enumerate((side.edge, side.inner)):
@@ -118,27 +138,36 @@
                 side.inward(lower, upper)[b], held[b + step]
             )
     for b in range(2, count - 2):
-        rhs = right_side(basis, b, size) + dot(lower[b], held[b - 1]) + dot(upper[b], held[b + 1])
-        middle[b - 2] = rounded(dot(inv[0, b], rounded(rhs)))
+        middle[b - 2] = rounded(dot(inv[0, b], rhs[b]))
 
 
 def first_pair_kernel(
-    count, inv, lower, upper, basis, low, high, below, above, middle, known, start, held, sem
+    count, inverses, lower, upper, basis, low, high, inv, below, above, base, middle, known,
+    start, held, rhs, sem,
 ):
     size, width = start.shape[1:]
-    copies = []
+    blocks = [slice(b * size, (b + 1) * size) for b in range(count)]
+    loads = [
+        pltpu.make_async_copy(inverses.at[0, b], inv.at[0, b], sem.at[b]) for b in range(count)
+    ]
+    base_load = pltpu.make_async_copy(basis, base, sem.at[3 * count])
+    couplings = []
     for b in range(count):
-        copies.append(pltpu.make_async_copy(lower.at[b], below.at[b], sem.at[2 * b]))
-        copies.append(pltpu.make_async_copy(upper.at[b], above.at[b], sem.at[2 * b + 1]))
-    for copy in copies:
+        couplings.append(pltpu.make_async_copy(lower.at[b], below.at[b], sem.at[count + 2 * b]))
+        couplings.append(pltpu.make_async_copy(upper.at[b], above.at[b], sem.at[count + 2 * b + 1]))
+    base_load.start()
+    for copy in loads + couplings:
         copy.start()
     start[0] = low[:, :width]
     start[count - 1] = high[:, :width]
-    for b in range(1, count - 1):
-        start[b] = rounded(dot(inv[0, b], basis[b * size : (b + 1) * size]))
-    for copy in copies:
+    base_load.wait()
+    for b in range(count):
+        loads[b].wait()
+        if 0 < b < count - 1:
+            start[b] = rounded(dot(inv[0, b], base[blocks[b]]))
+    for copy in couplings:
         copy.wait()
-    two_sweeps(count, size, inv, below, above, basis, lambda b: start[b], held, middle, known)
+    two_sweeps(count, size, inv, below, above, base, lambda b: start[b], held, rhs, middle, known)
 
 
 def pair_cost(count, size, width):
@@ -150,25 +179,28 @@
     return pl.pallas_call(
         functools.partial(first_pair_kernel, count),
         out_shape=(
+            jax.ShapeDtypeStruct(inverses.shape, BF16),
             couplings,
             couplings,
+            jax.ShapeDtypeStruct(basis.shape, BF16),
             jax.ShapeDtypeStruct((count - 4, size, width), BF16),
             jax.ShapeDtypeStruct((4, size, width), F32),
         ),
-        in_specs=[VM, HBM, HBM, VM, VM, VM],
-        out_specs=(VM, VM, VM, VM),
+        in_specs=[HBM, HBM, HBM, HBM, VM, VM],
+        out_specs=(VM,) * 6,
         scratch_shapes=[
             pltpu.VMEM((count, size, width), BF16),
             pltpu.VMEM((count, size, width), BF16),
-            pltpu.SemaphoreType.DMA((2 * count,)),
+            pltpu.VMEM((count, size, width), BF16),
+            pltpu.SemaphoreType.DMA((3 * count + 1,)),
         ],
         compiler_params=params(),
         cost_estimate=pair_cost(count, size, width),
         name="first_pair",
-    )(inverses, in_hbm(lower), in_hbm(upper), basis, low, high)
-
-
-def pair_kernel(count, inv, lower, upper, basis, low, high, inner, previous, middle, known, held):
+    )(in_hbm(inverses), in_hbm(lower), in_hbm(upper), in_hbm(basis), low, high)
+
+
+def pair_kernel(count, inv, lower, upper, basis, low, high, inner, previous, middle, known, held, rhs):
     size, width = held.shape[1:]
 
     def state(b):
@@ -182,7 +214,7 @@
             return inner[1]
         return previous[b - 2]
 
-    two_sweeps(count, size, inv, lower, upper, basis, state, held, middle, known)
+    two_sweeps(count, size, inv, lower, upper, basis, state, held, rhs, middle, known)
 
 
 def pair(inverses, lower, upper, basis, low, high, inner, previous):
@@ -196,24 +228,32 @@
         ),
         in_specs=[VM] * 8,
         out_specs=(VM, VM),
-        scratch_shapes=[pltpu.VMEM((count, size, width), BF16)],
+        scratch_shapes=[pltpu.VMEM((count, size, width), BF16)] * 2,
         compiler_params=params(),
         cost_estimate=pair_cost(count, size, width),
         name="pair",
     )(inverses, lower, upper, basis, low, high, inner, previous)
 
 
-def absorbed(k, side, inv, lower, upper, known, joint, halo_joint, own, halo, local):
+def absorbed(count, inv, lower, upper, known, pieces, local):
     width = known.shape[-1]
-    halo_next = rounded(
-        halo[:, width : 2 * width].astype(F32) + dot(halo_joint[:, 2 * width :], own[:, :width])
-    )
-    edge_next = rounded(local[k] + dot(joint[:, 2 * width :], halo[:, :width]))
-    out = []
-    for j, (b, value) in enumerate(((side.edge, halo_next), (side.inner, edge_next))):
-        rhs = known[2 * k + j] + dot(side.outward(lower, upper)[b], value)
-        out.append(rounded(dot(inv[0, b], rounded(rhs))))
-    return out
+    both = list(enumerate(sides(count)))
+    values = []
+    for k, side in both:
+        joint, halo_joint, own, halo = pieces[k]
+        halo_next = halo[:, width : 2 * width].astype(F32) + dot(
+            halo_joint[:, 2 * width :], own[:, :width]
+        )
+        edge_next = local[k] + dot(joint[:, 2 * width :], halo[:, :width])
+        values.append((rounded(halo_next), rounded(edge_next)))
+    rhs = []
+    for j in (1, 0):
+        for k, side in both:
+            b = side.inner if j else side.edge
+            value = known[2 * k + j] + dot(side.outward(lower, upper)[b], values[k][j])
+            rhs.append((b, rounded(value)))
+    inner_low, inner_high, edge_low, edge_high = [rounded(dot(inv[0, b], value)) for b, value in rhs]
+    return (edge_low, edge_high), (inner_low, inner_high)
 
 
 def meet_kernel(
@@ -221,17 +261,22 @@
     low_out, high_out, local_out, inner_out,
 ):
     size, width = known.shape[1:]
-    pieces = ((low, before, low_out), (high, after, high_out))
-    for k, (side, (own, halo, out)) in enumerate(zip(sides(count), pieces)):
-        edge, inner = absorbed(k, side, inv, lower, upper, known, own, halo, own, halo, local)
-        rhs = right_side(basis, side.edge, size) + dot(
-            side.inward(lower, upper)[side.edge], inner
+    pieces = ((low, before, low, before), (high, after, high, after))
+    edge, inner = absorbed(count, inv, lower, upper, known, pieces, local)
+    both = list(enumerate(sides(count)))
+    outs = (low_out, high_out)
+    rhs = []
+    for k, side in both:
+        value = right_side(basis, side.edge, size) + dot(
+            side.inward(lower, upper)[side.edge], inner[k]
         )
-        value = dot(inv[0, side.edge], rounded(rhs))
-        out[:, :width] = edge
-        out[:, width:] = rounded(value)
+        rhs.append(rounded(value))
+        outs[k][:, :width] = edge[k]
+        inner_out[k] = inner[k]
+    for k, side in both:
+        value = dot(inv[0, side.edge], rhs[k])
+        outs[k][:, width:] = rounded(value)
         local_out[k] = value
-        inner_out[k] = inner
 
 
 def meet(inverses, lower, upper, basis, known, low, high, local, before, after):
@@ -263,10 +308,10 @@
         (low_joint, before_joint, low, before),
         (high_joint, after_joint, high, after),
     )
-    for k, (side, parts) in enumerate(zip(sides(count), pieces)):
-        edge, inner = absorbed(k, side, inv, lower, upper, known, *parts, local)
-        out[side.edge, :size] = edge
-        out[side.inner, :size] = inner
+    edge, inner = absorbed(count, inv, lower, upper, known, pieces, local)
+    for k, side in enumerate(sides(count)):
+        out[side.edge, :size] = edge[k]
+        out[side.inner, :size] = inner[k]
     for b in range(2, count - 2):
         out[b, :size] = middle[b - 2]
     full = jnp.full((EXTRA, width), weight[0], F32)
@@ -434,7 +479,7 @@
     low, high, local = first_edges(inverses, lower, upper, basis, count, size, width)
     joints = (low, high)
     before, after = halo_joints = neighbours(low, high)
-    lower, upper, middle, known = first_pair(
+    inverses, lower, upper, basis, middle, known = first_pair(
         inverses, lower, upper, basis, low, high, count, size, width
     )
     for _ in range(SWEEPS // 2 - 1):

time: 125 us -> 117 us (0.936)
  Pallas kernels: 50.8 us -> 41.6 us
  waiting for transfers between devices: 0.01 us -> 1.49 us
  starting transfers between devices: 12.8 us -> 11.4 us
    pallas_call x1, Pallas kernels: 9.34 us -> 4.78 us  [pair(): pl.pallas_call(functools.partial(pair_kernel, count), out_shape=(jax.Shap...]
    pallas_call x1, Pallas kernels: 13.1 us -> 9.88 us  [first_pair(): pl.pallas_call(functools.partial(first_pair_kernel, count), out_shape=(ja...]
    ppermute x4, waiting for transfers between devices: 0.01 us -> 1.49 us  [neighbours(): return (lax.ppermute(last, ROW, up), lax.ppermute(first, ROW, down))]
    ppermute x4, starting transfers between devices: 12.8 us -> 11.4 us  [neighbours(): return (lax.ppermute(last, ROW, up), lax.ppermute(first, ROW, down))]
  transfers between devices with their start and end apart: 4 -> 4, of which waited for: 0 -> 1; matrix products, arithmetic and copies ran while one was open for 0% -> 0% of each run, Pallas kernels for 18% -> 13%
where the time goes in v4:
time: 117 us; the launch traced here: 116 us
  blocking collectives  61.2 us (52%)
  Pallas kernels  41.6 us (36%)
  starting transfers between devices  11.4 us (10%)
  waiting for transfers between devices  1.49 us (1%)
    all_to_all x4, blocking collectives, exchange(): return lax.all_to_all(value, axes, split_axis=0, concat_axis=0, tiled=True)  61.2 us
    pallas_call x1, Pallas kernels, orthonormal(): pl.pallas_call(functools.partial(orthonormal_kernel, float(total_rows)),...  17.5 us
    ppermute x4, starting transfers between devices, neighbours(): return (lax.ppermute(last, ROW, up), lax.ppermute(first, ROW, down))  11.4 us
    pallas_call x1, Pallas kernels, first_pair(): pl.pallas_call(functools.partial(first_pair_kernel, count), out_shape=(ja...  9.88 us
    pallas_call x1, Pallas kernels, pair(): pl.pallas_call(functools.partial(pair_kernel, count), out_shape=(jax.Shap...  4.78 us
    pallas_call x1, Pallas kernels, first_edges(): pl.pallas_call(functools.partial(first_edges_kernel, count), out_shape=(o...  4.65 us
    pallas_call x1, Pallas kernels, meet(): pl.pallas_call(functools.partial(meet_kernel, count), out_shape=(out, out...  2.4 us
  transfers between devices with their start and end apart: 4, of which 1 were waited for; matrix products, arithmetic and copies ran while one was open for 0% of the time, Pallas kernels for 13%

profile of v4, /device:TPU:1, one launch (start us, length us, event | category | flops | bytes accessed | tf_op | source)
XLA Modules:
  0.0 116.4 jit_solution(18088478744584333941)
XLA Ops:
  0.0 4.6 %first_edges.1 = (bf16[512,768]{1,0:T(8,128)(2,1)S(1)}, bf16[512,768]{1,0:T(8,128)(2,1)S(1)}, f32[2,512,128]{2,1,0:T(8,128)S(1)}) custom-call(bf16[1,8,512,512]{3,2,1,0:T(8,128)(2,1)} %inverses.3, bf16[8,512,512]{2,1,0:T(8,128)(2,1)} %lower.3, bf16[8,512,512]{2,1,0:T(8,128)(2,1)} %upper.3, bf16[4096,128]{1,0:T(8,128)(2,1)} %basis.3), custom_call_target="tpu_custom_call" | custom-call | tf_op jit(solution)/shard_map/first_edges/pallas_call | solution.py:104
  4.7 4.9 %collective-permute-start = (bf16[512,768]{1,0:T(8,128)(2,1)S(1)}, bf16[512,768]{1,0:T(8,128)(2,1)S(1)}, u32[]{:S(2)}, u32[]{:S(2)}) collective-permute-start(bf16[512,768]{1,0:T(8,128)(2,1)S(1)} %get-tuple-element.23.high.high_joint), channel_id=1, source_target_pairs={{0,1},{1,2},{2,3},{3,4},{4,5},{5,6},{6,7},{7,8},{8,9},{9,10},{10,1... | collective-permute-start | bytes 2359304 | tf_op jit(solution)/shard_map/ppermute | solution.py:468
  9.6 1.9 %collective-permute-start.1 = (bf16[512,768]{1,0:T(8,128)(2,1)S(1)}, bf16[512,768]{1,0:T(8,128)(2,1)S(1)}, u32[]{:S(2)}, u32[]{:S(2)}) collective-permute-start(bf16[512,768]{1,0:T(8,128)(2,1)S(1)} %get-tuple-element.22.low.low_joint), channel_id=1, source_target_pairs={{1,0},{2,1},{3,2},{4,3},{5,4},{6,5},{7,6},{8,7},{9,8},{10,9},{11,1... | collective-permute-start | bytes 2359304 | tf_op jit(solution)/shard_map/ppermute | solution.py:468
  11.5 9.9 %first_pair.1 = (bf16[1,8,512,512]{3,2,1,0:T(8,128)(2,1)S(1)}, bf16[8,512,512]{2,1,0:T(8,128)(2,1)S(1)}, bf16[8,512,512]{2,1,0:T(8,128)(2,1)S(1)}, bf16[4096,128...) custom-call(bf16[1,8,512,512]{3,2,1,0:T(8,128)(2,1)} %inverses.3, ...), custom_call_target="tpu_custom_call" | custom-call | flops 2415919104 | bytes 12582912 | tf_op jit(solution)/shard_map/first_pair/pallas_call | solution.py:179
  21.4 0.0 collective-permute-done.before.before_joint
  21.4 1.5 %collective-permute-done.1.after.after_joint = bf16[512,768]{1,0:T(8,128)(2,1)S(1)} collective-permute-done((bf16[512,768]{1,0:T(8,128)(2,1)S(1)}, bf16[512,768]{1,0:T(8,128)(2,1)S(1)}, u32[]{:S(2)}, u32[]{:S(2)}) %collective-permute-start.1) | collective-permute-done | bytes 786464 | tf_op jit(solution)/shard_map/ppermute | solution.py:468
  22.9 2.4 %meet.1 = (bf16[512,256]{1,0:T(8,128)(2,1)S(1)}, bf16[512,256]{1,0:T(8,128)(2,1)S(1)}, f32[2,512,128]{2,1,0:T(8,128)S(1)}, bf16[2,512,128]{2,1,0:T(8,128)(2,1)S(1)}) custom-call(bf16[1,8,512,512]{3,2,1,0:T(8,128)(2,1)S(1)} %get-tuple-element.24.inv, bf16[8,512,512]{2,1,0:T(8,128)(2,1)S(1)} %get-tuple-element.25.lower, ...), custom_call_target="tpu_custom_call" | custom-call | flops 1073741824 | bytes 6291456 | tf_op jit(solution)/shard_map/meet/pallas_call | solution.py:286
  25.3 2.2 %collective-permute-start.2 = (bf16[512,256]{1,0:T(8,128)(2,1)S(1)}, bf16[512,256]{1,0:T(8,128)(2,1)S(1)}, u32[]{:S(2)}, u32[]{:S(2)}) collective-permute-start(bf16[512,256]{1,0:T(8,128)(2,1)S(1)} %get-tuple-element.31.high), channel_id=1, source_target_pairs={{0,1},{1,2},{2,3},{3,4},{4,5},{5,6},{6,7},{7,8},{8,9},{9,10},{10,1... | collective-permute-start | bytes 786440 | tf_op jit(solution)/shard_map/ppermute | solution.py:468
  27.5 2.3 %collective-permute-start.3 = (bf16[512,256]{1,0:T(8,128)(2,1)S(1)}, bf16[512,256]{1,0:T(8,128)(2,1)S(1)}, u32[]{:S(2)}, u32[]{:S(2)}) collective-permute-start(bf16[512,256]{1,0:T(8,128)(2,1)S(1)} %get-tuple-element.30.low), channel_id=1, source_target_pairs={{1,0},{2,1},{3,2},{4,3},{5,4},{6,5},{7,6},{8,7},{9,8},{10,9},{11,1... | collective-permute-start | bytes 786440 | tf_op jit(solution)/shard_map/ppermute | solution.py:468
  30.5 4.8 %pair.1 = (bf16[4,512,128]{2,1,0:T(8,128)(2,1)S(1)}, f32[4,512,128]{2,1,0:T(8,128)S(1)}) custom-call(bf16[1,8,512,512]{3,2,1,0:T(8,128)(2,1)S(1)} %get-tuple-element.24.inv, bf16[8,512,512]{2,1,0:T(8,128)(2,1)S(1)} %get-tuple-element.25.lower, bf16[8,512,512]{2,1,0:T(8,128)(2,1)S(1)} %get-tuple-element.26.upper, ...), custom_call_target="tpu_custom_call" | custom-call | flops 2415919104 | bytes 12582912 | tf_op jit(solution)/shard_map/pair/pallas_call | solution.py:223
  35.3 0.0 collective-permute-done.2.before
  35.3 0.0 collective-permute-done.3.after
  35.3 1.8 %finish.1 = bf16[8,528,128]{2,1,0:T(8,128)(2,1)S(1)} custom-call(f32[1]{0:T(128)S(6)} %copy.6.weight, bf16[1,8,512,512]{3,2,1,0:T(8,128)(2,1)S(1)} %get-tuple-element.24.inv, bf16[8,512,512]{2,1,0:T(8,128)(2,1)S(1)} %get-tuple-element.25.lower, bf16[8,512,512]{2,1,0:T(8,128)(2,1)S(1)} %get-tuple-element.26.upper, ...), custom_call_target="tpu_custom_call" | custom-call | flops 805306368 | bytes 6291456 | tf_op jit(solution)/shard_map/finish/pallas_call | solution.py:335
  37.1 24.4 %all_to_all.20.received = bf16[8,528,128]{2,1,0:T(8,128)(2,1)S(1)} all-to-all(bf16[8,528,128]{2,1,0:T(8,128)(2,1)S(1)} %finish.1), channel_id=1, replica_groups=mesh['x_hi'=2,'y'=4,'x_lo'=2,'z'=8,'core'=2] {'x_hi','y'}, dimensions={0} | all-to-all | bytes 2162688 | tf_op jit(solution)/shard_map/all_to_all | solution.py:472
  61.5 0.6 gram.1
  62.0 9.1 %all_to_all.21 = f32[16,8,128]{2,1,0:T(8,128)S(1)} all-to-all(f32[16,8,128]{2,1,0:T(8,128)S(1)} %get-tuple-element.37), channel_id=1, replica_groups=mesh['x_hi'=2,'y'=4,'x_lo'=2,'z'=8,'core'=2] {'x_hi','y','x_lo'}, dimensions={0} | all-to-all | bytes 131072 | tf_op jit(solution)/shard_map/all_to_all | solution.py:472
  71.1 18.4 %all_to_all.22 = f32[16,8,128]{2,1,0:T(8,128)S(1)} all-to-all(f32[16,8,128]{2,1,0:T(8,128)S(1)} %broadcast_in_dim.4), channel_id=1, replica_groups=mesh['x_hi'=2,'y'=4,'x_lo'=2,'z'=8,'core'=2] {'z','core'}, dimensions={0} | all-to-all | bytes 131072 | tf_op jit(solution)/shard_map/all_to_all | solution.py:472
  89.6 9.4 %all_to_all.23.gram = f32[16,8,128]{2,1,0:T(8,128)S(1)} all-to-all(f32[16,8,128]{2,1,0:T(8,128)S(1)} %broadcast_in_dim.5), channel_id=1, replica_groups=mesh['x_hi'=2,'y'=4,'x_lo'=2,'z'=8,'core'=2] {'x_hi','y','x_lo'}, dimensions={0} | all-to-all | bytes 131072 | tf_op jit(solution)/shard_map/all_to_all | solution.py:472
  98.9 17.5 %orthonormal.1 = f32[512,128]{1,0:T(8,128)} custom-call(f32[16,8,128]{2,1,0:T(8,128)S(1)} %all_to_all.23.gram, f32[512,128]{1,0:T(8,128)S(1)} %get-tuple-element.38.filtered), custom_call_target="tpu_custom_call" | custom-call | tf_op jit(solution)/shard_map/orthonormal/pallas_call | solution.py:447
  (4 shorter events, 0.1 us)
Async XLA Ops:
  4.7 16.8 %collective-permute-start = (bf16[512,768]{1,0:T(8,128)(2,1)S(1)}, bf16[512,768]{1,0:T(8,128)(2,1)S(1)}, u32[]{:S(2)}, u32[]{:S(2)}) collective-permute-start(bf16[512,768]{1,0:T(8,128)(2,1)S(1)} %get-tuple-element.23.high.high_joint), channel_id=1, source_target_pairs={{0,1},{1,2},{2,3},{3,4},{4,5},{5,6},{6,7},{7,8},{8,9},{9,10},{10,1... | collective-permute-start | bytes 2359304 | tf_op jit(solution)/shard_map/ppermute | solution.py:468
  9.6 13.3 %collective-permute-start.1 = (bf16[512,768]{1,0:T(8,128)(2,1)S(1)}, bf16[512,768]{1,0:T(8,128)(2,1)S(1)}, u32[]{:S(2)}, u32[]{:S(2)}) collective-permute-start(bf16[512,768]{1,0:T(8,128)(2,1)S(1)} %get-tuple-element.22.low.low_joint), channel_id=1, source_target_pairs={{1,0},{2,1},{3,2},{4,3},{5,4},{6,5},{7,6},{8,7},{9,8},{10,9},{11,1... | collective-permute-start | bytes 2359304 | tf_op jit(solution)/shard_map/ppermute | solution.py:468
  25.3 10.0 %collective-permute-start.2 = (bf16[512,256]{1,0:T(8,128)(2,1)S(1)}, bf16[512,256]{1,0:T(8,128)(2,1)S(1)}, u32[]{:S(2)}, u32[]{:S(2)}) collective-permute-start(bf16[512,256]{1,0:T(8,128)(2,1)S(1)} %get-tuple-element.31.high), channel_id=1, source_target_pairs={{0,1},{1,2},{2,3},{3,4},{4,5},{5,6},{6,7},{7,8},{8,9},{9,10},{10,1... | collective-permute-start | bytes 786440 | tf_op jit(solution)/shard_map/ppermute | solution.py:468
  27.5 7.8 %collective-permute-start.3 = (bf16[512,256]{1,0:T(8,128)(2,1)S(1)}, bf16[512,256]{1,0:T(8,128)(2,1)S(1)}, u32[]{:S(2)}, u32[]{:S(2)}) collective-permute-start(bf16[512,256]{1,0:T(8,128)(2,1)S(1)} %get-tuple-element.30.low), channel_id=1, source_target_pairs={{1,0},{2,1},{3,2},{4,3},{5,4},{6,5},{7,6},{8,7},{9,8},{10,9},{11,1... | collective-permute-start | bytes 786440 | tf_op jit(solution)/shard_map/ppermute | solution.py:468

commit v5 on v4

v5 whole, which is shorter than its diff:
```python
import functools

import jax
import jax.numpy as jnp
from jax import lax
from jax.experimental import pallas as pl
from jax.experimental.pallas import tpu as pltpu
from jax.sharding import Mesh, PartitionSpec as P

SWEEPS = 4
EXTRA = 16
F32 = jnp.float32
BF16 = jnp.bfloat16
HI = lax.Precision.HIGHEST
VM = pl.BlockSpec(memory_space=pltpu.VMEM)
HBM = pl.BlockSpec(memory_space=pltpu.HBM)
SM = pl.BlockSpec(memory_space=pltpu.SMEM)
LIMIT = 16 << 20


def dot(a, b):
    return jnp.dot(a, b, preferred_element_type=F32)


def in_hbm(value):
    return pltpu.with_memory_space_constraint(value, pltpu.HBM)


def params():
    return pltpu.CompilerParams(vmem_limit_bytes=LIMIT)


def cost(flops, moved):
    return pl.CostEstimate(flops=int(flops), bytes_accessed=int(moved), transcendentals=0)


class Side:
    def __init__(self, which, count):
        self.low = lax.axis_index("core") == which
        self.edge = jnp.where(self.low, 0, count - 1)
        self.inner = jnp.where(self.low, 1, count - 2)
        self.third = jnp.where(self.low, 2, count - 3)
        self.outward = jnp.where(self.low, 0, 1)
        self.inward = 1 - self.outward


def sides(count):
    return Side(0, count), Side(1, count)


def rounded(value):
    return value.astype(BF16)


def first_edges_kernel(
    count, inverses, lower, upper, basis, cross, chip, local, inv, coupling, base, sem
):
    width = base.shape[-1]
    last = count - 1
    copies = {}

    def begin(name, source, target):
        copies[name] = pltpu.make_async_copy(source, target, sem.at[len(copies)])
        copies[name].start()

    def finished(*names):
        for name in names:
            copies[name].wait()

    def begin_coupling(direction, b):
        begin(("coupling", direction, b), (lower, upper)[direction].at[b], coupling.at[direction, b])

    for b in (0, last, 1, last - 1):
        begin(("basis", b), basis.at[b], base.at[b])
        begin(("inverse", b), inverses.at[0, b], inv.at[b])
    begin_coupling(1, 0)
    begin_coupling(0, last)
    begin_coupling(0, 0)
    begin_coupling(1, last)
    early = list(copies)
    for b in range(2, last - 1):
        begin(("basis", b), basis.at[b], base.at[b])
        begin(("inverse", b), inverses.at[0, b], inv.at[b])
    for b in range(1, last):
        begin_coupling(0, b)
        begin_coupling(1, b)
    both = list(enumerate(sides(count)))
    outs = (cross, chip)
    finished(("basis", 0), ("inverse", 0), ("basis", last), ("inverse", last))
    for k, side in both:
        outs[k][:, :width] = rounded(dot(inv[side.edge], base[side.edge]))
    finished(("basis", 1), ("inverse", 1), ("basis", last - 1), ("inverse", last - 1))
    inner = [rounded(dot(inv[side.inner], base[side.inner])) for k, side in both]
    finished(("coupling", 1, 0), ("coupling", 0, last))
    rhs = []
    for k, side in both:
        value = dot(coupling[side.inward, side.edge], inner[k])
        rhs.append(rounded(base[side.edge].astype(F32) + value))
    finished(("coupling", 0, 0), ("coupling", 1, last))
    for k, side in both:
        outs[k][:, 2 * width :] = rounded(dot(inv[side.edge], coupling[side.outward, side.edge]))
    for k, side in both:
        value = dot(inv[side.edge], rhs[k])
        outs[k][:, width : 2 * width] = rounded(value)
        local[k] = value
    finished(*(name for name in copies if name not in early))


def first_edges(inverses, lower, upper, basis):
    count, size, width = basis.shape
    out = jax.ShapeDtypeStruct((size, 2 * width + size), BF16)
    return pl.pallas_call(
        functools.partial(first_edges_kernel, count),
        out_shape=(
            out,
            out,
            jax.ShapeDtypeStruct((2, size, width), F32),
            jax.ShapeDtypeStruct((count, size, size), BF16),
            jax.ShapeDtypeStruct((2, count, size, size), BF16),
            jax.ShapeDtypeStruct((count, size, width), BF16),
        ),
        in_specs=[HBM] * 4,
        out_specs=(VM,) * 6,
        scratch_shapes=[pltpu.SemaphoreType.DMA((4 * count,))],
        compiler_params=params(),
        name="first_edges",
    )(in_hbm(inverses), in_hbm(lower), in_hbm(upper), in_hbm(basis))


def two_sweeps(count, inv, coupling, base, state, held, rhs, middle, known):
    for b in range(1, count - 1):
        value = dot(coupling[0, b], state[b - 1]) + dot(coupling[1, b], state[b + 1])
        rhs[b] = rounded(base[b].astype(F32) + value)
    for b in range(1, count - 1):
        held[b] = rounded(dot(inv[b], rhs[b]))
    for b in range(2, count - 2):
        value = dot(coupling[0, b], held[b - 1]) + dot(coupling[1, b], held[b + 1])
        rhs[b] = rounded(base[b].astype(F32) + value)
    for k, side in enumerate(sides(count)):
        for j, (b, further) in enumerate(((side.edge, side.inner), (side.inner, side.third))):
            known[2 * k + j] = base[b].astype(F32) + dot(coupling[side.inward, b], held[further])
    for b in range(2, count - 2):
        middle[b - 2] = rounded(dot(inv[b], rhs[b]))


def first_pair_kernel(count, inv, coupling, base, cross, chip, middle, known, state, held, rhs):
    width = base.shape[-1]
    for side, payload in zip(sides(count), (cross, chip)):
        state[side.edge] = payload[:, :width]
    for b in range(1, count - 1):
        state[b] = rounded(dot(inv[b], base[b]))
    two_sweeps(count, inv, coupling, base, state, held, rhs, middle, known)


def pair_kernel(
    count, inv, coupling, base, cross, chip, inner, previous, middle, known, state, held, rhs
):
    width = base.shape[-1]
    for k, (side, payload) in enumerate(zip(sides(count), (cross, chip))):
        state[side.edge] = payload[:, :width]
        state[side.inner] = inner[k]
    for b in range(2, count - 2):
        state[b] = previous[b - 2]
    two_sweeps(count, inv, coupling, base, state, held, rhs, middle, known)


def pair_call(kernel, name, *operands):
    count, size, width = operands[2].shape
    flops = 12 * (count - 2) * size * size * width
    return pl.pallas_call(
        functools.partial(kernel, count),
        out_shape=(
            jax.ShapeDtypeStruct((count - 4, size, width), BF16),
            jax.ShapeDtypeStruct((4, size, width), F32),
        ),
        in_specs=[VM] * len(operands),
        out_specs=(VM, VM),
        scratch_shapes=[pltpu.VMEM((count, size, width), BF16)] * 3,
        compiler_params=params(),
        cost_estimate=cost(flops, 6 * count * size * size),
        name=name,
    )(*operands)


def absorbed(count, inv, coupling, known, pieces, local):
    width = known.shape[-1]
    both = list(enumerate(sides(count)))
    values = []
    for k, side in both:
        joint, halo_joint, own, halo = pieces[k]
        halo_next = halo[:, width : 2 * width].astype(F32) + dot(
            halo_joint[:, 2 * width :], own[:, :width]
        )
        edge_next = local[k] + dot(joint[:, 2 * width :], halo[:, :width])
        values.append((rounded(halo_next), rounded(edge_next)))
    rhs = []
    for j in (1, 0):
        for k, side in both:
            b = side.inner if j else side.edge
            value = known[2 * k + j] + dot(coupling[side.outward, b], values[k][j])
            rhs.append((b, rounded(value)))
    inner_a, inner_b, edge_a, edge_b = [rounded(dot(inv[b], value)) for b, value in rhs]
    return (edge_a, edge_b), (inner_a, inner_b)


def meet_kernel(
    count, inv, coupling, base, known, cross, chip, local, from_cross, from_chip,
    cross_out, chip_out, local_out, inner_out,
):
    width = known.shape[-1]
    pieces = ((cross, from_cross, cross, from_cross), (chip, from_chip, chip, from_chip))
    edge, inner = absorbed(count, inv, coupling, known, pieces, local)
    both = list(enumerate(sides(count)))
    outs = (cross_out, chip_out)
    rhs = []
    for k, side in both:
        value = base[side.edge].astype(F32) + dot(coupling[side.inward, side.edge], inner[k])
        rhs.append(rounded(value))
        outs[k][:, :width] = edge[k]
        inner_out[k] = inner[k]
    for k, side in both:
        value = dot(inv[side.edge], rhs[k])
        outs[k][:, width:] = rounded(value)
        local_out[k] = value


def meet(*operands):
    count, size, width = operands[2].shape
    out = jax.ShapeDtypeStruct((size, 2 * width), BF16)
    return pl.pallas_call(
        functools.partial(meet_kernel, count),
        out_shape=(
            out,
            out,
            jax.ShapeDtypeStruct((2, size, width), F32),
            jax.ShapeDtypeStruct((2, size, width), BF16),
        ),
        in_specs=[VM] * len(operands),
        out_specs=(VM, VM, VM, VM),
        compiler_params=params(),
        cost_estimate=cost(32 * size * size * width, 24 * size * size),
        name="meet",
    )(*operands)


def finish_kernel(
    count, weight, inv, coupling, known, middle, cross_joint, chip_joint, from_cross_joint,
    from_chip_joint, cross, chip, local, from_cross, from_chip, out,
):
    size, width = known.shape[1:]
    pieces = (
        (cross_joint, from_cross_joint, cross, from_cross),
        (chip_joint, from_chip_joint, chip, from_chip),
    )
    edge, inner = absorbed(count, inv, coupling, known, pieces, local)
    for k, side in enumerate(sides(count)):
        out[side.edge, :size] = edge[k]
        out[side.inner, :size] = inner[k]
    for b in range(2, count - 2):
        out[b, :size] = middle[b - 2]
    full = jnp.full((EXTRA, width), weight[0], F32)
    high_part = rounded(full)
    rest = full - high_part.astype(F32)
    mid_part = rounded(rest)
    low_part = rounded(rest - mid_part.astype(F32))
    place = lax.broadcasted_iota(jnp.int32, (EXTRA, width), 0)
    rows = jnp.where(
        place == 0,
        high_part.astype(F32),
        jnp.where(place == 1, mid_part.astype(F32), low_part.astype(F32)),
    )
    for b in range(count):
        out[b, size:] = rounded(rows)


def finish(weight, *operands):
    count, size, _ = operands[0].shape
    width = operands[2].shape[-1]
    return pl.pallas_call(
        functools.partial(finish_kernel, count),
        out_shape=jax.ShapeDtypeStruct((count, size + EXTRA, width), BF16),
        in_specs=[SM] + [VM] * len(operands),
        out_specs=VM,
        compiler_params=params(),
        cost_estimate=cost(24 * size * size * width, 24 * size * size),
        name="finish",
    )(weight, *operands)


def gram_kernel(size, parts, received, filtered, gram):
    total = None
    for p in range(received.shape[0]):
        rows = received[p, size : size + 3].astype(F32)
        weight = rows[0:1] + rows[1:2] + rows[2:3]
        term = weight * received[p, :size].astype(F32)
        total = term if total is None else total + term
    filtered[...] = total
    value = lax.dot_general(
        total, total, (((0,), (0,)), ((), ())), precision=HI, preferred_element_type=F32
    )
    gram[...] = value.reshape(gram.shape)


def partial_gram(received, parts):
    poles, rows, width = received.shape
    size = rows - EXTRA
    return pl.pallas_call(
        functools.partial(gram_kernel, size, parts),
        out_shape=(
            jax.ShapeDtypeStruct((size, width), F32),
            jax.ShapeDtypeStruct((parts, width // parts, width), F32),
        ),
        in_specs=[VM],
        out_specs=(VM, VM),
        compiler_params=params(),
        name="gram",
    )(received)


def eliminate(value, work, inverse):
    n = value.shape[-1]
    subs = lax.broadcasted_iota(jnp.int32, (8, 2 * n), 0)
    work[:, :n] = value
    work[:, n:] = (
        lax.broadcasted_iota(jnp.int32, (n, n), 0) == lax.broadcasted_iota(jnp.int32, (n, n), 1)
    ).astype(F32)
    for p in range(n // 8):
        rows = work[8 * p : 8 * p + 8, :]
        for j in range(8):
            column = rows[:, 8 * p + j : 8 * p + j + 1]
            scale = lax.rsqrt(column[j : j + 1])
            pivot = rows[j : j + 1] * scale
            rows = jnp.where(
                subs == j, pivot, jnp.where(subs > j, rows - (column * scale) * pivot, rows)
            )
        work[8 * p : 8 * p + 8, :] = rows
        if 8 * p + 8 < n:
            change = lax.dot_general(
                rows[:, :n], rows, (((0,), (0,)), ((), ())), precision=HI, preferred_element_type=F32
            )
            work[8 * p + 8 :, :] = work[8 * p + 8 :, :] - change[8 * p + 8 :, :]
    inverse[...] = work[:, n:]


def orthonormal_kernel(total_rows, gram, filtered, out, work, inverse):
    n = out.shape[-1]
    value = gram[...].reshape(n, n) / total_rows
    rows = lax.broadcasted_iota(jnp.int32, (n, n), 0)
    cols = lax.broadcasted_iota(jnp.int32, (n, n), 1)
    same = rows == cols

    def phi(x):
        return jnp.where(rows > cols, x, jnp.where(same, 0.5 * x, 0.0))

    def exact(a, b):
        return jnp.dot(a, b, precision=HI, preferred_element_type=F32)

    def short(a, b):
        return dot(rounded(a), rounded(b))

    diagonal = jnp.where(same, value, 0.0)
    across = lax.rsqrt(jnp.sum(diagonal, axis=0, keepdims=True))
    down = lax.rsqrt(jnp.sum(diagonal, axis=1, keepdims=True))
    excess = jnp.where(same, 0.0, value * across * down)
    first = jnp.where(rows > cols, excess, 0.0)
    first_t = excess - first
    product = exact(first, excess)
    second_excess = -product - exact(first_t - product, first_t)
    second = phi(second_excess)
    second_t = second_excess - second
    product = short(second, second_excess)
    third_excess = -product - short(second_t - product, second_t)
    third = phi(third_excess)
    factor = exact(second, first) - first - second
    factor = jnp.where(same, 1.0 + factor, factor)
    factor = factor - short(third, factor)
    inverse[...] = factor * across
    error = jnp.sum(third_excess * third_excess)

    @pl.when(jnp.logical_not(error < 1e-7))
    def _():
        eliminate(value, work, inverse)

    out[...] = lax.dot_general(
        filtered[...], inverse[...], (((1,), (1,)), ((), ())), precision=HI, preferred_element_type=F32
    )


def orthonormal(gram, filtered, total_rows):
    n = filtered.shape[-1]
    return pl.pallas_call(
        functools.partial(orthonormal_kernel, float(total_rows)),
        out_shape=jax.ShapeDtypeStruct(filtered.shape, F32),
        in_specs=[VM, VM],
        out_specs=VM,
        scratch_shapes=[pltpu.VMEM((n, 2 * n), F32), pltpu.VMEM((n, n), F32)],
        compiler_params=params(),
        name="orthonormal",
    )(gram, filtered)


POLE = ("x_hi", "y")
ROW = ("x_lo", "z", "core")
PLANE = ("x_hi", "y", "x_lo")
LINE = ("z", "core")


def swapped(cross, chip):
    peers = lax.axis_size(ROW)
    links = [(i, i + 1) for i in range(1, peers - 1, 2)]
    pairs = [(i, i + 1) for i in range(0, peers, 2)]
    return tuple(
        lax.ppermute(value, ROW, joined + [(j, i) for i, j in joined])
        for value, joined in ((cross, links), (chip, pairs))
    )


def exchange(value, axes):
    return lax.all_to_all(value, axes, split_axis=0, concat_axis=0, tiled=True)


def shards(basis, inverses, lower, upper, pole_weights):
    rows, width = basis.shape
    count, size = inverses.shape[1:3]
    cross, chip, local, inv, coupling, base = first_edges(
        inverses, lower, upper, basis.reshape(count, size, width)
    )
    joints = (cross, chip)
    received = halo_joints = swapped(cross, chip)
    middle, known = pair_call(first_pair_kernel, "first_pair", inv, coupling, base, cross, chip)
    for _ in range(SWEEPS // 2 - 1):
        cross, chip, local, inner = meet(
            inv, coupling, base, known, cross, chip, local, *received
        )
        received = swapped(cross, chip)
        middle, known = pair_call(
            pair_kernel, "pair", inv, coupling, base, cross, chip, inner, middle
        )
    solved = finish(
        pole_weights, inv, coupling, known, middle, *joints, *halo_joints, cross, chip, local, *received
    )
    received = exchange(solved, POLE)
    plane = lax.axis_size(PLANE)
    filtered, gram = partial_gram(received, plane)
    gram = exchange(gram, PLANE).sum(0, keepdims=True)
    line = lax.axis_size(LINE)
    gram = exchange(jnp.broadcast_to(gram, (line, *gram.shape[1:])), LINE).sum(0, keepdims=True)
    gram = exchange(jnp.broadcast_to(gram, (plane, *gram.shape[1:])), PLANE)
    return orthonormal(gram, filtered, rows * lax.axis_size(ROW))


def solution(mesh):
    devices = mesh.devices.reshape(2, 4, 2, 8, 2)
    inner = Mesh(devices, ("x_hi", "y", "x_lo", "z", "core"))
    return jax.shard_map(
        shards,
        mesh=inner,
        in_specs=(
            P(ROW, None),
            P(POLE, ROW, None, None),
            P(ROW, None, None),
            P(ROW, None, None),
            P(POLE),
        ),
        out_specs=P(ROW + POLE, None),
        check_vma=False,
    )
```

time: 117 us -> 113 us (0.966)
  Pallas kernels: 41.6 us -> 37.9 us
  starting transfers between devices: 11.4 us -> 8.94 us
  waiting for transfers between devices: 1.49 us -> 3.93 us
    pallas_call x2, Pallas kernels: 14.7 us -> 10.5 us  [pair_call(): pl.pallas_call(functools.partial(kernel, count), out_shape=(jax.ShapeDtyp...]
    ppermute x4, waiting for transfers between devices: 1.49 us -> 3.93 us  [swapped(): lax.ppermute(value, ROW, joined + [(j, i) for i, j in joined])]
    ppermute x4, starting transfers between devices: 11.4 us -> 8.94 us  [swapped(): lax.ppermute(value, ROW, joined + [(j, i) for i, j in joined])]
  transfers between devices with their start and end apart: 4 -> 4, of which waited for: 1 -> 1; matrix products, arithmetic and copies ran while one was open for 0% -> 0% of each run, Pallas kernels for 13% -> 9%
where the time goes in v5:
time: 113 us
  blocking collectives  61 us (54%)
  Pallas kernels  37.9 us (34%)
  starting transfers between devices  8.94 us (8%)
  waiting for transfers between devices  3.93 us (3%)
    all_to_all x4, blocking collectives, exchange(): return lax.all_to_all(value, axes, split_axis=0, concat_axis=0, tiled=True)  61 us
    pallas_call x1, Pallas kernels, orthonormal(): pl.pallas_call(functools.partial(orthonormal_kernel, float(total_rows)),...  17.5 us
    pallas_call x2, Pallas kernels, pair_call(): pl.pallas_call(functools.partial(kernel, count), out_shape=(jax.ShapeDtyp...  10.5 us
    ppermute x4, starting transfers between devices, swapped(): lax.ppermute(value, ROW, joined + [(j, i) for i, j in joined])  8.94 us
    pallas_call x1, Pallas kernels, first_edges(): pl.pallas_call(functools.partial(first_edges_kernel, count), out_shape=(o...  5.18 us
    ppermute x4, waiting for transfers between devices, swapped(): lax.ppermute(value, ROW, joined + [(j, i) for i, j in joined])  3.93 us
    pallas_call x1, Pallas kernels, meet(): pl.pallas_call(functools.partial(meet_kernel, count), out_shape=(out, out...  2.4 us
  transfers between devices with their start and end apart: 4, of which 1 were waited for; matrix products, arithmetic and copies ran while one was open for 0% of the time, Pallas kernels for 9%

profile of v5, /device:TPU:1, one launch (start us, length us, event | category | flops | bytes accessed | tf_op | source)
XLA Modules:
  0.0 112.5 jit_solution(10071261574580813399)
XLA Ops:
  0.0 5.2 %first_edges.1 = (bf16[512,768]{1,0:T(8,128)(2,1)S(1)}, bf16[512,768]{1,0:T(8,128)(2,1)S(1)}, f32[2,512,128]{2,1,0:T(8,128)S(1)}, bf16[8,512,512]{2,1,0:T(8,128)...) custom-call(bf16[1,8,512,512]{3,2,1,0:T(8,128)(2,1)} %inverses.1, ...), custom_call_target="tpu_custom_call" | custom-call | tf_op jit(solution)/shard_map/first_edges/pallas_call | solution.py:112
  5.2 4.9 %collective-permute-start = (bf16[512,768]{1,0:T(8,128)(2,1)S(1)}, bf16[512,768]{1,0:T(8,128)(2,1)S(1)}, u32[]{:S(2)}, u32[]{:S(2)}) collective-permute-start(bf16[512,768]{1,0:T(8,128)(2,1)S(1)} %get-tuple-element.24.cross.cross_joint), channel_id=1, source_target_pairs={{1,2},{3,4},{5,6},{7,8},{9,10},{11,12},{13,14},{15,16},{17,18},{19... | collective-permute-start | bytes 2359304 | tf_op jit(solution)/shard_map/ppermute | solution.py:413
  10.1 0.1 collective-permute-start.1
  10.2 5.6 %first_pair.1 = (bf16[4,512,128]{2,1,0:T(8,128)(2,1)S(1)}, f32[4,512,128]{2,1,0:T(8,128)S(1)}) custom-call(bf16[8,512,512]{2,1,0:T(8,128)(2,1)S(1)} %get-tuple-element.21.inv, bf16[2,8,512,512]{3,2,1,0:T(8,128)(2,1)S(1)} %get-tuple-element.22.coupling, bf16[8,512,128]{2,1,0:T(8,128)(2,1)S(1)} %get-tuple-element.23.base, ...), custom_call_target="tpu_custom_call" | custom-call | flops 2415919104 | bytes 12582912 | tf_op jit(solution)/shard_map/first_pair/pallas_call | solution.py:170
  15.9 3.9 %collective-permute-done.from_cross.from_cross_joint = bf16[512,768]{1,0:T(8,128)(2,1)S(1)} collective-permute-done((bf16[512,768]{1,0:T(8,128)(2,1)S(1)}, bf16[512,768]{1,0:T(8,128)(2,1)S(1)}, u32[]{:S(2)}, u32[]{:S(2)}) %collective-permute-start) | collective-permute-done | bytes 786464 | tf_op jit(solution)/shard_map/ppermute | solution.py:413
  19.8 0.0 collective-permute-done.1.from_chip.from_chip_joint
  19.8 2.4 %meet.1 = (bf16[512,256]{1,0:T(8,128)(2,1)S(1)}, bf16[512,256]{1,0:T(8,128)(2,1)S(1)}, f32[2,512,128]{2,1,0:T(8,128)S(1)}, bf16[2,512,128]{2,1,0:T(8,128)(2,1)S(1)}) custom-call(bf16[8,512,512]{2,1,0:T(8,128)(2,1)S(1)} %get-tuple-element.21.inv, bf16[2,8,512,512]{3,2,1,0:T(8,128)(2,1)S(1)} %get-tuple-element.22.coupling, ...), custom_call_target="tpu_custom_call" | custom-call | flops 1073741824 | bytes 6291456 | tf_op jit(solution)/shard_map/meet/pallas_call | solution.py:230
  22.2 3.6 %collective-permute-start.2 = (bf16[512,256]{1,0:T(8,128)(2,1)S(1)}, bf16[512,256]{1,0:T(8,128)(2,1)S(1)}, u32[]{:S(2)}, u32[]{:S(2)}) collective-permute-start(bf16[512,256]{1,0:T(8,128)(2,1)S(1)} %get-tuple-element.28.cross), channel_id=1, source_target_pairs={{1,2},{3,4},{5,6},{7,8},{9,10},{11,12},{13,14},{15,16},{17,18},{19... | collective-permute-start | bytes 786440 | tf_op jit(solution)/shard_map/ppermute | solution.py:413
  25.8 0.3 collective-permute-start.3
  26.8 4.8 %pair.1 = (bf16[4,512,128]{2,1,0:T(8,128)(2,1)S(1)}, f32[4,512,128]{2,1,0:T(8,128)S(1)}) custom-call(bf16[8,512,512]{2,1,0:T(8,128)(2,1)S(1)} %get-tuple-element.21.inv, bf16[2,8,512,512]{3,2,1,0:T(8,128)(2,1)S(1)} %get-tuple-element.22.coupling, bf16[8,512,128]{2,1,0:T(8,128)(2,1)S(1)} %get-tuple-element.23.base, ...), custom_call_target="tpu_custom_call" | custom-call | flops 2415919104 | bytes 12582912 | tf_op jit(solution)/shard_map/pair/pallas_call | solution.py:170
  31.6 0.0 collective-permute-done.2.from_cross
  31.6 0.0 collective-permute-done.3.from_chip
  31.6 1.8 %finish.1 = bf16[8,528,128]{2,1,0:T(8,128)(2,1)S(1)} custom-call(f32[1]{0:T(128)S(6)} %copy.6.weight, bf16[8,512,512]{2,1,0:T(8,128)(2,1)S(1)} %get-tuple-element.21.inv, bf16[2,8,512,512]{3,2,1,0:T(8,128)(2,1)S(1)} %get-tuple-element.22.coupling, f32[4,512,128]{2,1,0:T(8,128)S(1)} %get-tuple-element.32.known, ...), custom_call_target="tpu_custom_call" | custom-call | flops 805306368 | bytes 6291456 | tf_op jit(solution)/shard_map/finish/pallas_call | solution.py:279
  33.5 23.1 %all_to_all.20.received = bf16[8,528,128]{2,1,0:T(8,128)(2,1)S(1)} all-to-all(bf16[8,528,128]{2,1,0:T(8,128)(2,1)S(1)} %finish.1), channel_id=1, replica_groups=mesh['x_hi'=2,'y'=4,'x_lo'=2,'z'=8,'core'=2] {'x_hi','y'}, dimensions={0} | all-to-all | bytes 2162688 | tf_op jit(solution)/shard_map/all_to_all | solution.py:419
  56.6 0.5 gram.1
  57.1 16.1 %all_to_all.21 = f32[16,8,128]{2,1,0:T(8,128)S(1)} all-to-all(f32[16,8,128]{2,1,0:T(8,128)S(1)} %get-tuple-element.35), channel_id=1, replica_groups=mesh['x_hi'=2,'y'=4,'x_lo'=2,'z'=8,'core'=2] {'x_hi','y','x_lo'}, dimensions={0} | all-to-all | bytes 131072 | tf_op jit(solution)/shard_map/all_to_all | solution.py:419
  73.2 12.4 %all_to_all.22 = f32[16,8,128]{2,1,0:T(8,128)S(1)} all-to-all(f32[16,8,128]{2,1,0:T(8,128)S(1)} %broadcast_in_dim.4), channel_id=1, replica_groups=mesh['x_hi'=2,'y'=4,'x_lo'=2,'z'=8,'core'=2] {'z','core'}, dimensions={0} | all-to-all | bytes 131072 | tf_op jit(solution)/shard_map/all_to_all | solution.py:419
  85.7 9.4 %all_to_all.23.gram = f32[16,8,128]{2,1,0:T(8,128)S(1)} all-to-all(f32[16,8,128]{2,1,0:T(8,128)S(1)} %broadcast_in_dim.5), channel_id=1, replica_groups=mesh['x_hi'=2,'y'=4,'x_lo'=2,'z'=8,'core'=2] {'x_hi','y','x_lo'}, dimensions={0} | all-to-all | bytes 131072 | tf_op jit(solution)/shard_map/all_to_all | solution.py:419
  95.0 17.5 %orthonormal.1 = f32[512,128]{1,0:T(8,128)} custom-call(f32[16,8,128]{2,1,0:T(8,128)S(1)} %all_to_all.23.gram, f32[512,128]{1,0:T(8,128)S(1)} %get-tuple-element.36.filtered), custom_call_target="tpu_custom_call" | custom-call | tf_op jit(solution)/shard_map/orthonormal/pallas_call | solution.py:391
  (4 shorter events, 0.1 us)
Async XLA Ops:
  5.2 14.6 %collective-permute-start = (bf16[512,768]{1,0:T(8,128)(2,1)S(1)}, bf16[512,768]{1,0:T(8,128)(2,1)S(1)}, u32[]{:S(2)}, u32[]{:S(2)}) collective-permute-start(bf16[512,768]{1,0:T(8,128)(2,1)S(1)} %get-tuple-element.24.cross.cross_joint), channel_id=1, source_target_pairs={{1,2},{3,4},{5,6},{7,8},{9,10},{11,12},{13,14},{15,16},{17,18},{19... | collective-permute-start | bytes 2359304 | tf_op jit(solution)/shard_map/ppermute | solution.py:413
  10.1 9.7 %collective-permute-start.1 = (bf16[512,768]{1,0:T(8,128)(2,1)S(1)}, bf16[512,768]{1,0:T(8,128)(2,1)S(1)}, u32[]{:S(2)}, u32[]{:S(2)}) collective-permute-start(bf16[512,768]{1,0:T(8,128)(2,1)S(1)} %get-tuple-element.25.chip.chip_joint), channel_id=1, source_target_pairs={{0,1},{2,3},{4,5},{6,7},{8,9},{10,11},{12,13},{14,15},{16,17},{18,... | collective-permute-start | bytes 2359304 | tf_op jit(solution)/shard_map/ppermute | solution.py:413
  22.2 9.4 %collective-permute-start.2 = (bf16[512,256]{1,0:T(8,128)(2,1)S(1)}, bf16[512,256]{1,0:T(8,128)(2,1)S(1)}, u32[]{:S(2)}, u32[]{:S(2)}) collective-permute-start(bf16[512,256]{1,0:T(8,128)(2,1)S(1)} %get-tuple-element.28.cross), channel_id=1, source_target_pairs={{1,2},{3,4},{5,6},{7,8},{9,10},{11,12},{13,14},{15,16},{17,18},{19... | collective-permute-start | bytes 786440 | tf_op jit(solution)/shard_map/ppermute | solution.py:413
  25.8 5.8 %collective-permute-start.3 = (bf16[512,256]{1,0:T(8,128)(2,1)S(1)}, bf16[512,256]{1,0:T(8,128)(2,1)S(1)}, u32[]{:S(2)}, u32[]{:S(2)}) collective-permute-start(bf16[512,256]{1,0:T(8,128)(2,1)S(1)} %get-tuple-element.29.chip), channel_id=1, source_target_pairs={{0,1},{2,3},{4,5},{6,7},{8,9},{10,11},{12,13},{14,15},{16,17},{18,... | collective-permute-start | bytes 786440 | tf_op jit(solution)/shard_map/ppermute | solution.py:413

commit v6 on v2

v6 whole, which is shorter than its diff:
```python
import functools

import jax
import jax.numpy as jnp
from jax import lax
from jax.experimental import pallas as pl
from jax.experimental.pallas import tpu as pltpu
from jax.sharding import Mesh, PartitionSpec as P

SWEEPS = 4
EXTRA = 16
F32 = jnp.float32
BF16 = jnp.bfloat16
HI = lax.Precision.HIGHEST
VM = pl.BlockSpec(memory_space=pltpu.VMEM)
SM = pl.BlockSpec(memory_space=pltpu.SMEM)
HBM = pl.BlockSpec(memory_space=pltpu.HBM)
LIMIT = 16 << 20


def dot(a, b):
    return jnp.dot(a, b, preferred_element_type=F32)


def in_hbm(value):
    return pltpu.with_memory_space_constraint(value, pltpu.HBM)


def params():
    return pltpu.CompilerParams(vmem_limit_bytes=LIMIT)


def cost(flops, moved):
    return pl.CostEstimate(flops=int(flops), bytes_accessed=int(moved), transcendentals=0)


class Side:
    def __init__(self, which, count):
        self.low = lax.axis_index("core") == which
        self.edge = jnp.where(self.low, 0, count - 1)
        self.inner = jnp.where(self.low, 1, count - 2)
        self.outward = jnp.where(self.low, 0, 1)
        self.inward = 1 - self.outward


def sides(count):
    return Side(0, count), Side(1, count)


def rounded(value):
    return value.astype(BF16)


def weight_rows(weight, shape):
    full = jnp.full(shape, weight, F32)
    high = rounded(full)
    rest = full - high.astype(F32)
    mid = rounded(rest)
    low = rounded(rest - mid.astype(F32))
    place = lax.broadcasted_iota(jnp.int32, shape, 0)
    rows = jnp.where(
        place == 0, high.astype(F32), jnp.where(place == 1, mid.astype(F32), low.astype(F32))
    )
    return rounded(rows)


def first_edges_kernel(
    count, inverses, basis, cross, chip, inv, base, sem
):
    ends = (0, count - 1)
    pairs = [(basis.at[b], base.at[k]) for k, b in enumerate(ends)]
    pairs += [(inverses.at[b], inv.at[k]) for k, b in enumerate(ends)]
    copies = [pltpu.make_async_copy(a, b, sem.at[i]) for i, (a, b) in enumerate(pairs)]
    for copy in copies:
        copy.start()
    for copy in copies:
        copy.wait()
    for side, out in zip(sides(2), (cross, chip)):
        out[...] = rounded(dot(inv[side.edge], base[side.edge]))


def first_edges(inverses, basis):
    count, size, width = basis.shape
    out = jax.ShapeDtypeStruct((size, width), BF16)
    return pl.pallas_call(
        functools.partial(first_edges_kernel, count),
        out_shape=(out, out),
        in_specs=[HBM] * 2,
        out_specs=(VM, VM),
        scratch_shapes=[
            pltpu.VMEM((2, size, size), BF16),
            pltpu.VMEM((2, size, width), BF16),
            pltpu.SemaphoreType.DMA((4,)),
        ],
        compiler_params=params(),
        name="first_edges",
    )(in_hbm(inverses), in_hbm(basis))


def advance(count, inv, coupling, base, state, rhs, middle, known, ready=lambda b: None):
    for b in range(1, count - 1):
        ready(b)
        value = dot(coupling[0, b], state[b - 1]) + dot(coupling[1, b], state[b + 1])
        rhs[b] = rounded(base[b].astype(F32) + value)
    ready(0)
    ready(count - 1)
    for k, side in enumerate(sides(count)):
        value = dot(coupling[side.inward, side.edge], state[side.inner])
        known[k] = base[side.edge].astype(F32) + value
    for b in range(1, count - 1):
        middle[b - 1] = rounded(dot(inv[b], rhs[b]))


def first_sweep_kernel(
    count, inv, lower, upper, base, cross, chip, coupling, middle, known, state, rhs, sem
):
    copies = []
    for b in range(count):
        copies.append(
            [
                pltpu.make_async_copy(source.at[b], coupling.at[k, b], sem.at[2 * b + k])
                for k, source in enumerate((lower, upper))
            ]
        )
    for b in [*range(1, count - 1), 0, count - 1]:
        for copy in copies[b]:
            copy.start()
    for side, edge in zip(sides(count), (cross, chip)):
        state[side.edge] = edge[...]
    for b in range(1, count - 1):
        state[b] = rounded(dot(inv[b], base[b]))

    def ready(b):
        for copy in copies[b]:
            copy.wait()

    advance(count, inv, coupling, base, state, rhs, middle, known, ready)


def sweep_kernel(count, inv, coupling, base, cross, chip, previous, middle, known, state, rhs):
    for side, edge in zip(sides(count), (cross, chip)):
        state[side.edge] = edge[...]
    for b in range(1, count - 1):
        state[b] = previous[b - 1]
    advance(count, inv, coupling, base, state, rhs, middle, known)


def sweep_shapes(count, size, width):
    return (
        jax.ShapeDtypeStruct((count - 2, size, width), BF16),
        jax.ShapeDtypeStruct((2, size, width), F32),
    )


def sweep_cost(count, size, width):
    return cost(6 * count * size * size * width, 6 * count * size * size)


def first_sweep(inv, lower, upper, base, cross, chip):
    count, size, width = base.shape
    return pl.pallas_call(
        functools.partial(first_sweep_kernel, count),
        out_shape=(
            jax.ShapeDtypeStruct((2, count, size, size), BF16),
            *sweep_shapes(count, size, width),
        ),
        in_specs=[VM, HBM, HBM, VM, VM, VM],
        out_specs=(VM,) * 3,
        scratch_shapes=[
            pltpu.VMEM((count, size, width), BF16),
            pltpu.VMEM((count, size, width), BF16),
            pltpu.SemaphoreType.DMA((2 * count,)),
        ],
        compiler_params=params(),
        cost_estimate=sweep_cost(count, size, width),
        name="first_sweep",
    )(inv, in_hbm(lower), in_hbm(upper), base, cross, chip)


def sweep(inv, coupling, base, cross, chip, middle):
    count, size, width = base.shape
    return pl.pallas_call(
        functools.partial(sweep_kernel, count),
        out_shape=sweep_shapes(count, size, width),
        in_specs=[VM] * 6,
        out_specs=(VM,) * 2,
        scratch_shapes=[pltpu.VMEM((count, size, width), BF16)] * 2,
        compiler_params=params(),
        cost_estimate=sweep_cost(count, size, width),
        name="sweep",
    )(inv, coupling, base, cross, chip, middle)


def edge_blocks(count, inv, coupling, known, halos):
    both = list(enumerate(sides(count)))
    rhs = []
    for k, side in both:
        value = known[k] + dot(coupling[side.outward, side.edge], halos[k][...])
        rhs.append(rounded(value))
    return [rounded(dot(inv[side.edge], rhs[k])) for k, side in both]


def edges_kernel(count, inv, coupling, known, from_cross, from_chip, cross, chip):
    cross[...], chip[...] = edge_blocks(count, inv, coupling, known, (from_cross, from_chip))


def edges(inv, coupling, known, from_cross, from_chip):
    count, size, _ = inv.shape
    width = known.shape[-1]
    out = jax.ShapeDtypeStruct((size, width), BF16)
    return pl.pallas_call(
        functools.partial(edges_kernel, count),
        out_shape=(out, out),
        in_specs=[VM] * 5,
        out_specs=(VM, VM),
        compiler_params=params(),
        cost_estimate=cost(8 * size * size * width, 8 * size * size),
        name="edges",
    )(inv, coupling, known, from_cross, from_chip)


def finish_kernel(count, weight, inv, coupling, known, from_cross, from_chip, middle, out):
    size, width = known.shape[1:]
    rows = weight_rows(weight[0], (EXTRA, width))
    for b in range(1, count - 1):
        out[b, :size] = middle[b - 1]
    for b in range(count):
        out[b, size:] = rows
    values = edge_blocks(count, inv, coupling, known, (from_cross, from_chip))
    for side, value in zip(sides(count), values):
        out[side.edge, :size] = value


def finish(weight, inv, coupling, known, from_cross, from_chip, middle):
    count, size, _ = inv.shape
    width = known.shape[-1]
    return pl.pallas_call(
        functools.partial(finish_kernel, count),
        out_shape=jax.ShapeDtypeStruct((count, size + EXTRA, width), BF16),
        in_specs=[SM] + [VM] * 6,
        out_specs=VM,
        compiler_params=params(),
        cost_estimate=cost(8 * size * size * width, 8 * size * size),
        name="finish",
    )(weight, inv, coupling, known, from_cross, from_chip, middle)


def gram_kernel(size, parts, received, filtered, gram):
    total = None
    for p in range(received.shape[0]):
        rows = received[p, size : size + 3].astype(F32)
        weight = rows[0:1] + rows[1:2] + rows[2:3]
        term = weight * received[p, :size].astype(F32)
        total = term if total is None else total + term
    filtered[...] = total
    value = lax.dot_general(
        total, total, (((0,), (0,)), ((), ())), precision=HI, preferred_element_type=F32
    )
    gram[...] = value.reshape(gram.shape)


def partial_gram(received, parts):
    poles, rows, width = received.shape
    size = rows - EXTRA
    return pl.pallas_call(
        functools.partial(gram_kernel, size, parts),
        out_shape=(
            jax.ShapeDtypeStruct((size, width), F32),
            jax.ShapeDtypeStruct((parts, width // parts, width), F32),
        ),
        in_specs=[VM],
        out_specs=(VM, VM),
        compiler_params=params(),
        name="gram",
    )(received)


def eliminate(value, work, inverse):
    n = value.shape[-1]
    subs = lax.broadcasted_iota(jnp.int32, (8, 2 * n), 0)
    work[:, :n] = value
    work[:, n:] = (
        lax.broadcasted_iota(jnp.int32, (n, n), 0) == lax.broadcasted_iota(jnp.int32, (n, n), 1)
    ).astype(F32)
    for p in range(n // 8):
        rows = work[8 * p : 8 * p + 8, :]
        for j in range(8):
            column = rows[:, 8 * p + j : 8 * p + j + 1]
            scale = lax.rsqrt(column[j : j + 1])
            pivot = rows[j : j + 1] * scale
            rows = jnp.where(
                subs == j, pivot, jnp.where(subs > j, rows - (column * scale) * pivot, rows)
            )
        work[8 * p : 8 * p + 8, :] = rows
        if 8 * p + 8 < n:
            change = lax.dot_general(
                rows[:, :n], rows, (((0,), (0,)), ((), ())), precision=HI, preferred_element_type=F32
            )
            work[8 * p + 8 :, :] = work[8 * p + 8 :, :] - change[8 * p + 8 :, :]
    inverse[...] = work[:, n:]


def orthonormal_kernel(total_rows, gram, filtered, out, work, inverse):
    n = out.shape[-1]
    value = gram[...].reshape(n, n) / total_rows
    rows = lax.broadcasted_iota(jnp.int32, (n, n), 0)
    cols = lax.broadcasted_iota(jnp.int32, (n, n), 1)
    same = rows == cols

    def phi(x):
        return jnp.where(rows > cols, x, jnp.where(same, 0.5 * x, 0.0))

    def exact(a, b):
        return jnp.dot(a, b, precision=HI, preferred_element_type=F32)

    def short(a, b):
        return dot(rounded(a), rounded(b))

    diagonal = jnp.where(same, value, 0.0)
    across = lax.rsqrt(jnp.sum(diagonal, axis=0, keepdims=True))
    down = lax.rsqrt(jnp.sum(diagonal, axis=1, keepdims=True))
    excess = jnp.where(same, 0.0, value * across * down)
    first = jnp.where(rows > cols, excess, 0.0)
    first_t = excess - first
    product = exact(first, excess)
    second_excess = -product - exact(first_t - product, first_t)
    second = phi(second_excess)
    second_t = second_excess - second
    product = short(second, second_excess)
    third_excess = -product - short(second_t - product, second_t)
    third = phi(third_excess)
    factor = exact(second, first) - first - second
    factor = jnp.where(same, 1.0 + factor, factor)
    factor = factor - short(third, factor)
    inverse[...] = factor * across
    error = jnp.sum(third_excess * third_excess)

    @pl.when(jnp.logical_not(error < 1e-7))
    def _():
        eliminate(value, work, inverse)

    out[...] = lax.dot_general(
        filtered[...], inverse[...], (((1,), (1,)), ((), ())), precision=HI, preferred_element_type=F32
    )


def orthonormal(gram, filtered, total_rows):
    n = filtered.shape[-1]
    return pl.pallas_call(
        functools.partial(orthonormal_kernel, float(total_rows)),
        out_shape=jax.ShapeDtypeStruct(filtered.shape, F32),
        in_specs=[VM, VM],
        out_specs=VM,
        scratch_shapes=[pltpu.VMEM((n, 2 * n), F32), pltpu.VMEM((n, n), F32)],
        compiler_params=params(),
        name="orthonormal",
    )(gram, filtered)


POLE = ("x_hi", "y")
ROW = ("x_lo", "z", "core")
PLANE = ("x_hi", "y", "x_lo")
LINE = ("z", "core")


def swapped(cross, chip):
    peers = lax.axis_size(ROW)
    links = [(i, i + 1) for i in range(1, peers - 1, 2)]
    pairs = [(i, i + 1) for i in range(0, peers, 2)]
    return tuple(
        lax.ppermute(value, ROW, joined + [(j, i) for i, j in joined])
        for value, joined in ((cross, links), (chip, pairs))
    )


def exchange(value, axes):
    return lax.all_to_all(value, axes, split_axis=0, concat_axis=0, tiled=True)


def shards(basis, inverses, lower, upper, pole_weights):
    rows, width = basis.shape
    count, size = inverses.shape[1:3]
    inv = inverses.reshape(count, size, size)
    base = basis.reshape(count, size, width)
    cross, chip = first_edges(inv, base)
    halos = swapped(cross, chip)
    coupling, middle, known = first_sweep(inv, lower, upper, base, cross, chip)
    for _ in range(SWEEPS - 1):
        cross, chip = edges(inv, coupling, known, *halos)
        halos = swapped(cross, chip)
        middle, known = sweep(inv, coupling, base, cross, chip, middle)
    solved = finish(pole_weights, inv, coupling, known, *halos, middle)
    received = exchange(solved, POLE)
    plane = lax.axis_size(PLANE)
    filtered, gram = partial_gram(received, plane)
    gram = exchange(gram, PLANE).sum(0, keepdims=True)
    line = lax.axis_size(LINE)
    gram = exchange(jnp.broadcast_to(gram, (line, *gram.shape[1:])), LINE).sum(0, keepdims=True)
    gram = exchange(jnp.broadcast_to(gram, (plane, *gram.shape[1:])), PLANE)
    return orthonormal(gram, filtered, rows * lax.axis_size(ROW))


def solution(mesh):
    devices = mesh.devices.reshape(2, 4, 2, 8, 2)
    inner = Mesh(devices, ("x_hi", "y", "x_lo", "z", "core"))
    return jax.shard_map(
        shards,
        mesh=inner,
        in_specs=(
            P(ROW, None),
            P(POLE, ROW, None, None),
            P(ROW, None, None),
            P(ROW, None, None),
            P(POLE),
        ),
        out_specs=P(ROW + POLE, None),
        check_vma=False,
    )
```

time: 127 us -> 119 us (0.937)
  waiting for transfers between devices: 5.61 us -> 0.02 us
  starting transfers between devices: 21.3 us -> 18.6 us
    ppermute x8, waiting for transfers between devices: 5.61 us -> 0.02 us  [swapped(): lax.ppermute(value, ROW, joined + [(j, i) for i, j in joined])]
    ppermute x8, starting transfers between devices: 21.3 us -> 18.6 us  [swapped(): lax.ppermute(value, ROW, joined + [(j, i) for i, j in joined])]
    pallas_call x5, Pallas kernels: 17 us -> 14.9 us  [the longest x3 8.85 us: sweep(): pl.pallas_call(functools.partial(sweep_kernel, count), out_shape=sweep_sh...]
  transfers between devices with their start and end apart: 8 -> 8, of which waited for: 3 -> 0; matrix products, arithmetic and copies ran while one was open for 0% -> 0% of each run, Pallas kernels for 13% -> 12%
where the time goes in v6:
time: 119 us; the launch traced here: 118 us
  blocking collectives  61.2 us (51%)
  Pallas kernels  37.4 us (31%)
  starting transfers between devices  18.6 us (16%)
    all_to_all x4, blocking collectives, exchange(): return lax.all_to_all(value, axes, split_axis=0, concat_axis=0, tiled=True)  61.2 us
    ppermute x8, starting transfers between devices, swapped(): lax.ppermute(value, ROW, joined + [(j, i) for i, j in joined])  18.6 us
    pallas_call x1, Pallas kernels, orthonormal(): pl.pallas_call(functools.partial(orthonormal_kernel, float(total_rows)),...  17.7 us
    pallas_call x3, Pallas kernels, sweep(): pl.pallas_call(functools.partial(sweep_kernel, count), out_shape=sweep_sh...  8.85 us
    pallas_call x1, Pallas kernels, first_sweep(): pl.pallas_call(functools.partial(first_sweep_kernel, count), out_shape=(j...  5.27 us
  transfers between devices with their start and end apart: 8, of which 0 were waited for; matrix products, arithmetic and copies ran while one was open for 0% of the time, Pallas kernels for 12%

profile of v6, /device:TPU:1, one launch (start us, length us, event | category | flops | bytes accessed | tf_op | source)
XLA Modules:
  0.0 118.2 jit_solution(2854947925469058912)
XLA Ops:
  0.0 0.0 copy-start
  0.0 0.0 copy-start.1
  0.0 1.9 %first_edges.1 = (bf16[512,128]{1,0:T(8,128)(2,1)S(1)}, bf16[512,128]{1,0:T(8,128)(2,1)S(1)}) custom-call(bf16[8,512,512]{2,1,0:T(8,128)(2,1)} %bitcast.2, bf16[8,512,128]{2,1,0:T(8,128)(2,1)} %bitcast.11), custom_call_target="tpu_custom_call" | custom-call | tf_op jit(solution)/shard_map/first_edges/pallas_call | solution.py:85
  2.0 5.1 %collective-permute-start = (bf16[512,128]{1,0:T(8,128)(2,1)S(1)}, bf16[512,128]{1,0:T(8,128)(2,1)S(1)}, u32[]{:S(2)}, u32[]{:S(2)}) collective-permute-start(bf16[512,128]{1,0:T(8,128)(2,1)S(1)} %get-tuple-element.24.cross), channel_id=1, source_target_pairs={{1,2},{3,4},{5,6},{7,8},{9,10},{11,12},{13,14},{15,16},{17,18},{19... | collective-permute-start | bytes 393224 | tf_op jit(solution)/shard_map/ppermute | solution.py:371
  7.0 0.1 collective-permute-start.1
  7.8 0.0 copy-done
  7.8 0.0 copy-done.1
  7.8 5.3 %first_sweep.1 = (bf16[2,8,512,512]{3,2,1,0:T(8,128)(2,1)S(1)}, bf16[6,512,128]{2,1,0:T(8,128)(2,1)S(1)}, f32[2,512,128]{2,1,0:T(8,128)S(1)}) custom-call(bf16[8,512,512]{2,1,0:T(8,128)(2,1)S(1)} %bitcast.3, bf16[8,512,512]{2,1,0:T(8,128)(2,1)} %lower.1, bf16[8,512,512]{2,1,0:T(8,128)(2,1)} %upper.1, bf16[8,512,128]{2,1,0:T(8,128)(2,1)S(1)} %bitcast.12, ...), custom_call_target="tpu_custom_call" | custom-call | flops 1610612736 | bytes 12582912 | tf_op jit(solution)/shard_map/first_sweep/pallas_call | solution.py:161
  13.1 0.0 collective-permute-done.from_cross
  13.1 0.0 collective-permute-done.1.from_chip
  13.1 0.8 edges.3
  13.9 3.9 %collective-permute-start.2 = (bf16[512,128]{1,0:T(8,128)(2,1)S(1)}, bf16[512,128]{1,0:T(8,128)(2,1)S(1)}, u32[]{:S(2)}, u32[]{:S(2)}) collective-permute-start(bf16[512,128]{1,0:T(8,128)(2,1)S(1)} %get-tuple-element.28.cross), channel_id=1, source_target_pairs={{1,2},{3,4},{5,6},{7,8},{9,10},{11,12},{13,14},{15,16},{17,18},{19... | collective-permute-start | bytes 393224 | tf_op jit(solution)/shard_map/ppermute | solution.py:371
  17.8 0.1 collective-permute-start.3
  17.9 2.9 %sweep.3 = (bf16[6,512,128]{2,1,0:T(8,128)(2,1)S(1)}, f32[2,512,128]{2,1,0:T(8,128)S(1)}) custom-call(bf16[8,512,512]{2,1,0:T(8,128)(2,1)S(1)} %bitcast.5, bf16[2,8,512,512]{3,2,1,0:T(8,128)(2,1)S(1)} %get-tuple-element.26.coupling, bf16[8,512,128]{2,1,0:T(8,128)(2,1)S(1)} %bitcast.13, bf16[512,128]{1,0:T(8,128)(2,1)S(1)} %get-tuple-element.28.cross, ...), custom_call_target="tpu_custom_call" | custom-call | flops 1610612736 | bytes 12582912 | tf_op jit(solution)/shard_map/sweep/pallas_call | solution.py:182
  20.9 0.0 collective-permute-done.2.from_cross
  20.9 0.0 collective-permute-done.3.from_chip
  20.9 0.8 edges.4
  21.6 3.9 %collective-permute-start.4 = (bf16[512,128]{1,0:T(8,128)(2,1)S(1)}, bf16[512,128]{1,0:T(8,128)(2,1)S(1)}, u32[]{:S(2)}, u32[]{:S(2)}) collective-permute-start(bf16[512,128]{1,0:T(8,128)(2,1)S(1)} %get-tuple-element.32.cross), channel_id=1, source_target_pairs={{1,2},{3,4},{5,6},{7,8},{9,10},{11,12},{13,14},{15,16},{17,18},{19... | collective-permute-start | bytes 393224 | tf_op jit(solution)/shard_map/ppermute | solution.py:371
  25.6 0.3 collective-permute-start.5
  25.9 2.9 %sweep.4 = (bf16[6,512,128]{2,1,0:T(8,128)(2,1)S(1)}, f32[2,512,128]{2,1,0:T(8,128)S(1)}) custom-call(bf16[8,512,512]{2,1,0:T(8,128)(2,1)S(1)} %bitcast.7, bf16[2,8,512,512]{3,2,1,0:T(8,128)(2,1)S(1)} %get-tuple-element.26.coupling, bf16[8,512,128]{2,1,0:T(8,128)(2,1)S(1)} %bitcast.14, bf16[512,128]{1,0:T(8,128)(2,1)S(1)} %get-tuple-element.32.cross, ...), custom_call_target="tpu_custom_call" | custom-call | flops 1610612736 | bytes 12582912 | tf_op jit(solution)/shard_map/sweep/pallas_call | solution.py:182
  28.8 0.0 collective-permute-done.4.from_cross
  28.8 0.0 collective-permute-done.5.from_chip
  28.8 0.8 edges.5
  29.6 5.1 %collective-permute-start.6 = (bf16[512,128]{1,0:T(8,128)(2,1)S(1)}, bf16[512,128]{1,0:T(8,128)(2,1)S(1)}, u32[]{:S(2)}, u32[]{:S(2)}) collective-permute-start(bf16[512,128]{1,0:T(8,128)(2,1)S(1)} %get-tuple-element.36.cross), channel_id=1, source_target_pairs={{1,2},{3,4},{5,6},{7,8},{9,10},{11,12},{13,14},{15,16},{17,18},{19... | collective-permute-start | bytes 393224 | tf_op jit(solution)/shard_map/ppermute | solution.py:371
  34.7 0.1 collective-permute-start.7
  34.8 3.0 %sweep.5 = (bf16[6,512,128]{2,1,0:T(8,128)(2,1)S(1)}, f32[2,512,128]{2,1,0:T(8,128)S(1)}) custom-call(bf16[8,512,512]{2,1,0:T(8,128)(2,1)S(1)} %bitcast.9, bf16[2,8,512,512]{3,2,1,0:T(8,128)(2,1)S(1)} %get-tuple-element.26.coupling, bf16[8,512,128]{2,1,0:T(8,128)(2,1)S(1)} %bitcast.15, bf16[512,128]{1,0:T(8,128)(2,1)S(1)} %get-tuple-element.36.cross, ...), custom_call_target="tpu_custom_call" | custom-call | flops 1610612736 | bytes 12582912 | tf_op jit(solution)/shard_map/sweep/pallas_call | solution.py:182
  37.8 0.0 collective-permute-done.6.from_cross
  37.8 0.0 collective-permute-done.7.from_chip
  37.8 0.8 finish.1
  38.6 23.1 %all_to_all.20.received = bf16[8,528,128]{2,1,0:T(8,128)(2,1)S(1)} all-to-all(bf16[8,528,128]{2,1,0:T(8,128)(2,1)S(1)} %finish.1), channel_id=1, replica_groups=mesh['x_hi'=2,'y'=4,'x_lo'=2,'z'=8,'core'=2] {'x_hi','y'}, dimensions={0} | all-to-all | bytes 2162688 | tf_op jit(solution)/shard_map/all_to_all | solution.py:377
  61.7 0.6 gram.1
  62.3 11.5 %all_to_all.21 = f32[16,8,128]{2,1,0:T(8,128)S(1)} all-to-all(f32[16,8,128]{2,1,0:T(8,128)S(1)} %get-tuple-element.41), channel_id=1, replica_groups=mesh['x_hi'=2,'y'=4,'x_lo'=2,'z'=8,'core'=2] {'x_hi','y','x_lo'}, dimensions={0} | all-to-all | bytes 131072 | tf_op jit(solution)/shard_map/all_to_all | solution.py:377
  73.8 17.2 %all_to_all.22 = f32[16,8,128]{2,1,0:T(8,128)S(1)} all-to-all(f32[16,8,128]{2,1,0:T(8,128)S(1)} %broadcast_in_dim.4), channel_id=1, replica_groups=mesh['x_hi'=2,'y'=4,'x_lo'=2,'z'=8,'core'=2] {'z','core'}, dimensions={0} | all-to-all | bytes 131072 | tf_op jit(solution)/shard_map/all_to_all | solution.py:377
  91.1 9.4 %all_to_all.23.gram = f32[16,8,128]{2,1,0:T(8,128)S(1)} all-to-all(f32[16,8,128]{2,1,0:T(8,128)S(1)} %broadcast_in_dim.5), channel_id=1, replica_groups=mesh['x_hi'=2,'y'=4,'x_lo'=2,'z'=8,'core'=2] {'x_hi','y','x_lo'}, dimensions={0} | all-to-all | bytes 131072 | tf_op jit(solution)/shard_map/all_to_all | solution.py:377
  100.5 17.7 %orthonormal.1 = f32[512,128]{1,0:T(8,128)} custom-call(f32[16,8,128]{2,1,0:T(8,128)S(1)} %all_to_all.23.gram, f32[512,128]{1,0:T(8,128)S(1)} %get-tuple-element.42.filtered), custom_call_target="tpu_custom_call" | custom-call | tf_op jit(solution)/shard_map/orthonormal/pallas_call | solution.py:349
  (4 shorter events, 0.1 us)
Async XLA Ops:
  0.0 7.8 %copy-start = (bf16[1,8,512,512]{3,2,1,0:T(8,128)(2,1)S(1)}, bf16[1,8,512,512]{3,2,1,0:T(8,128)(2,1)}, u32[]{:S(2)}) copy-start(bf16[1,8,512,512]{3,2,1,0:T(8,128)(2,1)} %param.6) | copy-start | bytes 12582916
  0.0 7.8 %copy-start.1 = (bf16[4096,128]{1,0:T(8,128)(2,1)S(1)}, bf16[4096,128]{1,0:T(8,128)(2,1)}, u32[]{:S(2)}) copy-start(bf16[4096,128]{1,0:T(8,128)(2,1)} %param.5) | copy-start | bytes 3145732
  2.0 11.1 %collective-permute-start = (bf16[512,128]{1,0:T(8,128)(2,1)S(1)}, bf16[512,128]{1,0:T(8,128)(2,1)S(1)}, u32[]{:S(2)}, u32[]{:S(2)}) collective-permute-start(bf16[512,128]{1,0:T(8,128)(2,1)S(1)} %get-tuple-element.24.cross), channel_id=1, source_target_pairs={{1,2},{3,4},{5,6},{7,8},{9,10},{11,12},{13,14},{15,16},{17,18},{19... | collective-permute-start | bytes 393224 | tf_op jit(solution)/shard_map/ppermute | solution.py:371
  7.0 6.1 %collective-permute-start.1 = (bf16[512,128]{1,0:T(8,128)(2,1)S(1)}, bf16[512,128]{1,0:T(8,128)(2,1)S(1)}, u32[]{:S(2)}, u32[]{:S(2)}) collective-permute-start(bf16[512,128]{1,0:T(8,128)(2,1)S(1)} %get-tuple-element.25.chip), channel_id=1, source_target_pairs={{0,1},{2,3},{4,5},{6,7},{8,9},{10,11},{12,13},{14,15},{16,17},{18,... | collective-permute-start | bytes 393224 | tf_op jit(solution)/shard_map/ppermute | solution.py:371
  13.9 7.0 %collective-permute-start.2 = (bf16[512,128]{1,0:T(8,128)(2,1)S(1)}, bf16[512,128]{1,0:T(8,128)(2,1)S(1)}, u32[]{:S(2)}, u32[]{:S(2)}) collective-permute-start(bf16[512,128]{1,0:T(8,128)(2,1)S(1)} %get-tuple-element.28.cross), channel_id=1, source_target_pairs={{1,2},{3,4},{5,6},{7,8},{9,10},{11,12},{13,14},{15,16},{17,18},{19... | collective-permute-start | bytes 393224 | tf_op jit(solution)/shard_map/ppermute | solution.py:371
  17.8 3.1 %collective-permute-start.3 = (bf16[512,128]{1,0:T(8,128)(2,1)S(1)}, bf16[512,128]{1,0:T(8,128)(2,1)S(1)}, u32[]{:S(2)}, u32[]{:S(2)}) collective-permute-start(bf16[512,128]{1,0:T(8,128)(2,1)S(1)} %get-tuple-element.29.chip), channel_id=1, source_target_pairs={{0,1},{2,3},{4,5},{6,7},{8,9},{10,11},{12,13},{14,15},{16,17},{18,... | collective-permute-start | bytes 393224 | tf_op jit(solution)/shard_map/ppermute | solution.py:371
  21.6 7.2 %collective-permute-start.4 = (bf16[512,128]{1,0:T(8,128)(2,1)S(1)}, bf16[512,128]{1,0:T(8,128)(2,1)S(1)}, u32[]{:S(2)}, u32[]{:S(2)}) collective-permute-start(bf16[512,128]{1,0:T(8,128)(2,1)S(1)} %get-tuple-element.32.cross), channel_id=1, source_target_pairs={{1,2},{3,4},{5,6},{7,8},{9,10},{11,12},{13,14},{15,16},{17,18},{19... | collective-permute-start | bytes 393224 | tf_op jit(solution)/shard_map/ppermute | solution.py:371
  25.6 3.2 %collective-permute-start.5 = (bf16[512,128]{1,0:T(8,128)(2,1)S(1)}, bf16[512,128]{1,0:T(8,128)(2,1)S(1)}, u32[]{:S(2)}, u32[]{:S(2)}) collective-permute-start(bf16[512,128]{1,0:T(8,128)(2,1)S(1)} %get-tuple-element.33.chip), channel_id=1, source_target_pairs={{0,1},{2,3},{4,5},{6,7},{8,9},{10,11},{12,13},{14,15},{16,17},{18,... | collective-permute-start | bytes 393224 | tf_op jit(solution)/shard_map/ppermute | solution.py:371
  29.6 8.2 %collective-permute-start.6 = (bf16[512,128]{1,0:T(8,128)(2,1)S(1)}, bf16[512,128]{1,0:T(8,128)(2,1)S(1)}, u32[]{:S(2)}, u32[]{:S(2)}) collective-permute-start(bf16[512,128]{1,0:T(8,128)(2,1)S(1)} %get-tuple-element.36.cross), channel_id=1, source_target_pairs={{1,2},{3,4},{5,6},{7,8},{9,10},{11,12},{13,14},{15,16},{17,18},{19... | collective-permute-start | bytes 393224 | tf_op jit(solution)/shard_map/ppermute | solution.py:371
  34.7 3.1 %collective-permute-start.7 = (bf16[512,128]{1,0:T(8,128)(2,1)S(1)}, bf16[512,128]{1,0:T(8,128)(2,1)S(1)}, u32[]{:S(2)}, u32[]{:S(2)}) collective-permute-start(bf16[512,128]{1,0:T(8,128)(2,1)S(1)} %get-tuple-element.37.chip), channel_id=1, source_target_pairs={{0,1},{2,3},{4,5},{6,7},{8,9},{10,11},{12,13},{14,15},{16,17},{18,... | collective-permute-start | bytes 393224 | tf_op jit(solution)/shard_map/ppermute | solution.py:371

commit v7 on v5

--- a/solution.py
+++ b/solution.py
@@ -7,8 +7,6 @@
 from jax.experimental.pallas import tpu as pltpu
 from jax.sharding import Mesh, PartitionSpec as P
 
-SWEEPS = 4
-EXTRA = 16
 F32 = jnp.float32
 BF16 = jnp.bfloat16
 HI = lax.Precision.HIGHEST
@@ -52,58 +50,74 @@
     return value.astype(BF16)
 
 
+class Loads:
+    def __init__(self, arguments, arrays, sem):
+        inverses, lower, upper, basis = arguments
+        inv, coupling, base = arrays
+        self.pairs = {
+            "inverse": (inverses, inv),
+            "basis": (basis, base),
+            "lower": (lower, coupling.at[0]),
+            "upper": (upper, coupling.at[1]),
+        }
+        self.sem = sem
+        self.copies = {}
+
+    def begin(self, name, *blocks):
+        source, target = self.pairs[name]
+        for b in blocks:
+            copy = pltpu.make_async_copy(source.at[b], target.at[b], self.sem.at[len(self.copies)])
+            self.copies[name, b] = copy
+            copy.start()
+
+    def wait(self, name, *blocks):
+        for b in blocks:
+            self.copies[name, b].wait()
+
+
 def first_edges_kernel(
     count, inverses, lower, upper, basis, cross, chip, local, inv, coupling, base, sem
 ):
     width = base.shape[-1]
     last = count - 1
-    copies = {}
-
-    def begin(name, source, target):
-        copies[name] = pltpu.make_async_copy(source, target, sem.at[len(copies)])
-        copies[name].start()
-
-    def finished(*names):
-        for name in names:
-            copies[name].wait()
-
-    def begin_coupling(direction, b):
-        begin(("coupling", direction, b), (lower, upper)[direction].at[b], coupling.at[direction, b])
-
-    for b in (0, last, 1, last - 1):
-        begin(("basis", b), basis.at[b], base.at[b])
-        begin(("inverse", b), inverses.at[0, b], inv.at[b])
-    begin_coupling(1, 0)
-    begin_coupling(0, last)
-    begin_coupling(0, 0)
-    begin_coupling(1, last)
-    early = list(copies)
-    for b in range(2, last - 1):
-        begin(("basis", b), basis.at[b], base.at[b])
-        begin(("inverse", b), inverses.at[0, b], inv.at[b])
-    for b in range(1, last):
-        begin_coupling(0, b)
-        begin_coupling(1, b)
+    loads = Loads((inverses, lower, upper, basis), (inv, coupling, base), sem)
+    loads.begin("inverse", 0, last)
+    loads.begin("lower", 0)
+    loads.begin("upper", last)
+    loads.begin("basis", 0, last, 1, last - 1)
+    loads.begin("inverse", 1, last - 1)
+    loads.begin("upper", 0)
+    loads.begin("lower", last)
     both = list(enumerate(sides(count)))
     outs = (cross, chip)
-    finished(("basis", 0), ("inverse", 0), ("basis", last), ("inverse", last))
+    loads.wait("inverse", 0, last)
+    loads.wait("lower", 0)
+    loads.wait("upper", last)
+    for k, side in both:
+        outs[k][:, 2 * width :] = rounded(dot(inv[side.edge], coupling[side.outward, side.edge]))
+    loads.wait("basis", 0, last, 1, last - 1)
+    loads.wait("inverse", 1, last - 1)
+    inner = [rounded(dot(inv[side.inner], base[side.inner])) for k, side in both]
     for k, side in both:
         outs[k][:, :width] = rounded(dot(inv[side.edge], base[side.edge]))
-    finished(("basis", 1), ("inverse", 1), ("basis", last - 1), ("inverse", last - 1))
-    inner = [rounded(dot(inv[side.inner], base[side.inner])) for k, side in both]
-    finished(("coupling", 1, 0), ("coupling", 0, last))
+    loads.wait("upper", 0)
+    loads.wait("lower", last)
     rhs = []
     for k, side in both:
         value = dot(coupling[side.inward, side.edge], inner[k])
         rhs.append(rounded(base[side.edge].astype(F32) + value))
-    finished(("coupling", 0, 0), ("coupling", 1, last))
-    for k, side in both:
-        outs[k][:, 2 * width :] = rounded(dot(inv[side.edge], coupling[side.outward, side.edge]))
     for k, side in both:
         value = dot(inv[side.edge], rhs[k])
         outs[k][:, width : 2 * width] = rounded(value)
         local[k] = value
-    finished(*(name for name in copies if name not in early))
+
+
+def array_shapes(count, size, width):
+    return (
+        jax.ShapeDtypeStruct((count, size, size), BF16),
+        jax.ShapeDtypeStruct((2, count, size, size), BF16),
+        jax.ShapeDtypeStruct((count, size, width), BF16),
+    )
 
 
 def first_edges(inverses, lower, upper, basis):
@@ -115,45 +129,101 @@
             out,
             out,
             jax.ShapeDtypeStruct((2, size, width), F32),
-            jax.ShapeDtypeStruct((count, size, size), BF16),
-            jax.ShapeDtypeStruct((2, count, size, size), BF16),
-            jax.ShapeDtypeStruct((count, size, width), BF16),
+            *array_shapes(count, size, width),
         ),
         in_specs=[HBM] * 4,
         out_specs=(VM,) * 6,
-        scratch_shapes=[pltpu.SemaphoreType.DMA((4 * count,))],
+        scratch_shapes=[pltpu.SemaphoreType.DMA((12,))],
         compiler_params=params(),
         name="first_edges",
-    )(in_hbm(inverses), in_hbm(lower), in_hbm(upper), in_hbm(basis))
-
-
-def two_sweeps(count, inv, coupling, base, state, held, rhs, middle, known):
-    for b in range(1, count - 1):
-        value = dot(coupling[0, b], state[b - 1]) + dot(coupling[1, b], state[b + 1])
-        rhs[b] = rounded(base[b].astype(F32) + value)
-    for b in range(1, count - 1):
+    )(*(in_hbm(x) for x in (inverses, lower, upper, basis)))
+
+
+def ahead_blocks(count):
+    return range(3, count - 3)
+
+
+def right_side(b, coupling, base, left, right):
+    value = dot(coupling[0, b], left) + dot(coupling[1, b], right)
+    return rounded(base[b].astype(F32) + value)
+
+
+def two_sweeps(count, inv, coupling, base, state, held, rhs, known, todo, ready=lambda b: None):
+    for b in todo:
+        ready(b)
+        rhs[b] = right_side(b, coupling, base, state[b - 1], state[b + 1])
+    for b in todo:
         held[b] = rounded(dot(inv[b], rhs[b]))
     for b in range(2, count - 2):
-        value = dot(coupling[0, b], held[b - 1]) + dot(coupling[1, b], held[b + 1])
-        rhs[b] = rounded(base[b].astype(F32) + value)
+        rhs[b] = right_side(b, coupling, base, held[b - 1], held[b + 1])
     for k, side in enumerate(sides(count)):
         for j, (b, further) in enumerate(((side.edge, side.inner), (side.inner, side.third))):
             known[2 * k + j] = base[b].astype(F32) + dot(coupling[side.inward, b], held[further])
-    for b in range(2, count - 2):
-        middle[b - 2] = rounded(dot(inv[b], rhs[b]))
-
-
-def first_pair_kernel(count, inv, coupling, base, cross, chip, middle, known, state, held, rhs):
+
+
+def first_pair_kernel(
+    count, weight, inverses, lower, upper, basis, inv_in, coupling_in, base_in, cross, chip,
+    inv, coupling, base, middle, known, ahead, state, held, rhs, sem,
+):
     width = base.shape[-1]
+    inside = range(1, count - 1)
+    deep = range(2, count - 2)
+    loads = Loads((inverses, lower, upper, basis), (inv, coupling, base), sem)
+    for b in deep:
+        loads.begin("basis", b)
+        loads.begin("inverse", b)
+    for b in inside:
+        loads.begin("lower", b)
+        loads.begin("upper", b)
     for side, payload in zip(sides(count), (cross, chip)):
         state[side.edge] = payload[:, :width]
-    for b in range(1, count - 1):
+    for b in (1, count - 2, *deep):
+        if b in deep:
+            loads.wait("basis", b)
+            loads.wait("inverse", b)
         state[b] = rounded(dot(inv[b], base[b]))
-    two_sweeps(count, inv, coupling, base, state, held, rhs, middle, known)
-
-
-def pair_kernel(
-    count, inv, coupling, base, cross, chip, inner, previous, middle, known, state, held, rhs
+
+    def ready(b):
+        loads.wait("lower", b)
+        loads.wait("upper", b)
+
+    two_sweeps(count, inv, coupling, base, state, held, rhs, known, inside, ready)
+    for b in deep:
+        middle[b - 2] = rounded(dot(inv[b], rhs[b]))
+    for b in ahead_blocks(count):
+        rhs[b] = right_side(b, coupling, base, middle[b - 3], middle[b - 1])
+    for b in ahead_blocks(count):
+        ahead[b - 3] = rounded(dot(inv[b], rhs[b]))
+
+
+def pair_cost(count, size, width):
+    return cost(12 * (count - 2) * size * size * width, 6 * count * size * size)
+
+
+def first_pair(weight, arguments, arrays, cross, chip):
+    count, size, width = arrays[2].shape
+    return pl.pallas_call(
+        functools.partial(first_pair_kernel, count),
+        out_shape=(
+            *array_shapes(count, size, width),
+            jax.ShapeDtypeStruct((count - 4, size, width), BF16),
+            jax.ShapeDtypeStruct((4, size, width), F32),
+            jax.ShapeDtypeStruct((count - 6, size, width), BF16),
+        ),
+        in_specs=[SM] + [HBM] * 4 + [VM] * 5,
+        out_specs=(VM,) * 6,
+        scratch_shapes=[pltpu.VMEM((count, size, width), BF16)] * 3
+        + [pltpu.SemaphoreType.DMA((4 * count,))],
+        input_output_aliases={5: 0, 6: 1, 7: 2},
+        compiler_params=params(),
+        cost_estimate=pair_cost(count, size, width),
+        name="first_pair",
+    )(weight, *(in_hbm(x) for x in arguments), *arrays, cross, chip)
+
+
+def last_pair_kernel(
+    count, weight, inv, coupling, base, cross, chip, inner, previous, ahead, middle, known,
+    state, held, rhs,
 ):
     width = base.shape[-1]
     for k, (side, payload) in enumerate(zip(sides(count), (cross, chip))):
@@ -161,28 +231,32 @@
         state[side.inner] = inner[k]
     for b in range(2, count - 2):
         state[b] = previous[b - 2]
-    two_sweeps(count, inv, coupling, base, state, held, rhs, middle, known)
-
-
-def pair_call(kernel, name, *operands):
+    for b in ahead_blocks(count):
+        held[b] = ahead[b - 3]
+    todo = [b for b in range(1, count - 1) if b not in ahead_blocks(count)]
+    two_sweeps(count, inv, coupling, base, state, held, rhs, known, todo)
+    for b in range(2, count - 2):
+        middle[b - 2] = rounded(weight[0] * dot(inv[b], rhs[b]))
+
+
+def last_pair(weight, *operands):
     count, size, width = operands[2].shape
-    flops = 12 * (count - 2) * size * size * width
-    return pl.pallas_call(
-        functools.partial(kernel, count),
+    return pl.pallas_call(
+        functools.partial(last_pair_kernel, count),
         out_shape=(
             jax.ShapeDtypeStruct((count - 4, size, width), BF16),
             jax.ShapeDtypeStruct((4, size, width), F32),
         ),
-        in_specs=[VM] * len(operands),
+        in_specs=[SM] + [VM] * len(operands),
         out_specs=(VM, VM),
         scratch_shapes=[pltpu.VMEM((count, size, width), BF16)] * 3,
         compiler_params=params(),
-        cost_estimate=cost(flops, 6 * count * size * size),
-        name=name,
-    )(*operands)
-
-
-def absorbed(count, inv, coupling, known, pieces, local):
+        cost_estimate=pair_cost(count, size, width),
+        name="last_pair",
+    )(weight, *operands)
+
+
+def absorbed(count, inv, coupling, known, pieces, local, scale=lambda value: value):
     width = known.shape[-1]
     both = list(enumerate(sides(count)))
     values = []
@@ -199,7 +273,9 @@
             b = side.inner if j else side.edge
             value = known[2 * k + j] + dot(coupling[side.outward, b], values[k][j])
             rhs.append((b, rounded(value)))
-    inner_a, inner_b, edge_a, edge_b = [rounded(dot(inv[b], value)) for b, value in rhs]
+    inner_a, inner_b, edge_a, edge_b = [
+        rounded(scale(dot(inv[b], value))) for b, value in rhs
+    ]
     return (edge_a, edge_b), (inner_a, inner_b)
 
 
@@ -247,30 +323,18 @@
     count, weight, inv, coupling, known, middle, cross_joint, chip_joint, from_cross_joint,
     from_chip_joint, cross, chip, local, from_cross, from_chip, out,
 ):
-    size, width = known.shape[1:]
     pieces = (
         (cross_joint, from_cross_joint, cross, from_cross),
         (chip_joint, from_chip_joint, chip, from_chip),
     )
-    edge, inner = absorbed(count, inv, coupling, known, pieces, local)
+    for b in range(2, count - 2):
+        out[b] = middle[b - 2]
+    edge, inner = absorbed(
+        count, inv, coupling, known, pieces, local, lambda value: weight[0] * value
+    )
     for k, side in enumerate(sides(count)):
-        out[side.edge, :size] = edge[k]
-        out[side.inner, :size] = inner[k]
-    for b in range(2, count - 2):
-        out[b, :size] = middle[b - 2]
-    full = jnp.full((EXTRA, width), weight[0], F32)
-    high_part = rounded(full)
-    rest = full - high_part.astype(F32)
-    mid_part = rounded(rest)
-    low_part = rounded(rest - mid_part.astype(F32))
-    place = lax.broadcasted_iota(jnp.int32, (EXTRA, width), 0)
-    rows = jnp.where(
-        place == 0,
-        high_part.astype(F32),
-        jnp.where(place == 1, mid_part.astype(F32), low_part.astype(F32)),
-    )
-    for b in range(count):
-        out[b, size:] = rounded(rows)
+        out[side.edge] = edge[k]
+        out[side.inner] = inner[k]
 
 
 def finish(weight, *operands):
@@ -278,7 +342,7 @@
     width = operands[2].shape[-1]
     return pl.pallas_call(
         functools.partial(finish_kernel, count),
-        out_shape=jax.ShapeDtypeStruct((count, size + EXTRA, width), BF16),
+        out_shape=jax.ShapeDtypeStruct((count, size, width), BF16),
         in_specs=[SM] + [VM] * len(operands),
         out_specs=VM,
         compiler_params=params(),
@@ -287,13 +351,10 @@
     )(weight, *operands)
 
 
-def gram_kernel(size, parts, received, filtered, gram):
-    total = None
-    for p in range(received.shape[0]):
-        rows = received[p, size : size + 3].astype(F32)
-        weight = rows[0:1] + rows[1:2] + rows[2:3]
-        term = weight * received[p, :size].astype(F32)
-        total = term if total is None else total + term
+def gram_kernel(received, filtered, gram):
+    total = received[0].astype(F32)
+    for p in range(1, received.shape[0]):
+        total = total + received[p].astype(F32)
     filtered[...] = total
     value = lax.dot_general(
         total, total, (((0,), (0,)), ((), ())), precision=HI, preferred_element_type=F32
@@ -302,10 +363,9 @@
 
 
 def partial_gram(received, parts):
-    poles, rows, width = received.shape
-    size = rows - EXTRA
-    return pl.pallas_call(
-        functools.partial(gram_kernel, size, parts),
+    poles, size, width = received.shape
+    return pl.pallas_call(
+        gram_kernel,
         out_shape=(
             jax.ShapeDtypeStruct((size, width), F32),
             jax.ShapeDtypeStruct((parts, width // parts, width), F32),
@@ -422,22 +482,22 @@
 def shards(basis, inverses, lower, upper, pole_weights):
     rows, width = basis.shape
     count, size = inverses.shape[1:3]
-    cross, chip, local, inv, coupling, base = first_edges(
-        inverses, lower, upper, basis.reshape(count, size, width)
-    )
+    arguments = (
+        inverses.reshape(count, size, size), lower, upper, basis.reshape(count, size, width)
+    )
+    cross, chip, local, *arrays = first_edges(*arguments)
     joints = (cross, chip)
-    received = halo_joints = swapped(cross, chip)
-    middle, known = pair_call(first_pair_kernel, "first_pair", inv, coupling, base, cross, chip)
-    for _ in range(SWEEPS // 2 - 1):
-        cross, chip, local, inner = meet(
-            inv, coupling, base, known, cross, chip, local, *received
-        )
-        received = swapped(cross, chip)
-        middle, known = pair_call(
-            pair_kernel, "pair", inv, coupling, base, cross, chip, inner, middle
-        )
+    halo_joints = swapped(cross, chip)
+    inv, coupling, base, middle, known, ahead = first_pair(
+        pole_weights, arguments, arrays, cross, chip
+    )
+    cross, chip, local, inner = meet(inv, coupling, base, known, cross, chip, local, *halo_joints)
+    halos = swapped(cross, chip)
+    middle, known = last_pair(
+        pole_weights, inv, coupling, base, cross, chip, inner, middle, ahead
+    )
     solved = finish(
-        pole_weights, inv, coupling, known, middle, *joints, *halo_joints, cross, chip, local, *received
+        pole_weights, inv, coupling, known, middle, *joints, *halo_joints, cross, chip, local, *halos
     )
     received = exchange(solved, POLE)
     plane = lax.axis_size(PLANE)

time: 113 us -> 110 us (0.973)
  waiting for transfers between devices: 3.93 us -> 0.01 us
  Pallas kernels: 37.9 us -> 39.9 us
  blocking collectives: 61 us -> 59.8 us
    ppermute x4, waiting for transfers between devices: 3.93 us -> 0.01 us  [swapped(): lax.ppermute(value, ROW, joined + [(j, i) for i, j in joined])]
    pallas_call x3, Pallas kernels: 11 us -> 14.4 us  [the longest x1 9.86 us: first_pair(): pl.pallas_call(functools.partial(first_pair_kernel, count), out_shape=(*a...]
    pallas_call x1, Pallas kernels: 5.18 us -> 3.82 us  [first_edges(): pl.pallas_call(functools.partial(first_edges_kernel, count), out_shape=(o...]
    all_to_all x4, blocking collectives: 61 us -> 59.8 us  [exchange(): return lax.all_to_all(value, axes, split_axis=0, concat_axis=0, tiled=True)]
  transfers between devices with their start and end apart: 4 -> 4, of which waited for: 1 -> 0; matrix products, arithmetic and copies ran while one was open for 0% -> 0% of each run, Pallas kernels for 9% -> 13%
where the time goes in v7:
time: 110 us
  blocking collectives  59.8 us (54%)
  Pallas kernels  39.9 us (36%)
  starting transfers between devices  9.22 us (8%)
    all_to_all x4, blocking collectives, exchange(): return lax.all_to_all(value, axes, split_axis=0, concat_axis=0, tiled=True)  59.8 us
    pallas_call x1, Pallas kernels, orthonormal(): pl.pallas_call(functools.partial(orthonormal_kernel, float(total_rows)),...  17.5 us
    pallas_call x1, Pallas kernels, first_pair(): pl.pallas_call(functools.partial(first_pair_kernel, count), out_shape=(*a...  9.86 us
    ppermute x4, starting transfers between devices, swapped(): lax.ppermute(value, ROW, joined + [(j, i) for i, j in joined])  9.22 us
    pallas_call x1, Pallas kernels, last_pair(): pl.pallas_call(functools.partial(last_pair_kernel, count), out_shape=(jax...  4.05 us
    pallas_call x1, Pallas kernels, first_edges(): pl.pallas_call(functools.partial(first_edges_kernel, count), out_shape=(o...  3.82 us
    pallas_call x1, Pallas kernels, meet(): pl.pallas_call(functools.partial(meet_kernel, count), out_shape=(out, out...  2.4 us
  transfers between devices with their start and end apart: 4, of which 0 were waited for; matrix products, arithmetic and copies ran while one was open for 0% of the time, Pallas kernels for 13%

profile of v7, /device:TPU:1, one launch (start us, length us, event | category | flops | bytes accessed | tf_op | source)
XLA Modules:
  0.0 109.7 jit_solution(14121943110666486314)
XLA Ops:
  0.0 3.8 %first_edges.1 = (bf16[512,768]{1,0:T(8,128)(2,1)S(1)}, bf16[512,768]{1,0:T(8,128)(2,1)S(1)}, f32[2,512,128]{2,1,0:T(8,128)S(1)}, bf16[8,512,512]{2,1,0:T(8,128)...) custom-call(bf16[8,512,512]{2,1,0:T(8,128)(2,1)} %bitcast.2, ...), custom_call_target="tpu_custom_call" | custom-call | tf_op jit(solution)/shard_map/first_edges/pallas_call | solution.py:126
  3.8 4.9 %collective-permute-start = (bf16[512,768]{1,0:T(8,128)(2,1)S(1)}, bf16[512,768]{1,0:T(8,128)(2,1)S(1)}, u32[]{:S(2)}, u32[]{:S(2)}) collective-permute-start(bf16[512,768]{1,0:T(8,128)(2,1)S(1)} %get-tuple-element.28.cross.cross_joint), channel_id=1, source_target_pairs={{1,2},{3,4},{5,6},{7,8},{9,10},{11,12},{13,14},{15,16},{17,18},{19... | collective-permute-start | bytes 2359304 | tf_op jit(solution)/shard_map/ppermute | solution.py:473
  8.8 0.1 collective-permute-start.1
  9.5 9.9 %first_pair.1 = (bf16[8,512,512]{2,1,0:T(8,128)(2,1)S(1)}, bf16[2,8,512,512]{3,2,1,0:T(8,128)(2,1)S(1)}, bf16[8,512,128]{2,1,0:T(8,128)(2,1)S(1)}, bf16[4,512,12...) custom-call(f32[1]{0:T(128)S(6)} %copy.12.weight, ...), custom_call_target="tpu_custom_call", output_to_operand_aliasing={{0}: (5, {}), {1}: (6, {}), {2}: (7, {})} | custom-call | flops 2415919104 | bytes 12582912 | tf_op jit(solution)/shard_map/first_pair/pallas_call | solution.py:205
  19.4 0.0 collective-permute-done.from_cross.from_cross_joint
  19.4 0.0 collective-permute-done.1.from_chip.from_chip_joint
  19.4 2.4 %meet.1 = (bf16[512,256]{1,0:T(8,128)(2,1)S(1)}, bf16[512,256]{1,0:T(8,128)(2,1)S(1)}, f32[2,512,128]{2,1,0:T(8,128)S(1)}, bf16[2,512,128]{2,1,0:T(8,128)(2,1)S(1)}) custom-call(bf16[8,512,512]{2,1,0:T(8,128)(2,1)S(1)} %get-tuple-element.30.inv, bf16[2,8,512,512]{3,2,1,0:T(8,128)(2,1)S(1)} %get-tuple-element.31.coupling, ...), custom_call_target="tpu_custom_call" | custom-call | flops 1073741824 | bytes 6291456 | tf_op jit(solution)/shard_map/meet/pallas_call | solution.py:306
  21.8 3.9 %collective-permute-start.2 = (bf16[512,256]{1,0:T(8,128)(2,1)S(1)}, bf16[512,256]{1,0:T(8,128)(2,1)S(1)}, u32[]{:S(2)}, u32[]{:S(2)}) collective-permute-start(bf16[512,256]{1,0:T(8,128)(2,1)S(1)} %get-tuple-element.35.cross), channel_id=1, source_target_pairs={{1,2},{3,4},{5,6},{7,8},{9,10},{11,12},{13,14},{15,16},{17,18},{19... | collective-permute-start | bytes 786440 | tf_op jit(solution)/shard_map/ppermute | solution.py:473
  25.7 0.3 collective-permute-start.3
  26.0 4.0 %last_pair.1 = (bf16[4,512,128]{2,1,0:T(8,128)(2,1)S(1)}, f32[4,512,128]{2,1,0:T(8,128)S(1)}) custom-call(f32[1]{0:T(128)S(6)} %copy.12.weight, bf16[8,512,512]{2,1,0:T(8,128)(2,1)S(1)} %get-tuple-element.30.inv, bf16[2,8,512,512]{3,2,1,0:T(8,128)(2,1)S(1)} %get-tuple-element.31.coupling, bf16[8,512,128]{2,1,0:T(8,128)(2,1)S(1)} %get-tuple-element.32.base, ...), custom_call_target="tpu_custom_call" | custom-call | flops 2415919104 | bytes 12582912 | tf_op jit(solution)/shard_map/last_pair/pallas_call | solution.py:244
  30.1 0.0 collective-permute-done.2.from_cross
  30.1 0.0 collective-permute-done.3.from_chip
  30.1 1.8 %finish.1 = bf16[8,512,128]{2,1,0:T(8,128)(2,1)S(1)} custom-call(f32[1]{0:T(128)S(6)} %copy.12.weight, bf16[8,512,512]{2,1,0:T(8,128)(2,1)S(1)} %get-tuple-element.30.inv, bf16[2,8,512,512]{3,2,1,0:T(8,128)(2,1)S(1)} %get-tuple-element.31.coupling, f32[4,512,128]{2,1,0:T(8,128)S(1)} %get-tuple-element.40.known, ...), custom_call_target="tpu_custom_call" | custom-call | flops 805306368 | bytes 6291456 | tf_op jit(solution)/shard_map/finish/pallas_call | solution.py:343
  31.9 22.1 %all_to_all.20.received = bf16[8,512,128]{2,1,0:T(8,128)(2,1)S(1)} all-to-all(bf16[8,512,128]{2,1,0:T(8,128)(2,1)S(1)} %finish.1), channel_id=1, replica_groups=mesh['x_hi'=2,'y'=4,'x_lo'=2,'z'=8,'core'=2] {'x_hi','y'}, dimensions={0} | all-to-all | bytes 2097152 | tf_op jit(solution)/shard_map/all_to_all | solution.py:479
  54.0 0.5 gram.1
  54.5 14.1 %all_to_all.21 = f32[16,8,128]{2,1,0:T(8,128)S(1)} all-to-all(f32[16,8,128]{2,1,0:T(8,128)S(1)} %get-tuple-element.43), channel_id=1, replica_groups=mesh['x_hi'=2,'y'=4,'x_lo'=2,'z'=8,'core'=2] {'x_hi','y','x_lo'}, dimensions={0} | all-to-all | bytes 131072 | tf_op jit(solution)/shard_map/all_to_all | solution.py:479
  68.7 14.2 %all_to_all.22 = f32[16,8,128]{2,1,0:T(8,128)S(1)} all-to-all(f32[16,8,128]{2,1,0:T(8,128)S(1)} %broadcast_in_dim.4), channel_id=1, replica_groups=mesh['x_hi'=2,'y'=4,'x_lo'=2,'z'=8,'core'=2] {'z','core'}, dimensions={0} | all-to-all | bytes 131072 | tf_op jit(solution)/shard_map/all_to_all | solution.py:479
  82.8 9.4 %all_to_all.23.gram = f32[16,8,128]{2,1,0:T(8,128)S(1)} all-to-all(f32[16,8,128]{2,1,0:T(8,128)S(1)} %broadcast_in_dim.5), channel_id=1, replica_groups=mesh['x_hi'=2,'y'=4,'x_lo'=2,'z'=8,'core'=2] {'x_hi','y','x_lo'}, dimensions={0} | all-to-all | bytes 131072 | tf_op jit(solution)/shard_map/all_to_all | solution.py:479
  92.2 17.5 %orthonormal.1 = f32[512,128]{1,0:T(8,128)} custom-call(f32[16,8,128]{2,1,0:T(8,128)S(1)} %all_to_all.23.gram, f32[512,128]{1,0:T(8,128)S(1)} %get-tuple-element.44.filtered), custom_call_target="tpu_custom_call" | custom-call | tf_op jit(solution)/shard_map/orthonormal/pallas_call | solution.py:451
  (4 shorter events, 0.1 us)
Async XLA Ops:
  3.8 15.6 %collective-permute-start = (bf16[512,768]{1,0:T(8,128)(2,1)S(1)}, bf16[512,768]{1,0:T(8,128)(2,1)S(1)}, u32[]{:S(2)}, u32[]{:S(2)}) collective-permute-start(bf16[512,768]{1,0:T(8,128)(2,1)S(1)} %get-tuple-element.28.cross.cross_joint), channel_id=1, source_target_pairs={{1,2},{3,4},{5,6},{7,8},{9,10},{11,12},{13,14},{15,16},{17,18},{19... | collective-permute-start | bytes 2359304 | tf_op jit(solution)/shard_map/ppermute | solution.py:473
  8.8 10.6 %collective-permute-start.1 = (bf16[512,768]{1,0:T(8,128)(2,1)S(1)}, bf16[512,768]{1,0:T(8,128)(2,1)S(1)}, u32[]{:S(2)}, u32[]{:S(2)}) collective-permute-start(bf16[512,768]{1,0:T(8,128)(2,1)S(1)} %get-tuple-element.29.chip.chip_joint), channel_id=1, source_target_pairs={{0,1},{2,3},{4,5},{6,7},{8,9},{10,11},{12,13},{14,15},{16,17},{18,... | collective-permute-start | bytes 2359304 | tf_op jit(solution)/shard_map/ppermute | solution.py:473
  21.8 8.3 %collective-permute-start.2 = (bf16[512,256]{1,0:T(8,128)(2,1)S(1)}, bf16[512,256]{1,0:T(8,128)(2,1)S(1)}, u32[]{:S(2)}, u32[]{:S(2)}) collective-permute-start(bf16[512,256]{1,0:T(8,128)(2,1)S(1)} %get-tuple-element.35.cross), channel_id=1, source_target_pairs={{1,2},{3,4},{5,6},{7,8},{9,10},{11,12},{13,14},{15,16},{17,18},{19... | collective-permute-start | bytes 786440 | tf_op jit(solution)/shard_map/ppermute | solution.py:473
  25.7 4.4 %collective-permute-start.3 = (bf16[512,256]{1,0:T(8,128)(2,1)S(1)}, bf16[512,256]{1,0:T(8,128)(2,1)S(1)}, u32[]{:S(2)}, u32[]{:S(2)}) collective-permute-start(bf16[512,256]{1,0:T(8,128)(2,1)S(1)} %get-tuple-element.36.chip), channel_id=1, source_target_pairs={{0,1},{2,3},{4,5},{6,7},{8,9},{10,11},{12,13},{14,15},{16,17},{18,... | collective-permute-start | bytes 786440 | tf_op jit(solution)/shard_map/ppermute | solution.py:473

commit v8 on v7

--- a/solution.py
+++ b/solution.py
@@ -51,15 +51,8 @@
 
 
 class Loads:
-    def __init__(self, arguments, arrays, sem):
-        inverses, lower, upper, basis = arguments
-        inv, coupling, base = arrays
-        self.pairs = {
-            "inverse": (inverses, inv),
-            "basis": (basis, base),
-            "lower": (lower, coupling.at[0]),
-            "upper": (upper, coupling.at[1]),
-        }
+    def __init__(self, pairs, sem):
+        self.pairs = pairs
         self.sem = sem
         self.copies = {}
 
@@ -76,11 +69,19 @@
 
 
 def first_edges_kernel(
-    count, inverses, lower, upper, basis, cross, chip, local, inv, coupling, base, sem
+    count, inverses, lower, upper, basis, cross, chip, local, coupling, inv, base, sem
 ):
     width = base.shape[-1]
     last = count - 1
-    loads = Loads((inverses, lower, upper, basis), (inv, coupling, base), sem)
+    loads = Loads(
+        {
+            "inverse": (inverses, inv),
+            "basis": (basis, base),
+            "lower": (lower, coupling.at[0]),
+            "upper": (upper, coupling.at[1]),
+        },
+        sem,
+    )
     loads.begin("inverse", 0, last)
     loads.begin("lower", 0)
     loads.begin("upper", last)
@@ -112,14 +113,6 @@
         local[k] = value
 
 
-def array_shapes(count, size, width):
-    return (
-        jax.ShapeDtypeStruct((count, size, size), BF16),
-        jax.ShapeDtypeStruct((2, count, size, size), BF16),
-        jax.ShapeDtypeStruct((count, size, width), BF16),
-    )
-
-
 def first_edges(inverses, lower, upper, basis):
     count, size, width = basis.shape
     out = jax.ShapeDtypeStruct((size, 2 * width + size), BF16)
@@ -129,11 +122,15 @@
             out,
             out,
             jax.ShapeDtypeStruct((2, size, width), F32),
-            *array_shapes(count, size, width),
+            jax.ShapeDtypeStruct((2, count, size, size), BF16),
         ),
         in_specs=[HBM] * 4,
-        out_specs=(VM,) * 6,
-        scratch_shapes=[pltpu.SemaphoreType.DMA((12,))],
+        out_specs=(VM,) * 4,
+        scratch_shapes=[
+            pltpu.VMEM((count, size, size), BF16),
+            pltpu.VMEM((count, size, width), BF16),
+            pltpu.SemaphoreType.DMA((12,)),
+        ],
         compiler_params=params(),
         name="first_edges",
     )(*(in_hbm(x) for x in (inverses, lower, upper, basis)))
@@ -162,25 +159,20 @@
 
 
 def first_pair_kernel(
-    count, weight, inverses, lower, upper, basis, inv_in, coupling_in, base_in, cross, chip,
-    inv, coupling, base, middle, known, ahead, state, held, rhs, sem,
+    count, weight, lower, upper, coupling_in, inv, base, cross, chip, coupling, middle, known,
+    ahead, factor, state, held, rhs, sem,
 ):
     width = base.shape[-1]
     inside = range(1, count - 1)
     deep = range(2, count - 2)
-    loads = Loads((inverses, lower, upper, basis), (inv, coupling, base), sem)
-    for b in deep:
-        loads.begin("basis", b)
-        loads.begin("inverse", b)
+    factor[...] = jnp.full(factor.shape, weight[0], F32)
+    loads = Loads({"lower": (lower, coupling.at[0]), "upper": (upper, coupling.at[1])}, sem)
     for b in inside:
         loads.begin("lower", b)
         loads.begin("upper", b)
     for side, payload in zip(sides(count), (cross, chip)):
         state[side.edge] = payload[:, :width]
-    for b in (1, count - 2, *deep):
-        if b in deep:
-            loads.wait("basis", b)
-            loads.wait("inverse", b)
+    for b in inside:
         state[b] = rounded(dot(inv[b], base[b]))
 
     def ready(b):
@@ -200,32 +192,35 @@
     return cost(12 * (count - 2) * size * size * width, 6 * count * size * size)
 
 
-def first_pair(weight, arguments, arrays, cross, chip):
-    count, size, width = arrays[2].shape
+def first_pair(weight, lower, upper, coupling, inv, base, cross, chip):
+    count, size, width = base.shape
     return pl.pallas_call(
         functools.partial(first_pair_kernel, count),
         out_shape=(
-            *array_shapes(count, size, width),
+            jax.ShapeDtypeStruct(coupling.shape, BF16),
             jax.ShapeDtypeStruct((count - 4, size, width), BF16),
             jax.ShapeDtypeStruct((4, size, width), F32),
             jax.ShapeDtypeStruct((count - 6, size, width), BF16),
+            jax.ShapeDtypeStruct((8, width), F32),
         ),
-        in_specs=[SM] + [HBM] * 4 + [VM] * 5,
-        out_specs=(VM,) * 6,
+        in_specs=[SM] + [HBM] * 2 + [VM] * 5,
+        out_specs=(VM,) * 5,
         scratch_shapes=[pltpu.VMEM((count, size, width), BF16)] * 3
-        + [pltpu.SemaphoreType.DMA((4 * count,))],
-        input_output_aliases={5: 0, 6: 1, 7: 2},
+        + [pltpu.SemaphoreType.DMA((2 * count,))],
+        input_output_aliases={3: 0},
         compiler_params=params(),
         cost_estimate=pair_cost(count, size, width),
         name="first_pair",
-    )(weight, *(in_hbm(x) for x in arguments), *arrays, cross, chip)
+    )(weight, in_hbm(lower), in_hbm(upper), coupling, inv, base, cross, chip)
 
 
 def last_pair_kernel(
-    count, weight, inv, coupling, base, cross, chip, inner, previous, ahead, middle, known,
-    state, held, rhs,
+    count, weight, inv, coupling, base, cross, chip, inner, previous, ahead, from_cross_joint,
+    from_chip_joint, middle, known, change, state, held, rhs,
 ):
     width = base.shape[-1]
+    for k, (own, halo_joint) in enumerate(((cross, from_cross_joint), (chip, from_chip_joint))):
+        change[k] = dot(halo_joint[:, 2 * width :], own[:, :width])
     for k, (side, payload) in enumerate(zip(sides(count), (cross, chip))):
         state[side.edge] = payload[:, :width]
         state[side.inner] = inner[k]
@@ -236,7 +231,7 @@
     todo = [b for b in range(1, count - 1) if b not in ahead_blocks(count)]
     two_sweeps(count, inv, coupling, base, state, held, rhs, known, todo)
     for b in range(2, count - 2):
-        middle[b - 2] = rounded(weight[0] * dot(inv[b], rhs[b]))
+        middle[b - 2] = rounded(weight[:1] * dot(inv[b], rhs[b]))
 
 
 def last_pair(weight, *operands):
@@ -246,9 +241,10 @@
         out_shape=(
             jax.ShapeDtypeStruct((count - 4, size, width), BF16),
             jax.ShapeDtypeStruct((4, size, width), F32),
+            jax.ShapeDtypeStruct((2, size, width), F32),
         ),
-        in_specs=[SM] + [VM] * len(operands),
-        out_specs=(VM, VM),
+        in_specs=[VM] * (1 + len(operands)),
+        out_specs=(VM,) * 3,
         scratch_shapes=[pltpu.VMEM((count, size, width), BF16)] * 3,
         compiler_params=params(),
         cost_estimate=pair_cost(count, size, width),
@@ -261,10 +257,8 @@
     both = list(enumerate(sides(count)))
     values = []
     for k, side in both:
-        joint, halo_joint, own, halo = pieces[k]
-        halo_next = halo[:, width : 2 * width].astype(F32) + dot(
-            halo_joint[:, 2 * width :], own[:, :width]
-        )
+        joint, halo_change, halo = pieces[k]
+        halo_next = halo[:, width : 2 * width].astype(F32) + halo_change
         edge_next = local[k] + dot(joint[:, 2 * width :], halo[:, :width])
         values.append((rounded(halo_next), rounded(edge_next)))
     rhs = []
@@ -284,7 +278,10 @@
     cross_out, chip_out, local_out, inner_out,
 ):
     width = known.shape[-1]
-    pieces = ((cross, from_cross, cross, from_cross), (chip, from_chip, chip, from_chip))
+    pieces = [
+        (own, dot(halo[:, 2 * width :], own[:, :width]), halo)
+        for own, halo in ((cross, from_cross), (chip, from_chip))
+    ]
     edge, inner = absorbed(count, inv, coupling, known, pieces, local)
     both = list(enumerate(sides(count)))
     outs = (cross_out, chip_out)
@@ -320,17 +317,14 @@
 
 
 def finish_kernel(
-    count, weight, inv, coupling, known, middle, cross_joint, chip_joint, from_cross_joint,
-    from_chip_joint, cross, chip, local, from_cross, from_chip, out,
+    count, weight, inv, coupling, known, change, middle, cross_joint, chip_joint, local,
+    from_cross, from_chip, out,
 ):
-    pieces = (
-        (cross_joint, from_cross_joint, cross, from_cross),
-        (chip_joint, from_chip_joint, chip, from_chip),
-    )
+    pieces = ((cross_joint, change[0], from_cross), (chip_joint, change[1], from_chip))
     for b in range(2, count - 2):
         out[b] = middle[b - 2]
     edge, inner = absorbed(
-        count, inv, coupling, known, pieces, local, lambda value: weight[0] * value
+        count, inv, coupling, known, pieces, local, lambda value: weight[:1] * value
     )
     for k, side in enumerate(sides(count)):
         out[side.edge] = edge[k]
@@ -343,7 +337,7 @@
     return pl.pallas_call(
         functools.partial(finish_kernel, count),
         out_shape=jax.ShapeDtypeStruct((count, size, width), BF16),
-        in_specs=[SM] + [VM] * len(operands),
+        in_specs=[VM] * (1 + len(operands)),
         out_specs=VM,
         compiler_params=params(),
         cost_estimate=cost(24 * size * size * width, 24 * size * size),
@@ -402,6 +396,18 @@
     inverse[...] = work[:, n:]
 
 
+def split_product(a, b):
+    a_high, b_high = rounded(a), rounded(b)
+    a_low = rounded(a - a_high.astype(F32))
+    b_low = rounded(b - b_high.astype(F32))
+    left = jnp.concatenate([a_high, a_low], axis=1)
+    right = jnp.concatenate([b_high, b_high], axis=1)
+    over = (((1,), (1,)), ((), ()))
+    return lax.dot_general(left, right, over, preferred_element_type=F32) + lax.dot_general(
+        a_high, b_low, over, preferred_element_type=F32
+    )
+
+
 def orthonormal_kernel(total_rows, gram, filtered, out, work, inverse):
     n = out.shape[-1]
     value = gram[...].reshape(n, n) / total_rows
@@ -441,9 +447,7 @@
     def _():
         eliminate(value, work, inverse)
 
-    out[...] = lax.dot_general(
-        filtered[...], inverse[...], (((1,), (1,)), ((), ())), precision=HI, preferred_element_type=F32
-    )
+    out[...] = split_product(filtered[...], inverse[...])
 
 
 def orthonormal(gram, filtered, total_rows):
@@ -482,22 +486,21 @@
 def shards(basis, inverses, lower, upper, pole_weights):
     rows, width = basis.shape
     count, size = inverses.shape[1:3]
-    arguments = (
-        inverses.reshape(count, size, size), lower, upper, basis.reshape(count, size, width)
-    )
-    cross, chip, local, *arrays = first_edges(*arguments)
+    inv = inverses.reshape(count, size, size)
+    base = basis.reshape(count, size, width)
+    cross, chip, local, coupling = first_edges(inv, lower, upper, base)
     joints = (cross, chip)
     halo_joints = swapped(cross, chip)
-    inv, coupling, base, middle, known, ahead = first_pair(
-        pole_weights, arguments, arrays, cross, chip
+    coupling, middle, known, ahead, weight = first_pair(
+        pole_weights, lower, upper, coupling, inv, base, cross, chip
     )
     cross, chip, local, inner = meet(inv, coupling, base, known, cross, chip, local, *halo_joints)
     halos = swapped(cross, chip)
-    middle, known = last_pair(
-        pole_weights, inv, coupling, base, cross, chip, inner, middle, ahead
+    middle, known, change = last_pair(
+        weight, inv, coupling, base, cross, chip, inner, middle, ahead, *halo_joints
     )
     solved = finish(
-        pole_weights, inv, coupling, known, middle, *joints, *halo_joints, cross, chip, local, *halos
+        weight, inv, coupling, known, change, middle, *joints, local, *halos
     )
     received = exchange(solved, POLE)
     plane = lax.axis_size(PLANE)

time: 110 us -> 109 us (level)
  Pallas kernels: 39.9 us -> 38.8 us
    pallas_call x1, Pallas kernels: 9.86 us -> 8.62 us  [first_pair(): pl.pallas_call(functools.partial(first_pair_kernel, count), out_shape=(ja...]
  transfers between devices with their start and end apart: 4 -> 4, of which waited for: 0 -> 1; matrix products, arithmetic and copies ran while one was open for 0% -> 0% of each run, Pallas kernels for 13% -> 12%
where the time goes in v8:
time: 109 us
  blocking collectives  60.3 us (55%)
  Pallas kernels  38.8 us (36%)
  starting transfers between devices  9 us (8%)
    all_to_all x4, blocking collectives, exchange(): return lax.all_to_all(value, axes, split_axis=0, concat_axis=0, tiled=True)  60.3 us
    pallas_call x1, Pallas kernels, orthonormal(): pl.pallas_call(functools.partial(orthonormal_kernel, float(total_rows)),...  17.4 us
    ppermute x4, starting transfers between devices, swapped(): lax.ppermute(value, ROW, joined + [(j, i) for i, j in joined])  9 us
    pallas_call x1, Pallas kernels, first_pair(): pl.pallas_call(functools.partial(first_pair_kernel, count), out_shape=(ja...  8.62 us
    pallas_call x1, Pallas kernels, last_pair(): pl.pallas_call(functools.partial(last_pair_kernel, count), out_shape=(jax...  4.36 us
    pallas_call x1, Pallas kernels, first_edges(): pl.pallas_call(functools.partial(first_edges_kernel, count), out_shape=(o...  3.97 us
    pallas_call x1, Pallas kernels, meet(): pl.pallas_call(functools.partial(meet_kernel, count), out_shape=(out, out...  2.4 us
  transfers between devices with their start and end apart: 4, of which 1 were waited for; matrix products, arithmetic and copies ran while one was open for 0% of the time, Pallas kernels for 12%

profile of v8, /device:TPU:1, one launch (start us, length us, event | category | flops | bytes accessed | tf_op | source)
XLA Modules:
  0.0 109.2 jit_solution(12389709421621190898)
XLA Ops:
  0.0 0.0 copy-start
  0.0 0.0 copy-start.1
  0.0 4.0 %first_edges.1 = (bf16[512,768]{1,0:T(8,128)(2,1)S(1)}, bf16[512,768]{1,0:T(8,128)(2,1)S(1)}, f32[2,512,128]{2,1,0:T(8,128)S(1)}, bf16[2,8,512,512]{3,2,1,0:T(8,128)(2,1)S(1)}) custom-call(bf16[8,512,512]{2,1,0:T(8,128)(2,1)} %bitcast.2, bf16[8,512,512]{2,1,0:T(8,128)(2,1)} %lower.3, bf16[8,512,512]{2,1,0:T(8,128)(2,1)} %upper.3, bf16[8,512,128]{2,1,0:T(8,128)(2,1)} %bitcast.7), custom_call_target="tpu_custom_call" | custom-call | tf_op jit(solution)/shard_map/first_edges/pallas_call | solution.py:119
  4.0 4.9 %collective-permute-start = (bf16[512,768]{1,0:T(8,128)(2,1)S(1)}, bf16[512,768]{1,0:T(8,128)(2,1)S(1)}, u32[]{:S(2)}, u32[]{:S(2)}) collective-permute-start(bf16[512,768]{1,0:T(8,128)(2,1)S(1)} %get-tuple-element.24.cross.cross_joint), channel_id=1, source_target_pairs={{1,2},{3,4},{5,6},{7,8},{9,10},{11,12},{13,14},{15,16},{17,18},{19... | collective-permute-start | bytes 2359304 | tf_op jit(solution)/shard_map/ppermute | solution.py:477
  8.9 0.1 collective-permute-start.1
  9.7 0.0 copy-done
  9.7 0.0 copy-done.1
  9.7 8.6 %first_pair.1 = (bf16[2,8,512,512]{3,2,1,0:T(8,128)(2,1)S(1)}, bf16[4,512,128]{2,1,0:T(8,128)(2,1)S(1)}, f32[4,512,128]{2,1,0:T(8,128)S(1)}, bf16[2,512,128]{2,1,0:T(8,128)(2,1)S(1)}, f32[8,128]{1,0:T(8,128)S(1)}) custom-call(f32[1]{0:T(128)S(6)} %copy.8.weight, bf16[8,512,512]{2,1,0:T(8,128)(2,1)} %lower.3, ...), custom_call_target="tpu_custom_call", output_to_operand_aliasing={{0}: (3, {})} | custom-call | flops 2415919104 | bytes 12582912 | tf_op jit(solution)/shard_map/first_pair/pallas_call | solution.py:197
  18.3 0.3 collective-permute-done.from_cross.from_cross_joint
  18.6 0.0 collective-permute-done.1.from_chip.from_chip_joint
  18.6 2.4 %meet.1 = (bf16[512,256]{1,0:T(8,128)(2,1)S(1)}, bf16[512,256]{1,0:T(8,128)(2,1)S(1)}, f32[2,512,128]{2,1,0:T(8,128)S(1)}, bf16[2,512,128]{2,1,0:T(8,128)(2,1)S(1)}) custom-call(bf16[8,512,512]{2,1,0:T(8,128)(2,1)S(1)} %bitcast.4, bf16[2,8,512,512]{3,2,1,0:T(8,128)(2,1)S(1)} %get-tuple-element.27.coupling, bf16[8,512,128]{2,1,0:T(8,128)(2,1)S(1)} %bitcast.9, ...), custom_call_target="tpu_custom_call" | custom-call | flops 1073741824 | bytes 6291456 | tf_op jit(solution)/shard_map/meet/pallas_call | solution.py:303
  21.0 3.7 %collective-permute-start.2 = (bf16[512,256]{1,0:T(8,128)(2,1)S(1)}, bf16[512,256]{1,0:T(8,128)(2,1)S(1)}, u32[]{:S(2)}, u32[]{:S(2)}) collective-permute-start(bf16[512,256]{1,0:T(8,128)(2,1)S(1)} %get-tuple-element.30.cross), channel_id=1, source_target_pairs={{1,2},{3,4},{5,6},{7,8},{9,10},{11,12},{13,14},{15,16},{17,18},{19... | collective-permute-start | bytes 786440 | tf_op jit(solution)/shard_map/ppermute | solution.py:477
  24.7 0.3 collective-permute-start.3
  25.0 4.4 %last_pair.1 = (bf16[4,512,128]{2,1,0:T(8,128)(2,1)S(1)}, f32[4,512,128]{2,1,0:T(8,128)S(1)}, f32[2,512,128]{2,1,0:T(8,128)S(1)}) custom-call(f32[8,128]{1,0:T(8,128)S(1)} %get-tuple-element.26.weight, bf16[8,512,512]{2,1,0:T(8,128)(2,1)S(1)} %bitcast.5, bf16[2,8,512,512]{3,2,1,0:T(8,128)(2,1)S(1)} %get-tuple-element.27.coupling, ...), custom_call_target="tpu_custom_call" | custom-call | flops 2415919104 | bytes 12582912 | tf_op jit(solution)/shard_map/last_pair/pallas_call | solution.py:239
  29.3 0.0 collective-permute-done.2.from_cross
  29.3 0.0 collective-permute-done.3.from_chip
  29.4 1.6 %finish.1 = bf16[8,512,128]{2,1,0:T(8,128)(2,1)S(1)} custom-call(f32[8,128]{1,0:T(8,128)S(1)} %get-tuple-element.26.weight, bf16[8,512,512]{2,1,0:T(8,128)(2,1)S(1)} %bitcast.6, bf16[2,8,512,512]{3,2,1,0:T(8,128)(2,1)S(1)} %get-tuple-element.27.coupling, f32[4,512,128]{2,1,0:T(8,128)S(1)} %get-tuple-element.35.known, ...), custom_call_target="tpu_custom_call" | custom-call | flops 805306368 | bytes 6291456 | tf_op jit(solution)/shard_map/finish/pallas_call | solution.py:337
  30.9 22.1 %all_to_all.20.received = bf16[8,512,128]{2,1,0:T(8,128)(2,1)S(1)} all-to-all(bf16[8,512,128]{2,1,0:T(8,128)(2,1)S(1)} %finish.1), channel_id=1, replica_groups=mesh['x_hi'=2,'y'=4,'x_lo'=2,'z'=8,'core'=2] {'x_hi','y'}, dimensions={0} | all-to-all | bytes 2097152 | tf_op jit(solution)/shard_map/all_to_all | solution.py:483
  53.0 0.5 gram.1
  53.5 16.7 %all_to_all.21 = f32[16,8,128]{2,1,0:T(8,128)S(1)} all-to-all(f32[16,8,128]{2,1,0:T(8,128)S(1)} %get-tuple-element.39), channel_id=1, replica_groups=mesh['x_hi'=2,'y'=4,'x_lo'=2,'z'=8,'core'=2] {'x_hi','y','x_lo'}, dimensions={0} | all-to-all | bytes 131072 | tf_op jit(solution)/shard_map/all_to_all | solution.py:483
  70.3 12.1 %all_to_all.22 = f32[16,8,128]{2,1,0:T(8,128)S(1)} all-to-all(f32[16,8,128]{2,1,0:T(8,128)S(1)} %broadcast_in_dim.4), channel_id=1, replica_groups=mesh['x_hi'=2,'y'=4,'x_lo'=2,'z'=8,'core'=2] {'z','core'}, dimensions={0} | all-to-all | bytes 131072 | tf_op jit(solution)/shard_map/all_to_all | solution.py:483
  82.4 9.4 %all_to_all.23.gram = f32[16,8,128]{2,1,0:T(8,128)S(1)} all-to-all(f32[16,8,128]{2,1,0:T(8,128)S(1)} %broadcast_in_dim.5), channel_id=1, replica_groups=mesh['x_hi'=2,'y'=4,'x_lo'=2,'z'=8,'core'=2] {'x_hi','y','x_lo'}, dimensions={0} | all-to-all | bytes 131072 | tf_op jit(solution)/shard_map/all_to_all | solution.py:483
  91.8 17.4 %orthonormal.1 = f32[512,128]{1,0:T(8,128)} custom-call(f32[16,8,128]{2,1,0:T(8,128)S(1)} %all_to_all.23.gram, f32[512,128]{1,0:T(8,128)S(1)} %get-tuple-element.40.filtered), custom_call_target="tpu_custom_call" | custom-call | tf_op jit(solution)/shard_map/orthonormal/pallas_call | solution.py:455
  (4 shorter events, 0.1 us)
Async XLA Ops:
  0.0 9.7 %copy-start = (bf16[1,8,512,512]{3,2,1,0:T(8,128)(2,1)S(1)}, bf16[1,8,512,512]{3,2,1,0:T(8,128)(2,1)}, u32[]{:S(2)}) copy-start(bf16[1,8,512,512]{3,2,1,0:T(8,128)(2,1)} %param.6) | copy-start | bytes 12582916
  0.0 9.7 %copy-start.1 = (bf16[4096,128]{1,0:T(8,128)(2,1)S(1)}, bf16[4096,128]{1,0:T(8,128)(2,1)}, u32[]{:S(2)}) copy-start(bf16[4096,128]{1,0:T(8,128)(2,1)} %param.5) | copy-start | bytes 3145732
  4.0 14.6 %collective-permute-start = (bf16[512,768]{1,0:T(8,128)(2,1)S(1)}, bf16[512,768]{1,0:T(8,128)(2,1)S(1)}, u32[]{:S(2)}, u32[]{:S(2)}) collective-permute-start(bf16[512,768]{1,0:T(8,128)(2,1)S(1)} %get-tuple-element.24.cross.cross_joint), channel_id=1, source_target_pairs={{1,2},{3,4},{5,6},{7,8},{9,10},{11,12},{13,14},{15,16},{17,18},{19... | collective-permute-start | bytes 2359304 | tf_op jit(solution)/shard_map/ppermute | solution.py:477
  8.9 9.7 %collective-permute-start.1 = (bf16[512,768]{1,0:T(8,128)(2,1)S(1)}, bf16[512,768]{1,0:T(8,128)(2,1)S(1)}, u32[]{:S(2)}, u32[]{:S(2)}) collective-permute-start(bf16[512,768]{1,0:T(8,128)(2,1)S(1)} %get-tuple-element.25.chip.chip_joint), channel_id=1, source_target_pairs={{0,1},{2,3},{4,5},{6,7},{8,9},{10,11},{12,13},{14,15},{16,17},{18,... | collective-permute-start | bytes 2359304 | tf_op jit(solution)/shard_map/ppermute | solution.py:477
  21.0 8.3 %collective-permute-start.2 = (bf16[512,256]{1,0:T(8,128)(2,1)S(1)}, bf16[512,256]{1,0:T(8,128)(2,1)S(1)}, u32[]{:S(2)}, u32[]{:S(2)}) collective-permute-start(bf16[512,256]{1,0:T(8,128)(2,1)S(1)} %get-tuple-element.30.cross), channel_id=1, source_target_pairs={{1,2},{3,4},{5,6},{7,8},{9,10},{11,12},{13,14},{15,16},{17,18},{19... | collective-permute-start | bytes 786440 | tf_op jit(solution)/shard_map/ppermute | solution.py:477
  24.7 4.7 %collective-permute-start.3 = (bf16[512,256]{1,0:T(8,128)(2,1)S(1)}, bf16[512,256]{1,0:T(8,128)(2,1)S(1)}, u32[]{:S(2)}, u32[]{:S(2)}) collective-permute-start(bf16[512,256]{1,0:T(8,128)(2,1)S(1)} %get-tuple-element.31.chip), channel_id=1, source_target_pairs={{0,1},{2,3},{4,5},{6,7},{8,9},{10,11},{12,13},{14,15},{16,17},{18,... | collective-permute-start | bytes 786440 | tf_op jit(solution)/shard_map/ppermute | solution.py:477

commit v9 on v8

--- a/solution.py
+++ b/solution.py
@@ -465,8 +465,8 @@
 
 POLE = ("x_hi", "y")
 ROW = ("x_lo", "z", "core")
-PLANE = ("x_hi", "y", "x_lo")
-LINE = ("z", "core")
+PLANE = ("y", "x_lo", "core")
+LINE = ("x_hi", "z")
 
 
 def swapped(cross, chip):

time: 109 us -> 110 us (level)
  no operation moved by 1% of the time
where the time goes in v9:
time: 110 us; the launch traced here: 109 us
  blocking collectives  60.5 us (55%)
  Pallas kernels  38.8 us (35%)
  starting transfers between devices  9 us (8%)
    all_to_all x4, blocking collectives, exchange(): return lax.all_to_all(value, axes, split_axis=0, concat_axis=0, tiled=True)  60.5 us
    pallas_call x1, Pallas kernels, orthonormal(): pl.pallas_call(functools.partial(orthonormal_kernel, float(total_rows)),...  17.4 us
    ppermute x4, starting transfers between devices, swapped(): lax.ppermute(value, ROW, joined + [(j, i) for i, j in joined])  9 us
    pallas_call x1, Pallas kernels, first_pair(): pl.pallas_call(functools.partial(first_pair_kernel, count), out_shape=(ja...  8.62 us
    pallas_call x1, Pallas kernels, last_pair(): pl.pallas_call(functools.partial(last_pair_kernel, count), out_shape=(jax...  4.36 us
    pallas_call x1, Pallas kernels, first_edges(): pl.pallas_call(functools.partial(first_edges_kernel, count), out_shape=(o...  3.97 us
    pallas_call x1, Pallas kernels, meet(): pl.pallas_call(functools.partial(meet_kernel, count), out_shape=(out, out...  2.4 us
  transfers between devices with their start and end apart: 4, of which 1 were waited for; matrix products, arithmetic and copies ran while one was open for 0% of the time, Pallas kernels for 12%

profile of v9, /device:TPU:1, one launch (start us, length us, event | category | flops | bytes accessed | tf_op | source)
XLA Modules:
  0.0 109.4 jit_solution(8287574981843663857)
XLA Ops:
  0.0 0.0 copy-start
  0.0 0.0 copy-start.1
  0.0 4.0 %first_edges.1 = (bf16[512,768]{1,0:T(8,128)(2,1)S(1)}, bf16[512,768]{1,0:T(8,128)(2,1)S(1)}, f32[2,512,128]{2,1,0:T(8,128)S(1)}, bf16[2,8,512,512]{3,2,1,0:T(8,128)(2,1)S(1)}) custom-call(bf16[8,512,512]{2,1,0:T(8,128)(2,1)} %bitcast.2, bf16[8,512,512]{2,1,0:T(8,128)(2,1)} %lower.3, bf16[8,512,512]{2,1,0:T(8,128)(2,1)} %upper.3, bf16[8,512,128]{2,1,0:T(8,128)(2,1)} %bitcast.7), custom_call_target="tpu_custom_call" | custom-call | tf_op jit(solution)/shard_map/first_edges/pallas_call | solution.py:119
  4.0 4.9 %collective-permute-start = (bf16[512,768]{1,0:T(8,128)(2,1)S(1)}, bf16[512,768]{1,0:T(8,128)(2,1)S(1)}, u32[]{:S(2)}, u32[]{:S(2)}) collective-permute-start(bf16[512,768]{1,0:T(8,128)(2,1)S(1)} %get-tuple-element.24.cross.cross_joint), channel_id=1, source_target_pairs={{1,2},{3,4},{5,6},{7,8},{9,10},{11,12},{13,14},{15,16},{17,18},{19... | collective-permute-start | bytes 2359304 | tf_op jit(solution)/shard_map/ppermute | solution.py:477
  8.9 0.1 collective-permute-start.1
  9.7 0.0 copy-done
  9.7 0.0 copy-done.1
  9.7 8.6 %first_pair.1 = (bf16[2,8,512,512]{3,2,1,0:T(8,128)(2,1)S(1)}, bf16[4,512,128]{2,1,0:T(8,128)(2,1)S(1)}, f32[4,512,128]{2,1,0:T(8,128)S(1)}, bf16[2,512,128]{2,1,0:T(8,128)(2,1)S(1)}, f32[8,128]{1,0:T(8,128)S(1)}) custom-call(f32[1]{0:T(128)S(6)} %copy.8.weight, bf16[8,512,512]{2,1,0:T(8,128)(2,1)} %lower.3, ...), custom_call_target="tpu_custom_call", output_to_operand_aliasing={{0}: (3, {})} | custom-call | flops 2415919104 | bytes 12582912 | tf_op jit(solution)/shard_map/first_pair/pallas_call | solution.py:197
  18.3 0.3 collective-permute-done.from_cross.from_cross_joint
  18.6 0.0 collective-permute-done.1.from_chip.from_chip_joint
  18.6 2.4 %meet.1 = (bf16[512,256]{1,0:T(8,128)(2,1)S(1)}, bf16[512,256]{1,0:T(8,128)(2,1)S(1)}, f32[2,512,128]{2,1,0:T(8,128)S(1)}, bf16[2,512,128]{2,1,0:T(8,128)(2,1)S(1)}) custom-call(bf16[8,512,512]{2,1,0:T(8,128)(2,1)S(1)} %bitcast.4, bf16[2,8,512,512]{3,2,1,0:T(8,128)(2,1)S(1)} %get-tuple-element.27.coupling, bf16[8,512,128]{2,1,0:T(8,128)(2,1)S(1)} %bitcast.9, ...), custom_call_target="tpu_custom_call" | custom-call | flops 1073741824 | bytes 6291456 | tf_op jit(solution)/shard_map/meet/pallas_call | solution.py:303
  21.0 3.7 %collective-permute-start.2 = (bf16[512,256]{1,0:T(8,128)(2,1)S(1)}, bf16[512,256]{1,0:T(8,128)(2,1)S(1)}, u32[]{:S(2)}, u32[]{:S(2)}) collective-permute-start(bf16[512,256]{1,0:T(8,128)(2,1)S(1)} %get-tuple-element.30.cross), channel_id=1, source_target_pairs={{1,2},{3,4},{5,6},{7,8},{9,10},{11,12},{13,14},{15,16},{17,18},{19... | collective-permute-start | bytes 786440 | tf_op jit(solution)/shard_map/ppermute | solution.py:477
  24.7 0.3 collective-permute-start.3
  25.0 4.4 %last_pair.1 = (bf16[4,512,128]{2,1,0:T(8,128)(2,1)S(1)}, f32[4,512,128]{2,1,0:T(8,128)S(1)}, f32[2,512,128]{2,1,0:T(8,128)S(1)}) custom-call(f32[8,128]{1,0:T(8,128)S(1)} %get-tuple-element.26.weight, bf16[8,512,512]{2,1,0:T(8,128)(2,1)S(1)} %bitcast.5, bf16[2,8,512,512]{3,2,1,0:T(8,128)(2,1)S(1)} %get-tuple-element.27.coupling, ...), custom_call_target="tpu_custom_call" | custom-call | flops 2415919104 | bytes 12582912 | tf_op jit(solution)/shard_map/last_pair/pallas_call | solution.py:239
  29.3 0.0 collective-permute-done.2.from_cross
  29.3 0.0 collective-permute-done.3.from_chip
  29.4 1.6 %finish.1 = bf16[8,512,128]{2,1,0:T(8,128)(2,1)S(1)} custom-call(f32[8,128]{1,0:T(8,128)S(1)} %get-tuple-element.26.weight, bf16[8,512,512]{2,1,0:T(8,128)(2,1)S(1)} %bitcast.6, bf16[2,8,512,512]{3,2,1,0:T(8,128)(2,1)S(1)} %get-tuple-element.27.coupling, f32[4,512,128]{2,1,0:T(8,128)S(1)} %get-tuple-element.35.known, ...), custom_call_target="tpu_custom_call" | custom-call | flops 805306368 | bytes 6291456 | tf_op jit(solution)/shard_map/finish/pallas_call | solution.py:337
  30.9 22.1 %all_to_all.20.received = bf16[8,512,128]{2,1,0:T(8,128)(2,1)S(1)} all-to-all(bf16[8,512,128]{2,1,0:T(8,128)(2,1)S(1)} %finish.1), channel_id=1, replica_groups=mesh['x_hi'=2,'y'=4,'x_lo'=2,'z'=8,'core'=2] {'x_hi','y'}, dimensions={0} | all-to-all | bytes 2097152 | tf_op jit(solution)/shard_map/all_to_all | solution.py:483
  53.0 0.5 gram.1
  53.5 16.4 %all_to_all.21 = f32[16,8,128]{2,1,0:T(8,128)S(1)} all-to-all(f32[16,8,128]{2,1,0:T(8,128)S(1)} %get-tuple-element.39), channel_id=1, replica_groups=mesh['x_hi'=2,'y'=4,'x_lo'=2,'z'=8,'core'=2] {'y','x_lo','core'}, dimensions={0} | all-to-all | bytes 131072 | tf_op jit(solution)/shard_map/all_to_all | solution.py:483
  69.9 11.9 %all_to_all.22 = f32[16,8,128]{2,1,0:T(8,128)S(1)} all-to-all(f32[16,8,128]{2,1,0:T(8,128)S(1)} %broadcast_in_dim.4), channel_id=1, replica_groups=mesh['x_hi'=2,'y'=4,'x_lo'=2,'z'=8,'core'=2] {'x_hi','z'}, dimensions={0} | all-to-all | bytes 131072 | tf_op jit(solution)/shard_map/all_to_all | solution.py:483
  81.8 10.1 %all_to_all.23.gram = f32[16,8,128]{2,1,0:T(8,128)S(1)} all-to-all(f32[16,8,128]{2,1,0:T(8,128)S(1)} %broadcast_in_dim.5), channel_id=1, replica_groups=mesh['x_hi'=2,'y'=4,'x_lo'=2,'z'=8,'core'=2] {'y','x_lo','core'}, dimensions={0} | all-to-all | bytes 131072 | tf_op jit(solution)/shard_map/all_to_all | solution.py:483
  92.0 17.4 %orthonormal.1 = f32[512,128]{1,0:T(8,128)} custom-call(f32[16,8,128]{2,1,0:T(8,128)S(1)} %all_to_all.23.gram, f32[512,128]{1,0:T(8,128)S(1)} %get-tuple-element.40.filtered), custom_call_target="tpu_custom_call" | custom-call | tf_op jit(solution)/shard_map/orthonormal/pallas_call | solution.py:455
  (4 shorter events, 0.1 us)
Async XLA Ops:
  0.0 9.7 %copy-start = (bf16[1,8,512,512]{3,2,1,0:T(8,128)(2,1)S(1)}, bf16[1,8,512,512]{3,2,1,0:T(8,128)(2,1)}, u32[]{:S(2)}) copy-start(bf16[1,8,512,512]{3,2,1,0:T(8,128)(2,1)} %param.6) | copy-start | bytes 12582916
  0.0 9.7 %copy-start.1 = (bf16[4096,128]{1,0:T(8,128)(2,1)S(1)}, bf16[4096,128]{1,0:T(8,128)(2,1)}, u32[]{:S(2)}) copy-start(bf16[4096,128]{1,0:T(8,128)(2,1)} %param.5) | copy-start | bytes 3145732
  4.0 14.6 %collective-permute-start = (bf16[512,768]{1,0:T(8,128)(2,1)S(1)}, bf16[512,768]{1,0:T(8,128)(2,1)S(1)}, u32[]{:S(2)}, u32[]{:S(2)}) collective-permute-start(bf16[512,768]{1,0:T(8,128)(2,1)S(1)} %get-tuple-element.24.cross.cross_joint), channel_id=1, source_target_pairs={{1,2},{3,4},{5,6},{7,8},{9,10},{11,12},{13,14},{15,16},{17,18},{19... | collective-permute-start | bytes 2359304 | tf_op jit(solution)/shard_map/ppermute | solution.py:477
  8.9 9.7 %collective-permute-start.1 = (bf16[512,768]{1,0:T(8,128)(2,1)S(1)}, bf16[512,768]{1,0:T(8,128)(2,1)S(1)}, u32[]{:S(2)}, u32[]{:S(2)}) collective-permute-start(bf16[512,768]{1,0:T(8,128)(2,1)S(1)} %get-tuple-element.25.chip.chip_joint), channel_id=1, source_target_pairs={{0,1},{2,3},{4,5},{6,7},{8,9},{10,11},{12,13},{14,15},{16,17},{18,... | collective-permute-start | bytes 2359304 | tf_op jit(solution)/shard_map/ppermute | solution.py:477
  21.0 8.3 %collective-permute-start.2 = (bf16[512,256]{1,0:T(8,128)(2,1)S(1)}, bf16[512,256]{1,0:T(8,128)(2,1)S(1)}, u32[]{:S(2)}, u32[]{:S(2)}) collective-permute-start(bf16[512,256]{1,0:T(8,128)(2,1)S(1)} %get-tuple-element.30.cross), channel_id=1, source_target_pairs={{1,2},{3,4},{5,6},{7,8},{9,10},{11,12},{13,14},{15,16},{17,18},{19... | collective-permute-start | bytes 786440 | tf_op jit(solution)/shard_map/ppermute | solution.py:477
  24.7 4.7 %collective-permute-start.3 = (bf16[512,256]{1,0:T(8,128)(2,1)S(1)}, bf16[512,256]{1,0:T(8,128)(2,1)S(1)}, u32[]{:S(2)}, u32[]{:S(2)}) collective-permute-start(bf16[512,256]{1,0:T(8,128)(2,1)S(1)} %get-tuple-element.31.chip), channel_id=1, source_target_pairs={{0,1},{2,3},{4,5},{6,7},{8,9},{10,11},{12,13},{14,15},{16,17},{18,... | collective-permute-start | bytes 786440 | tf_op jit(solution)/shard_map/ppermute | solution.py:477

commit v10 on v9

--- a/solution.py
+++ b/solution.py
@@ -396,13 +396,13 @@
     inverse[...] = work[:, n:]
 
 
-def split_product(a, b):
+def split_product(a, b, axis=0):
     a_high, b_high = rounded(a), rounded(b)
     a_low = rounded(a - a_high.astype(F32))
     b_low = rounded(b - b_high.astype(F32))
     left = jnp.concatenate([a_high, a_low], axis=1)
-    right = jnp.concatenate([b_high, b_high], axis=1)
-    over = (((1,), (1,)), ((), ()))
+    right = jnp.concatenate([b_high, b_high], axis=axis)
+    over = (((1,), (axis,)), ((), ()))
     return lax.dot_general(left, right, over, preferred_element_type=F32) + lax.dot_general(
         a_high, b_low, over, preferred_element_type=F32
     )
@@ -418,9 +418,6 @@
     def phi(x):
         return jnp.where(rows > cols, x, jnp.where(same, 0.5 * x, 0.0))
 
-    def exact(a, b):
-        return jnp.dot(a, b, precision=HI, preferred_element_type=F32)
-
     def short(a, b):
         return dot(rounded(a), rounded(b))
 
@@ -430,14 +427,14 @@
     excess = jnp.where(same, 0.0, value * across * down)
     first = jnp.where(rows > cols, excess, 0.0)
     first_t = excess - first
-    product = exact(first, excess)
-    second_excess = -product - exact(first_t - product, first_t)
+    product = split_product(first, excess)
+    second_excess = -product - split_product(first_t - product, first_t)
     second = phi(second_excess)
     second_t = second_excess - second
     product = short(second, second_excess)
     third_excess = -product - short(second_t - product, second_t)
     third = phi(third_excess)
-    factor = exact(second, first) - first - second
+    factor = split_product(second, first) - first - second
     factor = jnp.where(same, 1.0 + factor, factor)
     factor = factor - short(third, factor)
     inverse[...] = factor * across
@@ -447,7 +444,7 @@
     def _():
         eliminate(value, work, inverse)
 
-    out[...] = split_product(filtered[...], inverse[...])
+    out[...] = split_product(filtered[...], inverse[...], 1)
 
 
 def orthonormal(gram, filtered, total_rows):

time: 110 us -> 110 us (level)
  no operation moved by 1% of the time
where the time goes in v10:
time: 110 us; the launch traced here: 109 us
  blocking collectives  60.5 us (55%)
  Pallas kernels  38.7 us (35%)
  starting transfers between devices  9 us (8%)
    all_to_all x4, blocking collectives, exchange(): return lax.all_to_all(value, axes, split_axis=0, concat_axis=0, tiled=True)  60.5 us
    pallas_call x1, Pallas kernels, orthonormal(): pl.pallas_call(functools.partial(orthonormal_kernel, float(total_rows)),...  17.4 us
    ppermute x4, starting transfers between devices, swapped(): lax.ppermute(value, ROW, joined + [(j, i) for i, j in joined])  9 us
    pallas_call x1, Pallas kernels, first_pair(): pl.pallas_call(functools.partial(first_pair_kernel, count), out_shape=(ja...  8.62 us
    pallas_call x1, Pallas kernels, last_pair(): pl.pallas_call(functools.partial(last_pair_kernel, count), out_shape=(jax...  4.36 us
    pallas_call x1, Pallas kernels, first_edges(): pl.pallas_call(functools.partial(first_edges_kernel, count), out_shape=(o...  3.97 us
    pallas_call x1, Pallas kernels, meet(): pl.pallas_call(functools.partial(meet_kernel, count), out_shape=(out, out...  2.4 us
  transfers between devices with their start and end apart: 4, of which 1 were waited for; matrix products, arithmetic and copies ran while one was open for 0% of the time, Pallas kernels for 12%

profile of v10, /device:TPU:1, one launch (start us, length us, event | category | flops | bytes accessed | tf_op | source)
XLA Modules:
  0.0 109.3 jit_solution(11488483428686147117)
XLA Ops:
  0.0 0.0 copy-start
  0.0 0.0 copy-start.1
  0.0 4.0 %first_edges.1 = (bf16[512,768]{1,0:T(8,128)(2,1)S(1)}, bf16[512,768]{1,0:T(8,128)(2,1)S(1)}, f32[2,512,128]{2,1,0:T(8,128)S(1)}, bf16[2,8,512,512]{3,2,1,0:T(8,128)(2,1)S(1)}) custom-call(bf16[8,512,512]{2,1,0:T(8,128)(2,1)} %bitcast.2, bf16[8,512,512]{2,1,0:T(8,128)(2,1)} %lower.3, bf16[8,512,512]{2,1,0:T(8,128)(2,1)} %upper.3, bf16[8,512,128]{2,1,0:T(8,128)(2,1)} %bitcast.7), custom_call_target="tpu_custom_call" | custom-call | tf_op jit(solution)/shard_map/first_edges/pallas_call | solution.py:119
  4.0 4.9 %collective-permute-start = (bf16[512,768]{1,0:T(8,128)(2,1)S(1)}, bf16[512,768]{1,0:T(8,128)(2,1)S(1)}, u32[]{:S(2)}, u32[]{:S(2)}) collective-permute-start(bf16[512,768]{1,0:T(8,128)(2,1)S(1)} %get-tuple-element.24.cross.cross_joint), channel_id=1, source_target_pairs={{1,2},{3,4},{5,6},{7,8},{9,10},{11,12},{13,14},{15,16},{17,18},{19... | collective-permute-start | bytes 2359304 | tf_op jit(solution)/shard_map/ppermute | solution.py:474
  8.9 0.1 collective-permute-start.1
  9.7 0.0 copy-done
  9.7 0.0 copy-done.1
  9.7 8.6 %first_pair.1 = (bf16[2,8,512,512]{3,2,1,0:T(8,128)(2,1)S(1)}, bf16[4,512,128]{2,1,0:T(8,128)(2,1)S(1)}, f32[4,512,128]{2,1,0:T(8,128)S(1)}, bf16[2,512,128]{2,1,0:T(8,128)(2,1)S(1)}, f32[8,128]{1,0:T(8,128)S(1)}) custom-call(f32[1]{0:T(128)S(6)} %copy.8.weight, bf16[8,512,512]{2,1,0:T(8,128)(2,1)} %lower.3, ...), custom_call_target="tpu_custom_call", output_to_operand_aliasing={{0}: (3, {})} | custom-call | flops 2415919104 | bytes 12582912 | tf_op jit(solution)/shard_map/first_pair/pallas_call | solution.py:197
  18.3 0.3 collective-permute-done.from_cross.from_cross_joint
  18.6 0.0 collective-permute-done.1.from_chip.from_chip_joint
  18.6 2.4 %meet.1 = (bf16[512,256]{1,0:T(8,128)(2,1)S(1)}, bf16[512,256]{1,0:T(8,128)(2,1)S(1)}, f32[2,512,128]{2,1,0:T(8,128)S(1)}, bf16[2,512,128]{2,1,0:T(8,128)(2,1)S(1)}) custom-call(bf16[8,512,512]{2,1,0:T(8,128)(2,1)S(1)} %bitcast.4, bf16[2,8,512,512]{3,2,1,0:T(8,128)(2,1)S(1)} %get-tuple-element.27.coupling, bf16[8,512,128]{2,1,0:T(8,128)(2,1)S(1)} %bitcast.9, ...), custom_call_target="tpu_custom_call" | custom-call | flops 1073741824 | bytes 6291456 | tf_op jit(solution)/shard_map/meet/pallas_call | solution.py:303
  21.0 3.7 %collective-permute-start.2 = (bf16[512,256]{1,0:T(8,128)(2,1)S(1)}, bf16[512,256]{1,0:T(8,128)(2,1)S(1)}, u32[]{:S(2)}, u32[]{:S(2)}) collective-permute-start(bf16[512,256]{1,0:T(8,128)(2,1)S(1)} %get-tuple-element.30.cross), channel_id=1, source_target_pairs={{1,2},{3,4},{5,6},{7,8},{9,10},{11,12},{13,14},{15,16},{17,18},{19... | collective-permute-start | bytes 786440 | tf_op jit(solution)/shard_map/ppermute | solution.py:474
  24.7 0.3 collective-permute-start.3
  25.0 4.4 %last_pair.1 = (bf16[4,512,128]{2,1,0:T(8,128)(2,1)S(1)}, f32[4,512,128]{2,1,0:T(8,128)S(1)}, f32[2,512,128]{2,1,0:T(8,128)S(1)}) custom-call(f32[8,128]{1,0:T(8,128)S(1)} %get-tuple-element.26.weight, bf16[8,512,512]{2,1,0:T(8,128)(2,1)S(1)} %bitcast.5, bf16[2,8,512,512]{3,2,1,0:T(8,128)(2,1)S(1)} %get-tuple-element.27.coupling, ...), custom_call_target="tpu_custom_call" | custom-call | flops 2415919104 | bytes 12582912 | tf_op jit(solution)/shard_map/last_pair/pallas_call | solution.py:239
  29.3 0.0 collective-permute-done.2.from_cross
  29.3 0.0 collective-permute-done.3.from_chip
  29.4 1.6 %finish.1 = bf16[8,512,128]{2,1,0:T(8,128)(2,1)S(1)} custom-call(f32[8,128]{1,0:T(8,128)S(1)} %get-tuple-element.26.weight, bf16[8,512,512]{2,1,0:T(8,128)(2,1)S(1)} %bitcast.6, bf16[2,8,512,512]{3,2,1,0:T(8,128)(2,1)S(1)} %get-tuple-element.27.coupling, f32[4,512,128]{2,1,0:T(8,128)S(1)} %get-tuple-element.35.known, ...), custom_call_target="tpu_custom_call" | custom-call | flops 805306368 | bytes 6291456 | tf_op jit(solution)/shard_map/finish/pallas_call | solution.py:337
  30.9 22.1 %all_to_all.20.received = bf16[8,512,128]{2,1,0:T(8,128)(2,1)S(1)} all-to-all(bf16[8,512,128]{2,1,0:T(8,128)(2,1)S(1)} %finish.1), channel_id=1, replica_groups=mesh['x_hi'=2,'y'=4,'x_lo'=2,'z'=8,'core'=2] {'x_hi','y'}, dimensions={0} | all-to-all | bytes 2097152 | tf_op jit(solution)/shard_map/all_to_all | solution.py:480
  53.0 0.5 gram.1
  53.5 16.4 %all_to_all.21 = f32[16,8,128]{2,1,0:T(8,128)S(1)} all-to-all(f32[16,8,128]{2,1,0:T(8,128)S(1)} %get-tuple-element.39), channel_id=1, replica_groups=mesh['x_hi'=2,'y'=4,'x_lo'=2,'z'=8,'core'=2] {'y','x_lo','core'}, dimensions={0} | all-to-all | bytes 131072 | tf_op jit(solution)/shard_map/all_to_all | solution.py:480
  69.9 11.9 %all_to_all.22 = f32[16,8,128]{2,1,0:T(8,128)S(1)} all-to-all(f32[16,8,128]{2,1,0:T(8,128)S(1)} %broadcast_in_dim.4), channel_id=1, replica_groups=mesh['x_hi'=2,'y'=4,'x_lo'=2,'z'=8,'core'=2] {'x_hi','z'}, dimensions={0} | all-to-all | bytes 131072 | tf_op jit(solution)/shard_map/all_to_all | solution.py:480
  81.8 10.1 %all_to_all.23.gram = f32[16,8,128]{2,1,0:T(8,128)S(1)} all-to-all(f32[16,8,128]{2,1,0:T(8,128)S(1)} %broadcast_in_dim.5), channel_id=1, replica_groups=mesh['x_hi'=2,'y'=4,'x_lo'=2,'z'=8,'core'=2] {'y','x_lo','core'}, dimensions={0} | all-to-all | bytes 131072 | tf_op jit(solution)/shard_map/all_to_all | solution.py:480
  92.0 17.4 %orthonormal.1 = f32[512,128]{1,0:T(8,128)} custom-call(f32[16,8,128]{2,1,0:T(8,128)S(1)} %all_to_all.23.gram, f32[512,128]{1,0:T(8,128)S(1)} %get-tuple-element.40.filtered), custom_call_target="tpu_custom_call" | custom-call | tf_op jit(solution)/shard_map/orthonormal/pallas_call | solution.py:452
  (4 shorter events, 0.1 us)
Async XLA Ops:
  0.0 9.7 %copy-start = (bf16[1,8,512,512]{3,2,1,0:T(8,128)(2,1)S(1)}, bf16[1,8,512,512]{3,2,1,0:T(8,128)(2,1)}, u32[]{:S(2)}) copy-start(bf16[1,8,512,512]{3,2,1,0:T(8,128)(2,1)} %param.6) | copy-start | bytes 12582916
  0.0 9.7 %copy-start.1 = (bf16[4096,128]{1,0:T(8,128)(2,1)S(1)}, bf16[4096,128]{1,0:T(8,128)(2,1)}, u32[]{:S(2)}) copy-start(bf16[4096,128]{1,0:T(8,128)(2,1)} %param.5) | copy-start | bytes 3145732
  4.0 14.6 %collective-permute-start = (bf16[512,768]{1,0:T(8,128)(2,1)S(1)}, bf16[512,768]{1,0:T(8,128)(2,1)S(1)}, u32[]{:S(2)}, u32[]{:S(2)}) collective-permute-start(bf16[512,768]{1,0:T(8,128)(2,1)S(1)} %get-tuple-element.24.cross.cross_joint), channel_id=1, source_target_pairs={{1,2},{3,4},{5,6},{7,8},{9,10},{11,12},{13,14},{15,16},{17,18},{19... | collective-permute-start | bytes 2359304 | tf_op jit(solution)/shard_map/ppermute | solution.py:474
  8.9 9.7 %collective-permute-start.1 = (bf16[512,768]{1,0:T(8,128)(2,1)S(1)}, bf16[512,768]{1,0:T(8,128)(2,1)S(1)}, u32[]{:S(2)}, u32[]{:S(2)}) collective-permute-start(bf16[512,768]{1,0:T(8,128)(2,1)S(1)} %get-tuple-element.25.chip.chip_joint), channel_id=1, source_target_pairs={{0,1},{2,3},{4,5},{6,7},{8,9},{10,11},{12,13},{14,15},{16,17},{18,... | collective-permute-start | bytes 2359304 | tf_op jit(solution)/shard_map/ppermute | solution.py:474
  21.0 8.3 %collective-permute-start.2 = (bf16[512,256]{1,0:T(8,128)(2,1)S(1)}, bf16[512,256]{1,0:T(8,128)(2,1)S(1)}, u32[]{:S(2)}, u32[]{:S(2)}) collective-permute-start(bf16[512,256]{1,0:T(8,128)(2,1)S(1)} %get-tuple-element.30.cross), channel_id=1, source_target_pairs={{1,2},{3,4},{5,6},{7,8},{9,10},{11,12},{13,14},{15,16},{17,18},{19... | collective-permute-start | bytes 786440 | tf_op jit(solution)/shard_map/ppermute | solution.py:474
  24.7 4.7 %collective-permute-start.3 = (bf16[512,256]{1,0:T(8,128)(2,1)S(1)}, bf16[512,256]{1,0:T(8,128)(2,1)S(1)}, u32[]{:S(2)}, u32[]{:S(2)}) collective-permute-start(bf16[512,256]{1,0:T(8,128)(2,1)S(1)} %get-tuple-element.31.chip), channel_id=1, source_target_pairs={{0,1},{2,3},{4,5},{6,7},{8,9},{10,11},{12,13},{14,15},{16,17},{18,... | collective-permute-start | bytes 786440 | tf_op jit(solution)/shard_map/ppermute | solution.py:474

commit v11 on v8

--- a/solution.py
+++ b/solution.py
@@ -141,7 +141,8 @@
 
 
 def right_side(b, coupling, base, left, right):
-    value = dot(coupling[0, b], left) + dot(coupling[1, b], right)
+    both = jnp.concatenate([coupling[0, b], coupling[1, b]], axis=1)
+    value = dot(both, jnp.concatenate([left, right], axis=0))
     return rounded(base[b].astype(F32) + value)
 
 

time: 109 us -> 109 us (level)
  no operation moved by 1% of the time
where the time goes in v11:
time: 109 us
  blocking collectives  60.4 us (55%)
  Pallas kernels  38.7 us (36%)
  starting transfers between devices  8.94 us (8%)
    all_to_all x4, blocking collectives, exchange(): return lax.all_to_all(value, axes, split_axis=0, concat_axis=0, tiled=True)  60.4 us
    pallas_call x1, Pallas kernels, orthonormal(): pl.pallas_call(functools.partial(orthonormal_kernel, float(total_rows)),...  17.4 us
    ppermute x4, starting transfers between devices, swapped(): lax.ppermute(value, ROW, joined + [(j, i) for i, j in joined])  8.94 us
    pallas_call x1, Pallas kernels, first_pair(): pl.pallas_call(functools.partial(first_pair_kernel, count), out_shape=(ja...  8.5 us
    pallas_call x1, Pallas kernels, last_pair(): pl.pallas_call(functools.partial(last_pair_kernel, count), out_shape=(jax...  4.36 us
    pallas_call x1, Pallas kernels, first_edges(): pl.pallas_call(functools.partial(first_edges_kernel, count), out_shape=(o...  3.97 us
    pallas_call x1, Pallas kernels, meet(): pl.pallas_call(functools.partial(meet_kernel, count), out_shape=(out, out...  2.4 us
  transfers between devices with their start and end apart: 4, of which 1 were waited for; matrix products, arithmetic and copies ran while one was open for 0% of the time, Pallas kernels for 12%

profile of v11, /device:TPU:1, one launch (start us, length us, event | category | flops | bytes accessed | tf_op | source)
XLA Modules:
  0.0 109.2 jit_solution(17524683206544965068)
XLA Ops:
  0.0 0.0 copy-start
  0.0 0.0 copy-start.1
  0.0 4.0 %first_edges.1 = (bf16[512,768]{1,0:T(8,128)(2,1)S(1)}, bf16[512,768]{1,0:T(8,128)(2,1)S(1)}, f32[2,512,128]{2,1,0:T(8,128)S(1)}, bf16[2,8,512,512]{3,2,1,0:T(8,128)(2,1)S(1)}) custom-call(bf16[8,512,512]{2,1,0:T(8,128)(2,1)} %bitcast.2, bf16[8,512,512]{2,1,0:T(8,128)(2,1)} %lower.3, bf16[8,512,512]{2,1,0:T(8,128)(2,1)} %upper.3, bf16[8,512,128]{2,1,0:T(8,128)(2,1)} %bitcast.7), custom_call_target="tpu_custom_call" | custom-call | tf_op jit(solution)/shard_map/first_edges/pallas_call | solution.py:119
  4.0 4.9 %collective-permute-start = (bf16[512,768]{1,0:T(8,128)(2,1)S(1)}, bf16[512,768]{1,0:T(8,128)(2,1)S(1)}, u32[]{:S(2)}, u32[]{:S(2)}) collective-permute-start(bf16[512,768]{1,0:T(8,128)(2,1)S(1)} %get-tuple-element.24.cross.cross_joint), channel_id=1, source_target_pairs={{1,2},{3,4},{5,6},{7,8},{9,10},{11,12},{13,14},{15,16},{17,18},{19... | collective-permute-start | bytes 2359304 | tf_op jit(solution)/shard_map/ppermute | solution.py:478
  8.9 0.1 collective-permute-start.1
  9.7 0.0 copy-done
  9.7 0.0 copy-done.1
  9.7 8.5 %first_pair.1 = (bf16[2,8,512,512]{3,2,1,0:T(8,128)(2,1)S(1)}, bf16[4,512,128]{2,1,0:T(8,128)(2,1)S(1)}, f32[4,512,128]{2,1,0:T(8,128)S(1)}, bf16[2,512,128]{2,1,0:T(8,128)(2,1)S(1)}, f32[8,128]{1,0:T(8,128)S(1)}) custom-call(f32[1]{0:T(128)S(6)} %copy.8.weight, bf16[8,512,512]{2,1,0:T(8,128)(2,1)} %lower.3, ...), custom_call_target="tpu_custom_call", output_to_operand_aliasing={{0}: (3, {})} | custom-call | flops 2415919104 | bytes 12582912 | tf_op jit(solution)/shard_map/first_pair/pallas_call | solution.py:198
  18.2 0.4 collective-permute-done.from_cross.from_cross_joint
  18.6 0.0 collective-permute-done.1.from_chip.from_chip_joint
  18.6 2.4 %meet.1 = (bf16[512,256]{1,0:T(8,128)(2,1)S(1)}, bf16[512,256]{1,0:T(8,128)(2,1)S(1)}, f32[2,512,128]{2,1,0:T(8,128)S(1)}, bf16[2,512,128]{2,1,0:T(8,128)(2,1)S(1)}) custom-call(bf16[8,512,512]{2,1,0:T(8,128)(2,1)S(1)} %bitcast.4, bf16[2,8,512,512]{3,2,1,0:T(8,128)(2,1)S(1)} %get-tuple-element.27.coupling, bf16[8,512,128]{2,1,0:T(8,128)(2,1)S(1)} %bitcast.9, ...), custom_call_target="tpu_custom_call" | custom-call | flops 1073741824 | bytes 6291456 | tf_op jit(solution)/shard_map/meet/pallas_call | solution.py:304
  21.0 3.6 %collective-permute-start.2 = (bf16[512,256]{1,0:T(8,128)(2,1)S(1)}, bf16[512,256]{1,0:T(8,128)(2,1)S(1)}, u32[]{:S(2)}, u32[]{:S(2)}) collective-permute-start(bf16[512,256]{1,0:T(8,128)(2,1)S(1)} %get-tuple-element.30.cross), channel_id=1, source_target_pairs={{1,2},{3,4},{5,6},{7,8},{9,10},{11,12},{13,14},{15,16},{17,18},{19... | collective-permute-start | bytes 786440 | tf_op jit(solution)/shard_map/ppermute | solution.py:478
  24.6 0.3 collective-permute-start.3
  24.9 4.4 %last_pair.1 = (bf16[4,512,128]{2,1,0:T(8,128)(2,1)S(1)}, f32[4,512,128]{2,1,0:T(8,128)S(1)}, f32[2,512,128]{2,1,0:T(8,128)S(1)}) custom-call(f32[8,128]{1,0:T(8,128)S(1)} %get-tuple-element.26.weight, bf16[8,512,512]{2,1,0:T(8,128)(2,1)S(1)} %bitcast.5, bf16[2,8,512,512]{3,2,1,0:T(8,128)(2,1)S(1)} %get-tuple-element.27.coupling, ...), custom_call_target="tpu_custom_call" | custom-call | flops 2415919104 | bytes 12582912 | tf_op jit(solution)/shard_map/last_pair/pallas_call | solution.py:240
  29.3 0.0 collective-permute-done.2.from_cross
  29.3 0.0 collective-permute-done.3.from_chip
  29.3 1.6 %finish.1 = bf16[8,512,128]{2,1,0:T(8,128)(2,1)S(1)} custom-call(f32[8,128]{1,0:T(8,128)S(1)} %get-tuple-element.26.weight, bf16[8,512,512]{2,1,0:T(8,128)(2,1)S(1)} %bitcast.6, bf16[2,8,512,512]{3,2,1,0:T(8,128)(2,1)S(1)} %get-tuple-element.27.coupling, f32[4,512,128]{2,1,0:T(8,128)S(1)} %get-tuple-element.35.known, ...), custom_call_target="tpu_custom_call" | custom-call | flops 805306368 | bytes 6291456 | tf_op jit(solution)/shard_map/finish/pallas_call | solution.py:338
  30.9 22.1 %all_to_all.20.received = bf16[8,512,128]{2,1,0:T(8,128)(2,1)S(1)} all-to-all(bf16[8,512,128]{2,1,0:T(8,128)(2,1)S(1)} %finish.1), channel_id=1, replica_groups=mesh['x_hi'=2,'y'=4,'x_lo'=2,'z'=8,'core'=2] {'x_hi','y'}, dimensions={0} | all-to-all | bytes 2097152 | tf_op jit(solution)/shard_map/all_to_all | solution.py:484
  53.0 0.5 gram.1
  53.5 16.8 %all_to_all.21 = f32[16,8,128]{2,1,0:T(8,128)S(1)} all-to-all(f32[16,8,128]{2,1,0:T(8,128)S(1)} %get-tuple-element.39), channel_id=1, replica_groups=mesh['x_hi'=2,'y'=4,'x_lo'=2,'z'=8,'core'=2] {'x_hi','y','x_lo'}, dimensions={0} | all-to-all | bytes 131072 | tf_op jit(solution)/shard_map/all_to_all | solution.py:484
  70.3 12.1 %all_to_all.22 = f32[16,8,128]{2,1,0:T(8,128)S(1)} all-to-all(f32[16,8,128]{2,1,0:T(8,128)S(1)} %broadcast_in_dim.4), channel_id=1, replica_groups=mesh['x_hi'=2,'y'=4,'x_lo'=2,'z'=8,'core'=2] {'z','core'}, dimensions={0} | all-to-all | bytes 131072 | tf_op jit(solution)/shard_map/all_to_all | solution.py:484
  82.4 9.4 %all_to_all.23.gram = f32[16,8,128]{2,1,0:T(8,128)S(1)} all-to-all(f32[16,8,128]{2,1,0:T(8,128)S(1)} %broadcast_in_dim.5), channel_id=1, replica_groups=mesh['x_hi'=2,'y'=4,'x_lo'=2,'z'=8,'core'=2] {'x_hi','y','x_lo'}, dimensions={0} | all-to-all | bytes 131072 | tf_op jit(solution)/shard_map/all_to_all | solution.py:484
  91.8 17.4 %orthonormal.1 = f32[512,128]{1,0:T(8,128)} custom-call(f32[16,8,128]{2,1,0:T(8,128)S(1)} %all_to_all.23.gram, f32[512,128]{1,0:T(8,128)S(1)} %get-tuple-element.40.filtered), custom_call_target="tpu_custom_call" | custom-call | tf_op jit(solution)/shard_map/orthonormal/pallas_call | solution.py:456
  (4 shorter events, 0.1 us)
Async XLA Ops:
  0.0 9.7 %copy-start = (bf16[1,8,512,512]{3,2,1,0:T(8,128)(2,1)S(1)}, bf16[1,8,512,512]{3,2,1,0:T(8,128)(2,1)}, u32[]{:S(2)}) copy-start(bf16[1,8,512,512]{3,2,1,0:T(8,128)(2,1)} %param.6) | copy-start | bytes 12582916
  0.0 9.7 %copy-start.1 = (bf16[4096,128]{1,0:T(8,128)(2,1)S(1)}, bf16[4096,128]{1,0:T(8,128)(2,1)}, u32[]{:S(2)}) copy-start(bf16[4096,128]{1,0:T(8,128)(2,1)} %param.5) | copy-start | bytes 3145732
  4.0 14.6 %collective-permute-start = (bf16[512,768]{1,0:T(8,128)(2,1)S(1)}, bf16[512,768]{1,0:T(8,128)(2,1)S(1)}, u32[]{:S(2)}, u32[]{:S(2)}) collective-permute-start(bf16[512,768]{1,0:T(8,128)(2,1)S(1)} %get-tuple-element.24.cross.cross_joint), channel_id=1, source_target_pairs={{1,2},{3,4},{5,6},{7,8},{9,10},{11,12},{13,14},{15,16},{17,18},{19... | collective-permute-start | bytes 2359304 | tf_op jit(solution)/shard_map/ppermute | solution.py:478
  8.9 9.7 %collective-permute-start.1 = (bf16[512,768]{1,0:T(8,128)(2,1)S(1)}, bf16[512,768]{1,0:T(8,128)(2,1)S(1)}, u32[]{:S(2)}, u32[]{:S(2)}) collective-permute-start(bf16[512,768]{1,0:T(8,128)(2,1)S(1)} %get-tuple-element.25.chip.chip_joint), channel_id=1, source_target_pairs={{0,1},{2,3},{4,5},{6,7},{8,9},{10,11},{12,13},{14,15},{16,17},{18,... | collective-permute-start | bytes 2359304 | tf_op jit(solution)/shard_map/ppermute | solution.py:478
  21.0 8.3 %collective-permute-start.2 = (bf16[512,256]{1,0:T(8,128)(2,1)S(1)}, bf16[512,256]{1,0:T(8,128)(2,1)S(1)}, u32[]{:S(2)}, u32[]{:S(2)}) collective-permute-start(bf16[512,256]{1,0:T(8,128)(2,1)S(1)} %get-tuple-element.30.cross), channel_id=1, source_target_pairs={{1,2},{3,4},{5,6},{7,8},{9,10},{11,12},{13,14},{15,16},{17,18},{19... | collective-permute-start | bytes 786440 | tf_op jit(solution)/shard_map/ppermute | solution.py:478
  24.6 4.7 %collective-permute-start.3 = (bf16[512,256]{1,0:T(8,128)(2,1)S(1)}, bf16[512,256]{1,0:T(8,128)(2,1)S(1)}, u32[]{:S(2)}, u32[]{:S(2)}) collective-permute-start(bf16[512,256]{1,0:T(8,128)(2,1)S(1)} %get-tuple-element.31.chip), channel_id=1, source_target_pairs={{0,1},{2,3},{4,5},{6,7},{8,9},{10,11},{12,13},{14,15},{16,17},{18,... | collective-permute-start | bytes 786440 | tf_op jit(solution)/shard_map/ppermute | solution.py:478

commit v12 on v8

--- a/solution.py
+++ b/solution.py
@@ -89,6 +89,8 @@
     loads.begin("inverse", 1, last - 1)
     loads.begin("upper", 0)
     loads.begin("lower", last)
+    for name in ("lower", "upper"):
+        loads.begin(name, *early_blocks(count))
     both = list(enumerate(sides(count)))
     outs = (cross, chip)
     loads.wait("inverse", 0, last)
@@ -111,6 +113,12 @@
         value = dot(inv[side.edge], rhs[k])
         outs[k][:, width : 2 * width] = rounded(value)
         local[k] = value
+    for name in ("lower", "upper"):
+        loads.wait(name, *early_blocks(count))
+
+
+def early_blocks(count):
+    return range(1, count // 2 - 1)
 
 
 def first_edges(inverses, lower, upper, basis):
@@ -129,7 +137,7 @@
         scratch_shapes=[
             pltpu.VMEM((count, size, size), BF16),
             pltpu.VMEM((count, size, width), BF16),
-            pltpu.SemaphoreType.DMA((12,)),
+            pltpu.SemaphoreType.DMA((12 + count,)),
         ],
         compiler_params=params(),
         name="first_edges",
@@ -167,7 +175,8 @@
     deep = range(2, count - 2)
     factor[...] = jnp.full(factor.shape, weight[0], F32)
     loads = Loads({"lower": (lower, coupling.at[0]), "upper": (upper, coupling.at[1])}, sem)
-    for b in inside:
+    late = [b for b in inside if b not in early_blocks(count)]
+    for b in late:
         loads.begin("lower", b)
         loads.begin("upper", b)
     for side, payload in zip(sides(count), (cross, chip)):
@@ -176,8 +185,9 @@
         state[b] = rounded(dot(inv[b], base[b]))
 
     def ready(b):
-        loads.wait("lower", b)
-        loads.wait("upper", b)
+        if b in late:
+            loads.wait("lower", b)
+            loads.wait("upper", b)
 
     two_sweeps(count, inv, coupling, base, state, held, rhs, known, inside, ready)
     for b in deep:

time: 109 us -> 110 us (level)
  transfers between devices with their start and end apart: 4 -> 4, of which waited for: 1 -> 1; matrix products, arithmetic and copies ran while one was open for 0% -> 0% of each run, Pallas kernels for 12% -> 11%
where the time goes in v12:
time: 110 us; the launch traced here: 109 us
  blocking collectives  60.4 us (55%)
  Pallas kernels  38.1 us (35%)
  starting transfers between devices  8.94 us (8%)
    all_to_all x4, blocking collectives, exchange(): return lax.all_to_all(value, axes, split_axis=0, concat_axis=0, tiled=True)  60.4 us
    pallas_call x1, Pallas kernels, orthonormal(): pl.pallas_call(functools.partial(orthonormal_kernel, float(total_rows)),...  17.4 us
    ppermute x4, starting transfers between devices, swapped(): lax.ppermute(value, ROW, joined + [(j, i) for i, j in joined])  8.94 us
    pallas_call x1, Pallas kernels, first_pair(): pl.pallas_call(functools.partial(first_pair_kernel, count), out_shape=(ja...  7.85 us
    pallas_call x1, Pallas kernels, last_pair(): pl.pallas_call(functools.partial(last_pair_kernel, count), out_shape=(jax...  4.36 us
    pallas_call x1, Pallas kernels, first_edges(): pl.pallas_call(functools.partial(first_edges_kernel, count), out_shape=(o...  4.04 us
    pallas_call x1, Pallas kernels, meet(): pl.pallas_call(functools.partial(meet_kernel, count), out_shape=(out, out...  2.4 us
  transfers between devices with their start and end apart: 4, of which 1 were waited for; matrix products, arithmetic and copies ran while one was open for 0% of the time, Pallas kernels for 11%

profile of v12, /device:TPU:1, one launch (start us, length us, event | category | flops | bytes accessed | tf_op | source)
XLA Modules:
  0.0 109.3 jit_solution(2315170407454895410)
XLA Ops:
  0.0 0.0 copy-start
  0.0 0.0 copy-start.1
  0.0 4.0 %first_edges.1 = (bf16[512,768]{1,0:T(8,128)(2,1)S(1)}, bf16[512,768]{1,0:T(8,128)(2,1)S(1)}, f32[2,512,128]{2,1,0:T(8,128)S(1)}, bf16[2,8,512,512]{3,2,1,0:T(8,128)(2,1)S(1)}) custom-call(bf16[8,512,512]{2,1,0:T(8,128)(2,1)} %bitcast.2, bf16[8,512,512]{2,1,0:T(8,128)(2,1)} %lower.3, bf16[8,512,512]{2,1,0:T(8,128)(2,1)} %upper.3, bf16[8,512,128]{2,1,0:T(8,128)(2,1)} %bitcast.7), custom_call_target="tpu_custom_call" | custom-call | tf_op jit(solution)/shard_map/first_edges/pallas_call | solution.py:127
  4.1 4.9 %collective-permute-start = (bf16[512,768]{1,0:T(8,128)(2,1)S(1)}, bf16[512,768]{1,0:T(8,128)(2,1)S(1)}, u32[]{:S(2)}, u32[]{:S(2)}) collective-permute-start(bf16[512,768]{1,0:T(8,128)(2,1)S(1)} %get-tuple-element.24.cross.cross_joint), channel_id=1, source_target_pairs={{1,2},{3,4},{5,6},{7,8},{9,10},{11,12},{13,14},{15,16},{17,18},{19... | collective-permute-start | bytes 2359304 | tf_op jit(solution)/shard_map/ppermute | solution.py:487
  9.0 0.1 collective-permute-start.1
  9.7 0.0 copy-done
  9.8 0.0 copy-done.1
  9.8 7.8 %first_pair.1 = (bf16[2,8,512,512]{3,2,1,0:T(8,128)(2,1)S(1)}, bf16[4,512,128]{2,1,0:T(8,128)(2,1)S(1)}, f32[4,512,128]{2,1,0:T(8,128)S(1)}, bf16[2,512,128]{2,1,0:T(8,128)(2,1)S(1)}, f32[8,128]{1,0:T(8,128)S(1)}) custom-call(f32[1]{0:T(128)S(6)} %copy.8.weight, bf16[8,512,512]{2,1,0:T(8,128)(2,1)} %lower.3, ...), custom_call_target="tpu_custom_call", output_to_operand_aliasing={{0}: (3, {})} | custom-call | flops 2415919104 | bytes 12582912 | tf_op jit(solution)/shard_map/first_pair/pallas_call | solution.py:207
  17.6 1.0 collective-permute-done.from_cross.from_cross_joint
  18.7 0.0 collective-permute-done.1.from_chip.from_chip_joint
  18.7 2.4 %meet.1 = (bf16[512,256]{1,0:T(8,128)(2,1)S(1)}, bf16[512,256]{1,0:T(8,128)(2,1)S(1)}, f32[2,512,128]{2,1,0:T(8,128)S(1)}, bf16[2,512,128]{2,1,0:T(8,128)(2,1)S(1)}) custom-call(bf16[8,512,512]{2,1,0:T(8,128)(2,1)S(1)} %bitcast.4, bf16[2,8,512,512]{3,2,1,0:T(8,128)(2,1)S(1)} %get-tuple-element.27.coupling, bf16[8,512,128]{2,1,0:T(8,128)(2,1)S(1)} %bitcast.9, ...), custom_call_target="tpu_custom_call" | custom-call | flops 1073741824 | bytes 6291456 | tf_op jit(solution)/shard_map/meet/pallas_call | solution.py:313
  21.1 3.6 %collective-permute-start.2 = (bf16[512,256]{1,0:T(8,128)(2,1)S(1)}, bf16[512,256]{1,0:T(8,128)(2,1)S(1)}, u32[]{:S(2)}, u32[]{:S(2)}) collective-permute-start(bf16[512,256]{1,0:T(8,128)(2,1)S(1)} %get-tuple-element.30.cross), channel_id=1, source_target_pairs={{1,2},{3,4},{5,6},{7,8},{9,10},{11,12},{13,14},{15,16},{17,18},{19... | collective-permute-start | bytes 786440 | tf_op jit(solution)/shard_map/ppermute | solution.py:487
  24.7 0.3 collective-permute-start.3
  25.0 4.4 %last_pair.1 = (bf16[4,512,128]{2,1,0:T(8,128)(2,1)S(1)}, f32[4,512,128]{2,1,0:T(8,128)S(1)}, f32[2,512,128]{2,1,0:T(8,128)S(1)}) custom-call(f32[8,128]{1,0:T(8,128)S(1)} %get-tuple-element.26.weight, bf16[8,512,512]{2,1,0:T(8,128)(2,1)S(1)} %bitcast.5, bf16[2,8,512,512]{3,2,1,0:T(8,128)(2,1)S(1)} %get-tuple-element.27.coupling, ...), custom_call_target="tpu_custom_call" | custom-call | flops 2415919104 | bytes 12582912 | tf_op jit(solution)/shard_map/last_pair/pallas_call | solution.py:249
  29.4 0.0 collective-permute-done.2.from_cross
  29.4 0.0 collective-permute-done.3.from_chip
  29.4 1.6 %finish.1 = bf16[8,512,128]{2,1,0:T(8,128)(2,1)S(1)} custom-call(f32[8,128]{1,0:T(8,128)S(1)} %get-tuple-element.26.weight, bf16[8,512,512]{2,1,0:T(8,128)(2,1)S(1)} %bitcast.6, bf16[2,8,512,512]{3,2,1,0:T(8,128)(2,1)S(1)} %get-tuple-element.27.coupling, f32[4,512,128]{2,1,0:T(8,128)S(1)} %get-tuple-element.35.known, ...), custom_call_target="tpu_custom_call" | custom-call | flops 805306368 | bytes 6291456 | tf_op jit(solution)/shard_map/finish/pallas_call | solution.py:347
  30.9 22.1 %all_to_all.20.received = bf16[8,512,128]{2,1,0:T(8,128)(2,1)S(1)} all-to-all(bf16[8,512,128]{2,1,0:T(8,128)(2,1)S(1)} %finish.1), channel_id=1, replica_groups=mesh['x_hi'=2,'y'=4,'x_lo'=2,'z'=8,'core'=2] {'x_hi','y'}, dimensions={0} | all-to-all | bytes 2097152 | tf_op jit(solution)/shard_map/all_to_all | solution.py:493
  53.0 0.5 gram.1
  53.5 16.8 %all_to_all.21 = f32[16,8,128]{2,1,0:T(8,128)S(1)} all-to-all(f32[16,8,128]{2,1,0:T(8,128)S(1)} %get-tuple-element.39), channel_id=1, replica_groups=mesh['x_hi'=2,'y'=4,'x_lo'=2,'z'=8,'core'=2] {'x_hi','y','x_lo'}, dimensions={0} | all-to-all | bytes 131072 | tf_op jit(solution)/shard_map/all_to_all | solution.py:493
  70.3 12.1 %all_to_all.22 = f32[16,8,128]{2,1,0:T(8,128)S(1)} all-to-all(f32[16,8,128]{2,1,0:T(8,128)S(1)} %broadcast_in_dim.4), channel_id=1, replica_groups=mesh['x_hi'=2,'y'=4,'x_lo'=2,'z'=8,'core'=2] {'z','core'}, dimensions={0} | all-to-all | bytes 131072 | tf_op jit(solution)/shard_map/all_to_all | solution.py:493
  82.5 9.4 %all_to_all.23.gram = f32[16,8,128]{2,1,0:T(8,128)S(1)} all-to-all(f32[16,8,128]{2,1,0:T(8,128)S(1)} %broadcast_in_dim.5), channel_id=1, replica_groups=mesh['x_hi'=2,'y'=4,'x_lo'=2,'z'=8,'core'=2] {'x_hi','y','x_lo'}, dimensions={0} | all-to-all | bytes 131072 | tf_op jit(solution)/shard_map/all_to_all | solution.py:493
  91.9 17.4 %orthonormal.1 = f32[512,128]{1,0:T(8,128)} custom-call(f32[16,8,128]{2,1,0:T(8,128)S(1)} %all_to_all.23.gram, f32[512,128]{1,0:T(8,128)S(1)} %get-tuple-element.40.filtered), custom_call_target="tpu_custom_call" | custom-call | tf_op jit(solution)/shard_map/orthonormal/pallas_call | solution.py:465
  (4 shorter events, 0.1 us)
Async XLA Ops:
  0.0 9.7 %copy-start = (bf16[1,8,512,512]{3,2,1,0:T(8,128)(2,1)S(1)}, bf16[1,8,512,512]{3,2,1,0:T(8,128)(2,1)}, u32[]{:S(2)}) copy-start(bf16[1,8,512,512]{3,2,1,0:T(8,128)(2,1)} %param.6) | copy-start | bytes 12582916
  0.0 9.8 %copy-start.1 = (bf16[4096,128]{1,0:T(8,128)(2,1)S(1)}, bf16[4096,128]{1,0:T(8,128)(2,1)}, u32[]{:S(2)}) copy-start(bf16[4096,128]{1,0:T(8,128)(2,1)} %param.5) | copy-start | bytes 3145732
  4.1 14.6 %collective-permute-start = (bf16[512,768]{1,0:T(8,128)(2,1)S(1)}, bf16[512,768]{1,0:T(8,128)(2,1)S(1)}, u32[]{:S(2)}, u32[]{:S(2)}) collective-permute-start(bf16[512,768]{1,0:T(8,128)(2,1)S(1)} %get-tuple-element.24.cross.cross_joint), channel_id=1, source_target_pairs={{1,2},{3,4},{5,6},{7,8},{9,10},{11,12},{13,14},{15,16},{17,18},{19... | collective-permute-start | bytes 2359304 | tf_op jit(solution)/shard_map/ppermute | solution.py:487
  9.0 9.7 %collective-permute-start.1 = (bf16[512,768]{1,0:T(8,128)(2,1)S(1)}, bf16[512,768]{1,0:T(8,128)(2,1)S(1)}, u32[]{:S(2)}, u32[]{:S(2)}) collective-permute-start(bf16[512,768]{1,0:T(8,128)(2,1)S(1)} %get-tuple-element.25.chip.chip_joint), channel_id=1, source_target_pairs={{0,1},{2,3},{4,5},{6,7},{8,9},{10,11},{12,13},{14,15},{16,17},{18,... | collective-permute-start | bytes 2359304 | tf_op jit(solution)/shard_map/ppermute | solution.py:487
  21.1 8.3 %collective-permute-start.2 = (bf16[512,256]{1,0:T(8,128)(2,1)S(1)}, bf16[512,256]{1,0:T(8,128)(2,1)S(1)}, u32[]{:S(2)}, u32[]{:S(2)}) collective-permute-start(bf16[512,256]{1,0:T(8,128)(2,1)S(1)} %get-tuple-element.30.cross), channel_id=1, source_target_pairs={{1,2},{3,4},{5,6},{7,8},{9,10},{11,12},{13,14},{15,16},{17,18},{19... | collective-permute-start | bytes 786440 | tf_op jit(solution)/shard_map/ppermute | solution.py:487
  24.7 4.7 %collective-permute-start.3 = (bf16[512,256]{1,0:T(8,128)(2,1)S(1)}, bf16[512,256]{1,0:T(8,128)(2,1)S(1)}, u32[]{:S(2)}, u32[]{:S(2)}) collective-permute-start(bf16[512,256]{1,0:T(8,128)(2,1)S(1)} %get-tuple-element.31.chip), channel_id=1, source_target_pairs={{0,1},{2,3},{4,5},{6,7},{8,9},{10,11},{12,13},{14,15},{16,17},{18,... | collective-permute-start | bytes 786440 | tf_op jit(solution)/shard_map/ppermute | solution.py:487
